TPU v7x, 512 devices: a whole 4x4x16 slice. The times are simulated.
512 devices in a mesh: ctx: 32 (over x, y, core), exp: 16 (over z).
Axes of the slice: x: 4, y: 4, z: 16, core: 2. Of those that a mesh axis runs over, the one named last changes fastest.
Arguments:
- residual: bfloat16 [4096, 2048], P('ctx', 'exp'), may hold values from -60 to 60
- ssd_input: bfloat16 [4096, 2048], P('ctx', 'exp'), may hold values from -6 to 6
- state_in: bfloat16 [4096, 128], P('ctx'), may hold values from -0.015625 to 0.015625
- state_out: bfloat16 [4096, 128], P('ctx'), may hold values from -6 to 6
- log_decay: float32 [4096, 64], P('ctx', 'exp'), may hold values from -1 to 0
- skip_gain: float32 [64], P('exp'), may hold values from 0.5 to 1.5
- norm_gain: float32 [2048], P('exp'), may hold values from 0.1 to 1.9
- route_weight: float32 [4096, 2], P('ctx'), may hold values from 0.2 to 1
- expert_ids: int32 [4096, 2], P('ctx'), may hold values from 0 to 15, all different within a row; in each aligned block of 128 rows (0 to 127, 128 to 255, ...) at most 16 rows name the same one
- weight_in: bfloat16 [16, 2048, 8192], P('exp', None, 'ctx'), may hold values from -0.125 to 0.125
- weight_down: bfloat16 [16, 8192, 2048], P('exp', 'ctx'), may hold values from -0.125 to 0.125
- out_grad: bfloat16 [4096, 2048], P('ctx', 'exp'), may hold values from -6 to 6
Outputs:
- block_out: bfloat16 [4096, 2048], P('ctx', 'exp')
- grad_residual: bfloat16 [4096, 2048], P('ctx', 'exp')
- grad_input: bfloat16 [4096, 2048], P('ctx', 'exp')
- grad_weight_in: bfloat16 [16, 2048, 8192], P('exp', None, 'ctx')
- grad_weight_down: bfloat16 [16, 8192, 2048], P('exp', 'ctx')
Inputs may be any that keep to these rules, and one draw needn't show every extreme that they name: `expert_ids`: the two experts of a token differ; in each aligned block of 128 rows (the tokens of one index of ctx) every expert is named by exactly 16 rows.
All inputs are finite; a program needn't handle non-finite values.
Results may differ from a plain program's by a relative error of at most 0.015.
Values may be sent and summed in bfloat16 or wider, within the bound.
No kernel may reach another device: no remote copies, remote signals or barrier semaphores. Data moves between devices by JAX's collectives and lax.ppermute only.
A program may use at most 64 MiB of HBM per device.

v0:
```python
import jax
import jax.numpy as jnp
from jax import lax
from jax.sharding import PartitionSpec as P

D = 2048


epsilon = 1e-05
highest = lax.Precision.HIGHEST


def carried_in(value, axis, combine, identity, reverse):
    peers, index = (lax.axis_size(axis), lax.axis_index(axis))
    everything = jax.tree.map(
        lambda part, kind: lax.all_gather(part.astype(kind), axis),
        value,
        (jnp.bfloat16, jnp.bfloat16),
    )
    start = jax.tree.map(
        lambda part, zero: jnp.broadcast_to(jnp.asarray(zero, part.dtype), part.shape),
        value,
        identity,
    )

    def step(k, before):
        at = peers - 1 - k if reverse else k
        reached = at > index if reverse else at < index
        new = combine(
            before, jax.tree.map(lambda part, own: part[at].astype(own.dtype), everything, value)
        )
        return jax.tree.map(lambda a, b: jnp.where(reached, a, b), new, before)

    return lax.fori_loop(0, peers, step, start)


def carry_state(earlier, later):
    return (earlier[0] * later[0], later[0][:, None, None] * earlier[1] + later[1])


def block_mixing(log_decay, state_in_wide, state_out_wide):
    cumulative = jnp.cumsum(log_decay, axis=0)
    inner_state = jnp.dot(state_out_wide, state_in_wide.T, precision=highest)
    location_list = jnp.arange(cumulative.shape[0])
    causal = location_list[:, None] >= location_list[None, :]
    gap_log = cumulative[:, None, :] - cumulative[None, :, :]
    weights = inner_state[:, :, None] * jnp.exp(jnp.where(causal[:, :, None], gap_log, -jnp.inf))
    return (cumulative, weights)


def collect_routes(dispatch_table, returned):
    flattened = returned.reshape(-1, returned.shape[2])
    routed = lax.dot_general(
        dispatch_table, flattened, (((0,), (0,)), ((), ())), preferred_element_type=jnp.float32
    )
    return routed.reshape(-1, 2, flattened.shape[1])


def body(
    residual,
    ssd_input,
    state_in,
    state_out,
    log_decay,
    skip_gain,
    norm_gain,
    route_weight,
    expert_ids,
    weight_in,
    weight_down,
    out_grad,
):
    tokens_here = residual.shape[0]
    heads_here = log_decay.shape[1]
    feature_width = residual.shape[1]
    head_width = feature_width // heads_here
    exp_count = lax.axis_size("exp")
    capacity = 2 * tokens_here // exp_count
    state_in_wide = state_in.astype(jnp.float32)
    state_out_wide = state_out.astype(jnp.float32)
    cumulative, weights = block_mixing(log_decay, state_in_wide, state_out_wide)
    head_input = ssd_input.astype(jnp.float32).reshape(tokens_here, heads_here, head_width)
    ending = cumulative[-1]
    tail_decay = jnp.exp(ending[None, :] - cumulative)
    block_state = jnp.einsum(
        "sh,sn,shp->hnp", tail_decay, state_in_wide, head_input, precision=highest
    )
    block_decay = jnp.exp(ending)
    identity = (jnp.ones_like(block_decay), jnp.zeros_like(block_state))
    incoming = carried_in((block_decay, block_state), "ctx", carry_state, identity, False)[1]
    ssd_out = jnp.einsum("tsh,shp->thp", weights, head_input, precision=highest)
    ssd_out = ssd_out + jnp.exp(cumulative)[:, :, None] * jnp.einsum(
        "tn,hnp->thp", state_out_wide, incoming, precision=highest
    )
    ssd_out = ssd_out + skip_gain[None, :, None] * head_input
    mixed = (residual.astype(jnp.float32) + ssd_out.reshape(tokens_here, feature_width)).astype(
        jnp.bfloat16
    )
    mixed_wide = mixed.astype(jnp.float32)
    square_sum = lax.psum(jnp.sum(mixed_wide * mixed_wide, axis=1), "exp")
    inv_rms = lax.rsqrt(square_sum / D + epsilon)[:, None]
    normed = (mixed_wide * inv_rms * norm_gain[None, :]).astype(jnp.bfloat16)
    route_ids = expert_ids.reshape(-1)
    onehot = (route_ids[:, None] == jnp.arange(exp_count)[None, :]).astype(jnp.int32)
    before = jnp.cumsum(onehot, axis=0) - onehot
    slot_index = jnp.sum(before * onehot, axis=1)
    target = route_ids * capacity + slot_index
    dispatch_table = (jnp.arange(exp_count * capacity)[:, None] == target[None, :]).astype(
        jnp.bfloat16
    )
    route_rows = jnp.repeat(normed, 2, axis=0)
    out_grad_wide = out_grad.astype(jnp.float32)
    route_cot = (route_weight.reshape(-1)[:, None] * jnp.repeat(out_grad_wide, 2, axis=0)).astype(
        jnp.bfloat16
    )
    spread_rows = (
        jnp.dot(dispatch_table, route_rows, preferred_element_type=jnp.float32)
        .astype(jnp.bfloat16)
        .reshape(exp_count, capacity, feature_width)
    )
    spread_cot = (
        jnp.dot(dispatch_table, route_cot, preferred_element_type=jnp.float32)
        .astype(jnp.bfloat16)
        .reshape(exp_count, capacity, feature_width)
    )
    arrived_rows, arrived_cot = (
        lax.all_to_all(spread_rows, "exp", split_axis=0, concat_axis=2, tiled=True),
        lax.all_to_all(spread_cot, "exp", split_axis=0, concat_axis=2, tiled=True),
    )
    expert_rows, cot_rows = (
        lax.all_gather(arrived_rows[0], "ctx", axis=0, tiled=True),
        lax.all_gather(arrived_cot[0], "ctx", axis=0, tiled=True),
    )
    matrix_in = weight_in[0]
    matrix_down = weight_down[0]
    hidden = jnp.dot(expert_rows, matrix_in, preferred_element_type=jnp.float32)
    activated = jax.nn.silu(hidden).astype(jnp.bfloat16)
    row_piece = activated
    out_rows = lax.psum_scatter(
        jnp.dot(row_piece, matrix_down, preferred_element_type=jnp.float32).astype(jnp.bfloat16),
        "ctx",
        scatter_dimension=0,
        tiled=True,
    )
    returned = lax.all_to_all(out_rows[None], "exp", split_axis=2, concat_axis=0, tiled=True)
    routed = collect_routes(dispatch_table, returned)
    expert_mix = jnp.sum(routed * route_weight[:, :, None], axis=1)
    block_out = (mixed_wide + expert_mix).astype(jnp.bfloat16)
    d_act = lax.dot_general(
        cot_rows, matrix_down, (((1,), (1,)), ((), ())), preferred_element_type=jnp.float32
    )
    sigmoid_h = jax.nn.sigmoid(hidden)
    d_hidden = (d_act * sigmoid_h * (1.0 + hidden * (1.0 - sigmoid_h))).astype(jnp.bfloat16)
    grad_down = lax.dot_general(
        activated, cot_rows, (((0,), (0,)), ((), ())), preferred_element_type=jnp.float32
    )
    grad_in = lax.dot_general(
        expert_rows, d_hidden, (((0,), (0,)), ((), ())), preferred_element_type=jnp.float32
    )
    row_piece = d_hidden
    d_rows = lax.psum_scatter(
        lax.dot_general(
            row_piece, matrix_in, (((1,), (1,)), ((), ())), preferred_element_type=jnp.float32
        ).astype(jnp.bfloat16),
        "ctx",
        scatter_dimension=0,
        tiled=True,
    )
    returned_grads = lax.all_to_all(d_rows[None], "exp", split_axis=2, concat_axis=0, tiled=True)
    d_normed = jnp.sum(collect_routes(dispatch_table, returned_grads), axis=1)
    scaled = norm_gain[None, :] * d_normed
    dot_terms = lax.psum(jnp.sum(scaled * mixed_wide, axis=1), "exp")[:, None]
    d_mixed = (
        out_grad_wide + inv_rms * scaled - mixed_wide * inv_rms * inv_rms * inv_rms * dot_terms / D
    )
    head_grad = d_mixed.reshape(tokens_here, heads_here, head_width)
    grad_heads = jnp.einsum("tsh,thp->shp", weights, head_grad, precision=highest)
    lead_decay = jnp.exp(cumulative)
    block_cot = jnp.einsum(
        "th,tn,thp->hnp", lead_decay, state_out_wide, head_grad, precision=highest
    )
    later_state = carried_in((block_decay, block_cot), "ctx", carry_state, identity, True)[1]
    grad_heads = grad_heads + tail_decay[:, :, None] * jnp.einsum(
        "sn,hnp->shp", state_in_wide, later_state, precision=highest
    )
    grad_heads = grad_heads + skip_gain[None, :, None] * head_grad
    grad_input = grad_heads.reshape(tokens_here, feature_width).astype(jnp.bfloat16)
    return (
        block_out,
        d_mixed.astype(jnp.bfloat16),
        grad_input,
        grad_in.astype(jnp.bfloat16)[None],
        grad_down.astype(jnp.bfloat16)[None],
    )


def solution(mesh):
    placed = (
        P("ctx", "exp"),
        P("ctx", "exp"),
        P("ctx", None),
        P("ctx", None),
        P("ctx", "exp"),
        P("exp"),
        P("exp"),
        P("ctx", None),
        P("ctx", None),
        P("exp", None, "ctx"),
        P("exp", "ctx", None),
        P("ctx", "exp"),
    )
    return jax.shard_map(
        body,
        mesh=mesh,
        in_specs=placed,
        out_specs=(
            P("ctx", "exp"),
            P("ctx", "exp"),
            P("ctx", "exp"),
            P("exp", None, "ctx"),
            P("exp", "ctx", None),
        ),
        check_vma=False,
    )
```

profile of v0, /device:TPU:1, one launch (start us, length us, event | category | flops | bytes accessed | tf_op | source)
XLA Modules:
  0.0 650.2 jit_solution(7748751069555235195)
XLA Ops:
  7.2 0.9 copy.92
  8.2 0.8 copy.89
  9.2 1.6 fusion.14
  10.9 0.8 copy.100
  12.9 24.1 %all-gather.2 = bf16[32,1,4]{2,1,0:T(2,128)(2,1)S(1)} all-gather(bf16[1,1,4]{2,1,0:T(2,128)(2,1)S(1)} %get-tuple-element.356), channel_id=1, replica_groups=mesh['ctx'=32,'exp'=16] {'ctx'}, dimensions={0}, use_global_device_ids=true | all-gather | bytes 264 | tf_op jit(solution)/shard_map/all_gather | solution.py:16
  37.4 0.9 fusion.62
  38.3 37.0 %all-gather.12.cloned.1.call-done = bf16[128,128,32]{1,2,0:T(8,128)(2,1)} async-done(((bf16[4,128,32]{1,2,0:T(8,128)(2,1)}), bf16[128,128,32]{1,2,0:T(8,128)(2,1)}) %all-gather.12.cloned.1.call-update) | async-done | bytes 1048592 | tf_op jit(solution)/shard_map/all_gather | solution.py:16
  75.3 33.7 %while.30 = (s32[]{:T(128)}, f32[4,128,32]{2,1,0:T(8,128)S(1)}, s32[]{:T(128)}, bf16[32,4]{1,0:T(8,128)(2,1)S(1)}, bf16[32,4,128,32]{2,3,1,0:T(8,128)(2,1)}, /*index=5*/s32[]{:T(128)}, s32[]{:T(128)}) while((s32[]{:T(128)}, f32[4,128,32]{2,1,0:T(8,128)S(1)}, s32[]{:T(128)}, bf16[32,4]{1,0:T(8,128)(2,1)S(1)}, ...), condition=%wide.region_2.3_spmd.clone, body=%wide.region_1.2_spmd.clone.sunk | while | flops 81928 | bytes 295065 | solution.py:34
  75.3 0.8 constant_dynamic-slice_fusion.4
  78.5 0.8 constant_dynamic-slice_fusion.4
  79.6 0.8 constant_dynamic-slice_fusion.4
  82.7 0.8 constant_dynamic-slice_fusion.4
  83.8 0.8 constant_dynamic-slice_fusion.4
  88.0 0.8 constant_dynamic-slice_fusion.4
  89.1 0.8 constant_dynamic-slice_fusion.4
  93.3 0.8 constant_dynamic-slice_fusion.4
  94.3 0.8 constant_dynamic-slice_fusion.4
  98.5 0.8 constant_dynamic-slice_fusion.4
  99.6 0.8 constant_dynamic-slice_fusion.4
  102.8 0.8 constant_dynamic-slice_fusion.4
  103.8 0.8 constant_dynamic-slice_fusion.4
  108.0 0.8 constant_dynamic-slice_fusion.4
  110.1 24.8 %psum.14 = f32[128]{0:T(128)S(1)} all-reduce(f32[128]{0:T(128)S(1)} %get-tuple-element.351), channel_id=1, replica_groups=mesh['ctx'=32,'exp'=16] {'exp'}, use_global_device_ids=true, to_apply=%region_7.8 | all-reduce | flops 128 | bytes 1024 | tf_op jit(solution)/shard_map/psum | solution.py:100
  135.2 19.0 %all_to_all.60 = bf16[16,16,128]{2,1,0:T(8,128)(2,1)S(1)} all-to-all(bf16[16,16,128]{2,1,0:T(8,128)(2,1)S(1)} %bitcast.189), channel_id=1, replica_groups=mesh['ctx'=32,'exp'=16] {'exp'}, dimensions={0} | all-to-all | bytes 131072 | tf_op jit(solution)/shard_map/all_to_all | solution.py:127
  155.6 14.2 %all_to_all.61 = bf16[16,16,128]{2,1,0:T(8,128)(2,1)S(1)} all-to-all(bf16[16,16,128]{2,1,0:T(8,128)(2,1)S(1)} %bitcast.168), channel_id=1, replica_groups=mesh['ctx'=32,'exp'=16] {'exp'}, dimensions={0} | all-to-all | bytes 131072 | tf_op jit(solution)/shard_map/all_to_all | solution.py:128
  170.6 42.3 %all-gather.8.cloned.1.call-done = bf16[512,2048]{1,0:T(8,128)(2,1)} async-done(((bf16[16,2048]{1,0:T(8,128)(2,1)}), bf16[512,2048]{1,0:T(8,128)(2,1)}) %all-gather.8.cloned.1.call-update) | async-done | bytes 2097168 | tf_op jit(solution)/shard_map/all_gather | solution.py:131
  212.9 2.3 fusion.19
  215.2 2.1 convolution_convert_fusion.1
  217.6 57.4 %all-gather.10.cloned.1.call-done = bf16[512,2048]{1,0:T(8,128)(2,1)} async-done(((bf16[16,2048]{1,0:T(8,128)(2,1)}), bf16[512,2048]{1,0:T(8,128)(2,1)}) %all-gather.10.cloned.1.call-update) | async-done | bytes 2097168 | tf_op jit(solution)/shard_map/all_gather | solution.py:132
  274.9 2.4 fusion.5
  277.3 2.1 convolution_convert_fusion
  279.4 99.2 %reduce-scatter.3.cloned.1.call-done = bf16[16,2048]{1,0:T(8,128)(2,1)} async-done(((bf16[512,2048]{1,0:T(8,128)(2,1)}), bf16[16,2048]{1,0:T(8,128)(2,1)}) %reduce-scatter.3.cloned.1.call-update) | async-done | bytes 65552 | tf_op jit(solution)/shard_map/reduce_scatter | solution.py:139
  378.6 2.0 copy.104
  381.1 11.5 %reduce.3 = bf16[2048,16]{1,0:T(8,128)(2,1)S(1)} reduce(bf16[2048,1,16]{2,1,0:T(2,128)(2,1)S(1)} %bitcast.163, bf16[]{:T(256)} %broadcast.81), dimensions={1}, to_apply=%bitcast.131.reduce_sub_computation | reduce | bytes 131074
  392.6 1.2 reshape.206
  393.8 12.0 %all-to-all-start.1 = ((bf16[16,2,1024]{2,1,0:T(2,128)(2,1)}), bf16[16,2,1024]{2,1,0:T(2,128)(2,1)S(1)}, u32[]{:S(2)}, u32[]{:S(2)}) async-start(bf16[16,2,1024]{2,1,0:T(2,128)(2,1)} %reshape.206), calls=%async_computation.2 | async-start | bytes 131072 | tf_op jit(solution)/shard_map/all_to_all | solution.py:145
  405.8 78.6 %reduce-scatter.5.cloned.1.call-done = bf16[16,2048]{1,0:T(8,128)(2,1)} async-done(((bf16[512,2048]{1,0:T(8,128)(2,1)}), bf16[16,2048]{1,0:T(8,128)(2,1)}) %reduce-scatter.5.cloned.1.call-update) | async-done | bytes 65552 | tf_op jit(solution)/shard_map/reduce_scatter | solution.py:161
  484.4 2.0 copy.110
  486.4 11.5 %reduce.2 = bf16[2048,16]{1,0:T(8,128)(2,1)S(1)} reduce(bf16[2048,1,16]{2,1,0:T(2,128)(2,1)S(1)} %bitcast.164, bf16[]{:T(256)} %broadcast.81), dimensions={1}, to_apply=%bitcast.133.reduce_sub_computation | reduce | bytes 131074
  497.9 1.2 reshape.208
  499.1 12.0 %all-to-all-start.3 = ((bf16[16,2,1024]{2,1,0:T(2,128)(2,1)}), bf16[16,2,1024]{2,1,0:T(2,128)(2,1)S(1)}, u32[]{:S(2)}, u32[]{:S(2)}) async-start(bf16[16,2,1024]{2,1,0:T(2,128)(2,1)} %reshape.208), calls=%async_computation.5 | async-start | bytes 131072 | tf_op jit(solution)/shard_map/all_to_all | solution.py:169
  511.4 0.9 reshape.207
  512.9 9.8 %all-to-all-done.3 = bf16[16,2,1024]{2,1,0:T(2,128)(2,1)S(1)} async-done(((bf16[16,2,1024]{2,1,0:T(2,128)(2,1)}), bf16[16,2,1024]{2,1,0:T(2,128)(2,1)S(1)}, u32[]{:S(2)}, u32[]{:S(2)}) %all-to-all-start.3) | async-done | bytes 65568 | tf_op jit(solution)/shard_map/all_to_all | solution.py:169
  522.7 0.9 reshape.209
  524.7 21.7 %psum.15 = f32[128]{0:T(128)S(1)} all-reduce(f32[128]{0:T(128)S(1)} %fusion.44), channel_id=1, replica_groups=mesh['ctx'=32,'exp'=16] {'exp'}, use_global_device_ids=true, to_apply=%region_13.14 | all-reduce | flops 128 | bytes 1024 | tf_op jit(solution)/shard_map/psum | solution.py:172
  547.3 0.8 fusion.15
  548.1 3.5 fusion.2
  551.6 1.7 fusion.3
  553.4 54.5 %all-gather.14.cloned.1.call-done = bf16[128,128,32]{1,2,0:T(8,128)(2,1)} async-done(((bf16[4,128,32]{1,2,0:T(8,128)(2,1)}), bf16[128,128,32]{1,2,0:T(8,128)(2,1)}) %all-gather.14.cloned.1.call-update) | async-done | bytes 1048592 | tf_op jit(solution)/shard_map/all_gather | solution.py:16
  607.9 33.9 %while.31 = (s32[]{:T(128)}, f32[4,128,32]{2,1,0:T(8,128)S(1)}, s32[]{:T(128)}, bf16[32,4]{1,0:T(8,128)(2,1)S(1)}, bf16[32,4,128,32]{2,3,1,0:T(8,128)(2,1)}, /*index=5*/s32[]{:T(128)}, s32[]{:T(128)}, s32[]{:T(128)}, s32[]{:T(128)}) while((s32[]{:T(128)}, f32[4,128,32]{2,1,0:T(8,128)S(1)}, s32[]{:T(128)}, ...), condition=%wide.region_15.16_spmd.clone, body=%wide.region_14.15_spmd.clone.sunk | while | flops 81932 | bytes 295127 | solution.py:34
  608.9 0.8 constant_dynamic-slice_fusion.5
  611.1 0.8 constant_dynamic-slice_fusion.5
  614.2 0.8 constant_dynamic-slice_fusion.5
  617.4 0.8 constant_dynamic-slice_fusion.5
  619.5 0.8 constant_dynamic-slice_fusion.5
  620.6 0.8 constant_dynamic-slice_fusion.5
  622.7 0.8 constant_dynamic-slice_fusion.5
  625.9 0.8 constant_dynamic-slice_fusion.5
  629.1 0.8 constant_dynamic-slice_fusion.5
  631.2 0.8 constant_dynamic-slice_fusion.5
  634.4 0.8 constant_dynamic-slice_fusion.5
  637.6 0.8 constant_dynamic-slice_fusion.5
  639.7 0.8 constant_dynamic-slice_fusion.5
  640.8 0.8 constant_dynamic-slice_fusion.5
  (320 shorter events, 53.8 us)
Async XLA Ops:
  7.2 208.0 %copy-start = (bf16[1,256,2048]{2,1,0:T(8,128)(2,1)S(1)}, bf16[1,256,2048]{2,1,0:T(8,128)(2,1)}, u32[]{:S(2)}) copy-start(bf16[1,256,2048]{2,1,0:T(8,128)(2,1)} %param.26) | copy-start | bytes 3145732
  7.2 68.1 %all-gather.12.cloned.1.call-start = ((), (), s32[]{:S(2)}) async-start(), calls=%async_computation.10 | async-start | bytes 1081344 | tf_op jit(solution)/shard_map/all_gather | solution.py:16
  10.8 202.0 %all-gather.8.cloned.1.call-start = ((), (), s32[]{:S(2)}) async-start(), calls=%async_computation.6 | async-start | bytes 2162688 | tf_op jit(solution)/shard_map/all_gather | solution.py:131
  75.3 33.8 %copy-start.3 = (bf16[128,128]{1,0:T(8,128)(2,1)S(1)}, bf16[128,128]{1,0:T(8,128)(2,1)}, u32[]{:S(2)}) copy-start(bf16[128,128]{1,0:T(8,128)(2,1)} %param.19) | copy-start | bytes 98308
  75.3 34.2 %copy-start.9 = (f32[4]{0:T(128)S(1)}, f32[4]{0:T(128)}, u32[]{:S(2)}) copy-start(f32[4]{0:T(128)} %param.21) | copy-start | bytes 52
  75.3 34.7 %copy-start.5 = (bf16[128,128]{1,0:T(8,128)(2,1)S(1)}, bf16[128,128]{1,0:T(8,128)(2,1)}, u32[]{:S(2)}) copy-start(bf16[128,128]{1,0:T(8,128)(2,1)} %param.16) | copy-start | bytes 98308
  75.3 59.6 %copy-start.6 = (f32[128]{0:T(128)S(1)}, f32[128]{0:T(128)}, u32[]{:S(2)}) copy-start(f32[128]{0:T(128)} %param.22) | copy-start | bytes 1540
  75.3 79.7 %copy-start.7 = (f32[128,2]{0,1:T(2,128)S(1)}, f32[128,2]{0,1:T(2,128)}, u32[]{:S(2)}) copy-start(f32[128,2]{0,1:T(2,128)} %param.23) | copy-start | bytes 3076
  75.3 80.0 %copy-start.4 = (bf16[128,128]{1,0:T(8,128)(2,1)S(1)}, bf16[128,128]{1,0:T(8,128)(2,1)}, u32[]{:S(2)}) copy-start(bf16[128,128]{1,0:T(8,128)(2,1)} %param.27) | copy-start | bytes 98308
  109.0 103.8 %copy-start.1 = (bf16[1,2048,256]{2,1,0:T(8,128)(2,1)S(1)}, bf16[1,2048,256]{2,1,0:T(8,128)(2,1)}, u32[]{:S(2)}) copy-start(bf16[1,2048,256]{2,1,0:T(8,128)(2,1)} %param.25) | copy-start | bytes 3145732
  154.9 120.0 %all-gather.10.cloned.1.call-start = ((), (), s32[]{:S(2)}) async-start(), calls=%async_computation.8 | async-start | bytes 2162688 | tf_op jit(solution)/shard_map/all_gather | solution.py:132
  170.5 208.1 %reduce-scatter.3.cloned.1.call-start = ((), (), s32[]{:S(2)}) async-start(), calls=%async_computation.7 | async-start | bytes 2162688 | tf_op jit(solution)/shard_map/reduce_scatter | solution.py:139
  215.2 59.7 %copy-start.10 = (f32[512,256]{1,0:T(8,128)}, f32[512,256]{1,0:T(8,128)S(1)}, u32[]{:S(2)}) copy-start(f32[512,256]{1,0:T(8,128)S(1)} %fusion.19) | copy-start | bytes 1572868
  217.3 267.1 %reduce-scatter.5.cloned.1.call-start = ((), (), s32[]{:S(2)}) async-start(), calls=%async_computation.9 | async-start | bytes 2162688 | tf_op jit(solution)/shard_map/reduce_scatter | solution.py:161
  393.8 105.3 %all-to-all-start.1 = ((bf16[16,2,1024]{2,1,0:T(2,128)(2,1)}), bf16[16,2,1024]{2,1,0:T(2,128)(2,1)S(1)}, u32[]{:S(2)}, u32[]{:S(2)}) async-start(bf16[16,2,1024]{2,1,0:T(2,128)(2,1)} %reshape.206), calls=%async_computation.2 | async-start | bytes 131072 | tf_op jit(solution)/shard_map/all_to_all | solution.py:145
  499.1 23.6 %all-to-all-start.3 = ((bf16[16,2,1024]{2,1,0:T(2,128)(2,1)}), bf16[16,2,1024]{2,1,0:T(2,128)(2,1)S(1)}, u32[]{:S(2)}, u32[]{:S(2)}) async-start(bf16[16,2,1024]{2,1,0:T(2,128)(2,1)} %reshape.208), calls=%async_computation.5 | async-start | bytes 131072 | tf_op jit(solution)/shard_map/all_to_all | solution.py:169
  511.2 96.7 %all-gather.14.cloned.1.call-start = ((), (), s32[]{:S(2)}) async-start(), calls=%async_computation.11 | async-start | bytes 1081344 | tf_op jit(solution)/shard_map/all_gather | solution.py:16
  548.1 3.5 copy-start.8
  548.1 3.5 copy-start.11
  607.9 33.9 %copy-start.2 = (bf16[128,128]{1,0:T(8,128)(2,1)S(1)}, bf16[128,128]{1,0:T(8,128)(2,1)}, u32[]{:S(2)}) copy-start(bf16[128,128]{1,0:T(8,128)(2,1)} %param.18) | copy-start | bytes 98308
Sparse Core Ops, SparseCore 0:
  11.7 63.5 all-gather.11
  155.1 57.7 all-gather.7
  216.6 58.3 all-gather.9
  279.2 99.3 reduce-scatter.2
  382.9 101.5 reduce-scatter.4
  548.2 59.5 all-gather.13
where the time goes:
time: 655 us; the launch traced here: 650 us
  waiting for transfers between devices  379 us (58%)
  blocking collectives  104 us (16%)
  local copies, waits for them, and re-layouts  73.3 us (11%)
  other arithmetic  32.8 us (5%)
  starting transfers between devices  24.5 us (4%)
  matrix products  19.7 us (3%)
  between operations  14.5 us (2%)
    reduce_scatter x1, waiting for transfers between devices, body(): lax.psum_scatter(jnp.dot(row_piece, matrix_down, preferred_element_type=j...  99.2 us
    all_gather x2, waiting for transfers between devices, carried_in(): lax.all_gather(part.astype(kind), axis)  91.5 us
    reduce_scatter x1, waiting for transfers between devices, body(): lax.psum_scatter(lax.dot_general(row_piece, matrix_in, (((1,), (1,)), (()...  78.6 us
    dynamic_slice x128, local copies, waits for them, and re-layouts, step(): part[at].astype(own.dtype)  57.5 us
    all_gather x1, waiting for transfers between devices, body(): lax.all_gather(arrived_cot[0], 'ctx', axis=0, tiled=True)  57.4 us
    all_gather x1, waiting for transfers between devices, body(): lax.all_gather(arrived_rows[0], 'ctx', axis=0, tiled=True)  42.3 us
    psum x1, blocking collectives, body(): square_sum = lax.psum(jnp.sum(mixed_wide * mixed_wide, axis=1), 'exp')  24.8 us
    all_gather x1, blocking collectives, carried_in(): lax.all_gather(part.astype(kind), axis)  24.1 us
  transfers between devices with their start and end apart: 8, of which 7 were waited for; matrix products, arithmetic and copies ran while one was open for 8% of the time, Pallas kernels for 0%

commit v1 on v0

v1 whole, which is shorter than its diff:
```python
import functools
import jax
import jax.numpy as jnp
from jax import lax
from jax.experimental import pallas as pl
from jax.experimental.pallas import tpu as pltpu
from jax.sharding import PartitionSpec as P

D = 2048
epsilon = 1e-05
f32 = jnp.float32
bf16 = jnp.bfloat16


def iota(shape, axis):
    return lax.broadcasted_iota(jnp.int32, shape, axis)


def mm(a, b):
    return jnp.dot(a, b, preferred_element_type=f32)


def mm_t(a, b):
    return lax.dot_general(a, b, (((0,), (0,)), ((), ())), preferred_element_type=f32)


def mm_nt(a, b):
    return lax.dot_general(a, b, (((1,), (1,)), ((), ())), preferred_element_type=f32)


def split2(a):
    high = a.astype(bf16)
    return high, (a - high.astype(f32)).astype(bf16)


def split3(a):
    high = a.astype(bf16)
    rest = a - high.astype(f32)
    middle = rest.astype(bf16)
    return high, middle, (rest - middle.astype(f32)).astype(bf16)


def join3(parts):
    return parts[0].astype(f32) + parts[1].astype(f32) + parts[2].astype(f32)


def per_head(columns, shape, width):
    lane = iota(shape, 1)
    value = jnp.broadcast_to(columns[:, 0:1], shape)
    for head in range(1, columns.shape[1]):
        value = jnp.where(lane >= head * width, columns[:, head : head + 1], value)
    return value


def ones_where(condition, dtype=bf16):
    return jnp.where(condition, 1.0, 0.0).astype(dtype)


def call(kernel, outs, *args, smem=()):
    return pl.pallas_call(
        kernel,
        out_shape=outs,
        in_specs=[
            pl.BlockSpec(memory_space=pltpu.SMEM if i in smem else pltpu.VMEM)
            for i in range(len(args))
        ],
        out_specs=jax.tree.map(lambda o: pl.BlockSpec(memory_space=pltpu.VMEM), outs),
    )(*args)


def shape_of(shape, dtype):
    return jax.ShapeDtypeStruct(shape, dtype)


def route_kernel(ids_ref, ids_t_ref, weight_ref, grad_ref, gain_ref, to_rows_ref, from_ref, pay_ref):
    tokens, features = grad_ref.shape
    experts, _, _ = pay_ref.shape
    rows = to_rows_ref.shape[0]
    capacity = rows // experts
    square = (tokens, tokens)
    grad = grad_ref[...].astype(f32)
    hits_t = [ids_t_ref[k : k + 1, :] == iota(square, 0) for k in range(2)]
    sum_t = ones_where(hits_t[0] | hits_t[1])
    before_t = mm(sum_t, ones_where(iota(square, 0) < iota(square, 1)))
    hits = [ids_ref[:, k : k + 1] == iota(square, 1) for k in range(2)]
    both = ones_where(hits[0] | hits[1])
    before = mm(ones_where(iota(square, 1) < iota(square, 0)), both)
    spread = []
    cot = jnp.zeros((rows, features), f32)
    for k in range(2):
        slot_t = jnp.sum(jnp.where(hits_t[k], before_t, 0.0), axis=0, keepdims=True)
        row_t = ids_t_ref[k : k + 1, :] * capacity + slot_t.astype(jnp.int32)
        table_t = ones_where(iota((rows, tokens), 0) == row_t)
        spread.append(table_t)
        scaled = (weight_ref[:, k : k + 1] * grad).astype(bf16)
        cot = cot + mm(table_t, scaled)
        slot = jnp.sum(jnp.where(hits[k], before, 0.0), axis=1, keepdims=True)
        row = ids_ref[:, k : k + 1] * capacity + slot.astype(jnp.int32)
        from_ref[k] = ones_where(iota((tokens, rows), 1) == row)
    to_rows_ref[...] = spread[0] + spread[1]
    pay_ref[:, :capacity, :] = cot.astype(bf16).reshape(experts, capacity, features)
    high, middle, low = split3(gain_ref[...])
    place = iota((capacity, features), 0)
    pieces = jnp.where(
        place == 0,
        high.astype(f32),
        jnp.where(place == 1, middle.astype(f32), jnp.where(place == 2, low.astype(f32), 0.0)),
    ).astype(bf16)
    pay_ref[:, capacity:, :] = jnp.broadcast_to(pieces[None], (experts, capacity, features))


def state_kernel(x_ref, b_ref, decay_ref, pay_ref, cum_ref):
    tokens, features = x_ref.shape
    width = features // decay_ref.shape[1]
    square = (tokens, tokens)
    spread = per_head(decay_ref[...], (tokens, features), width)
    causal = ones_where(iota(square, 1) <= iota(square, 0))
    high, middle, low = split3(spread)
    cum = mm(causal, high) + mm(causal, middle) + mm(causal, low)
    cum_ref[...] = cum
    ending = cum[tokens - 1 : tokens, :]
    tail = jnp.exp(ending - cum)
    moved_high, moved_low = split2(tail * x_ref[...].astype(f32))
    b = b_ref[...]
    state = (mm_t(b, moved_high) + mm_t(b, moved_low)).astype(bf16)
    states = state.shape[0]
    parts = split3(ending)
    place = iota((pay_ref.shape[1] - states, features), 0)
    extra = jnp.where(
        place == 0,
        parts[0].astype(f32),
        jnp.where(place == 1, parts[1].astype(f32), jnp.where(place == 2, parts[2].astype(f32), 0.0)),
    ).astype(bf16)
    for j in range(pay_ref.shape[0]):
        pay_ref[j, :states, :] = state
        pay_ref[j, states:, :] = extra


def local_kernel(x_ref, b_ref, c_ref, cum_ref, skip_ref, residual_ref, local_ref, back_ref):
    tokens, features = x_ref.shape
    heads = back_ref.shape[1]
    width = features // heads
    square = (tokens, tokens)
    x = x_ref[...]
    cum = cum_ref[...]
    cum_t = cum.T
    inner = mm_nt(c_ref[...], b_ref[...])
    inner_t = mm_nt(b_ref[...], c_ref[...])
    causal = iota(square, 1) <= iota(square, 0)
    causal_t = iota(square, 0) <= iota(square, 1)
    lane = iota((tokens, features), 1)
    skip = per_head(skip_ref[...], (1, features), width)
    total = residual_ref[...].astype(f32) + skip * x.astype(f32)
    for head in range(heads):
        column = cum[:, head * width : head * width + 1]
        row = cum_t[head * width : head * width + 1, :]
        gap = jnp.where(causal, column - row, -jnp.inf)
        high, low = split2(inner * jnp.exp(gap))
        product = mm(high, x) + mm(low, x)
        inside = (lane >= head * width) & (lane < (head + 1) * width)
        total = total + jnp.where(inside, product, 0.0)
        gap_t = jnp.where(causal_t, row - column, -jnp.inf)
        high, low = split2(inner_t * jnp.exp(gap_t))
        back_ref[0, head] = high
        back_ref[1, head] = low
    local_ref[...] = total


def block_sums(states_ref, rows_at):
    blocks = states_ref.shape[0]
    features = states_ref.shape[2]
    extra = states_ref[:, rows_at : rows_at + 16, :].astype(f32)
    place = iota((blocks, 16, features), 1)
    return [
        jnp.sum(jnp.where(place == k, extra, 0.0), axis=1).astype(bf16) for k in range(3)
    ]


def weighted(states_ref, weights, states):
    total = jnp.zeros((states, states_ref.shape[2]), f32)
    for j in range(states_ref.shape[0]):
        total = total + weights[j : j + 1, :] * states_ref[j, :states, :].astype(f32)
    return total


def mixed_kernel(me_ref, states_ref, c_ref, cum_ref, local_ref, table_ref, mixed_ref, rows_ref, later_ref):
    blocks = states_ref.shape[0]
    states = c_ref.shape[1]
    me = me_ref[0]
    parts = block_sums(states_ref, states)
    source, between = iota((blocks, blocks), 0), iota((blocks, blocks), 1)
    mask = ones_where((between > source) & (between < me))
    sums = mm(mask, parts[0]) + mm(mask, parts[1]) + mm(mask, parts[2])
    which = iota((blocks, states_ref.shape[2]), 0)
    weights = jnp.where(which < me, jnp.exp(sums), 0.0)
    high, low = split2(weighted(states_ref, weights, states))
    c = c_ref[...]
    total = local_ref[...] + jnp.exp(cum_ref[...]) * (mm(c, high) + mm(c, low))
    mixed = total.astype(bf16)
    mixed_ref[...] = mixed
    rows_ref[...] = mm(table_ref[...], mixed).astype(bf16).reshape(rows_ref.shape)
    mask = ones_where((between < source) & (between > me))
    sums = mm(mask, parts[0]) + mm(mask, parts[1]) + mm(mask, parts[2])
    later_ref[...] = jnp.where(which > me, jnp.exp(sums), 0.0)


def cot_kernel(in_ref, out_ref, gain_ref):
    peers, capacity, features = in_ref.shape[0], out_ref.shape[1], in_ref.shape[2]
    for e in range(peers):
        here = slice(e * features, (e + 1) * features)
        piece = in_ref[e, :capacity, :]
        for j in range(out_ref.shape[0]):
            out_ref[j, :, here] = piece
        extra = in_ref[e, capacity : 2 * capacity, :].astype(f32)
        gain_ref[:, here] = jnp.sum(extra, axis=0, keepdims=True)


def norm_kernel(in_ref, gain_ref, out_ref, raw_ref, inv_ref):
    peers, capacity, features = in_ref.shape
    square = jnp.zeros((capacity, features), f32)
    for e in range(peers):
        piece = in_ref[e].astype(f32)
        square = square + piece * piece
    inv = lax.rsqrt(jnp.sum(square, axis=1, keepdims=True) / D + epsilon)
    inv_ref[...] = jnp.broadcast_to(inv, inv_ref.shape)
    for e in range(peers):
        here = slice(e * features, (e + 1) * features)
        piece = in_ref[e]
        raw_ref[:, here] = piece
        normed = (piece.astype(f32) * inv * gain_ref[:, here]).astype(bf16)
        for j in range(out_ref.shape[0]):
            out_ref[j, :, here] = normed


def grad_rows_kernel(parts_ref, raw_ref, inv_ref, gain_ref, out_ref):
    peers, capacity, features = out_ref.shape
    total = parts_ref[0].astype(f32)
    for j in range(1, parts_ref.shape[0]):
        total = total + parts_ref[j].astype(f32)
    total = total.astype(bf16).astype(f32)
    scaled = gain_ref[...] * total
    raw = raw_ref[...].astype(f32)
    inv = inv_ref[:, 0:1]
    inner = jnp.sum(scaled * raw, axis=1, keepdims=True)
    result = inv * scaled - raw * (inv * inv * inv * inner / D)
    for e in range(peers):
        out_ref[e] = result[:, e * features : (e + 1) * features].astype(bf16)


def out_rows_kernel(parts_ref, out_ref):
    peers, capacity, features = out_ref.shape
    total = parts_ref[0].astype(f32)
    for j in range(1, parts_ref.shape[0]):
        total = total + parts_ref[j].astype(f32)
    for e in range(peers):
        out_ref[e] = total[:, e * features : (e + 1) * features].astype(bf16)


def block_out_kernel(rows_ref, from_ref, weight_ref, mixed_ref, out_ref):
    rows = rows_ref[...].reshape(from_ref.shape[2], rows_ref.shape[2])
    total = mixed_ref[...].astype(f32)
    extra = weight_ref[:, 0:1] * mm(from_ref[0], rows) + weight_ref[:, 1:2] * mm(from_ref[1], rows)
    out_ref[...] = (total + extra).astype(bf16)


def cot_state_kernel(rows_ref, from_ref, grad_ref, c_ref, cum_ref, residual_ref, wide_ref, pay_ref):
    rows = rows_ref[...].reshape(from_ref.shape[2], rows_ref.shape[2])
    table = from_ref[0] + from_ref[1]
    total = grad_ref[...].astype(f32) + mm(table, rows)
    wide_ref[...] = total
    residual_ref[...] = total.astype(bf16)
    high, low = split2(jnp.exp(cum_ref[...]) * total)
    c = c_ref[...]
    state = (mm_t(c, high) + mm_t(c, low)).astype(bf16)
    for j in range(pay_ref.shape[0]):
        pay_ref[j] = state


def back_local_kernel(wide_ref, back_ref, skip_ref, out_ref):
    tokens, features = wide_ref.shape
    heads = back_ref.shape[1]
    width = features // heads
    wide = wide_ref[...]
    high, low = split2(wide)
    lane = iota((tokens, features), 1)
    total = per_head(skip_ref[...], (1, features), width) * wide
    for head in range(heads):
        product = mm(back_ref[0, head], high) + mm(back_ref[1, head], high) + mm(back_ref[0, head], low)
        inside = (lane >= head * width) & (lane < (head + 1) * width)
        total = total + jnp.where(inside, product, 0.0)
    out_ref[...] = total


def final_kernel(states_ref, later_ref, b_ref, cum_ref, local_ref, out_ref):
    tokens = cum_ref.shape[0]
    high, low = split2(weighted(states_ref, later_ref[...], states_ref.shape[1]))
    cum = cum_ref[...]
    tail = jnp.exp(cum[tokens - 1 : tokens, :] - cum)
    b = b_ref[...]
    out_ref[...] = (local_ref[...] + tail * (mm(b, high) + mm(b, low))).astype(bf16)


def swap(a, axis):
    return lax.all_to_all(a, axis, split_axis=0, concat_axis=0, tiled=True)


def body(
    residual,
    ssd_input,
    state_in,
    state_out,
    log_decay,
    skip_gain,
    norm_gain,
    route_weight,
    expert_ids,
    weight_in,
    weight_down,
    out_grad,
):
    tokens, features = residual.shape
    heads = log_decay.shape[1]
    states = state_in.shape[1]
    experts = lax.axis_size("exp")
    blocks = lax.axis_size("ctx")
    rows = 2 * tokens
    capacity = rows // experts
    me = lax.axis_index("ctx").astype(jnp.int32).reshape(1)
    skip = skip_gain.reshape(1, heads)
    matrix_in = weight_in[0]
    matrix_down = weight_down[0]

    state_pay, cum = call(
        state_kernel,
        (shape_of((blocks, states + 16, features), bf16), shape_of((tokens, features), f32)),
        ssd_input, state_in, log_decay,
    )
    state_all = swap(state_pay, "ctx")

    to_rows, from_rows, cot_pay = call(
        route_kernel,
        (
            shape_of((rows, tokens), bf16),
            shape_of((2, tokens, rows), bf16),
            shape_of((experts, 2 * capacity, features), bf16),
        ),
        expert_ids, expert_ids.T, route_weight, out_grad, norm_gain.reshape(1, features),
    )
    cot_arrived = swap(cot_pay, "exp")
    local, back = call(
        local_kernel,
        (shape_of((tokens, features), f32), shape_of((2, heads, tokens, tokens), bf16)),
        ssd_input, state_in, state_out, cum, skip, residual,
    )
    cot_spread, gain = call(
        cot_kernel,
        (shape_of((blocks, capacity, D), bf16), shape_of((1, D), f32)),
        cot_arrived,
    )
    cot_rows = swap(cot_spread, "ctx").reshape(blocks * capacity, D)
    d_act = mm_nt(cot_rows, matrix_down)

    mixed, mixed_rows, later = call(
        mixed_kernel,
        (
            shape_of((tokens, features), bf16),
            shape_of((experts, capacity, features), bf16),
            shape_of((blocks, features), f32),
        ),
        me, state_all, state_out, cum, local, to_rows,
        smem=(0,),
    )
    arrived = swap(mixed_rows, "exp")
    normed_spread, raw, inv = call(
        norm_kernel,
        (
            shape_of((blocks, capacity, D), bf16),
            shape_of((capacity, D), bf16),
            shape_of((capacity, 128), f32),
        ),
        arrived, gain,
    )
    expert_rows = swap(normed_spread, "ctx").reshape(blocks * capacity, D)

    hidden = mm(expert_rows, matrix_in)
    sigmoid_h = jax.nn.sigmoid(hidden)
    d_hidden = (d_act * sigmoid_h * (1.0 + hidden * (1.0 - sigmoid_h))).astype(bf16)
    d_parts = mm_nt(d_hidden, matrix_in).astype(bf16).reshape(blocks, capacity, D)
    d_all = swap(d_parts, "ctx")
    activated = (hidden * sigmoid_h).astype(bf16)
    out_parts = mm(activated, matrix_down).astype(bf16).reshape(blocks, capacity, D)
    out_all = swap(out_parts, "ctx")
    grad_down = mm_t(activated, cot_rows).astype(bf16)
    grad_in = mm_t(expert_rows, d_hidden).astype(bf16)

    d_back = call(
        grad_rows_kernel, shape_of((experts, capacity, features), bf16), d_all, raw, inv, gain
    )
    d_returned = swap(d_back, "exp")
    out_back = call(out_rows_kernel, shape_of((experts, capacity, features), bf16), out_all)
    out_returned = swap(out_back, "exp")

    grad_residual, wide, cot_pay_state = call(
        cot_state_kernel,
        (
            shape_of((tokens, features), bf16),
            shape_of((tokens, features), f32),
            shape_of((blocks, states, features), bf16),
        ),
        d_returned, from_rows, out_grad, state_out, cum,
    )
    cot_states = swap(cot_pay_state, "ctx")
    back_local = call(
        back_local_kernel, shape_of((tokens, features), f32), wide, back, skip
    )
    block_out = call(
        block_out_kernel, shape_of((tokens, features), bf16), out_returned, from_rows, route_weight, mixed
    )
    grad_input = call(
        final_kernel, shape_of((tokens, features), bf16), cot_states, later, state_in, cum, back_local
    )
    return (block_out, grad_residual, grad_input, grad_in[None], grad_down[None])


def solution(mesh):
    placed = (
        P("ctx", "exp"),
        P("ctx", "exp"),
        P("ctx", None),
        P("ctx", None),
        P("ctx", "exp"),
        P("exp"),
        P("exp"),
        P("ctx", None),
        P("ctx", None),
        P("exp", None, "ctx"),
        P("exp", "ctx", None),
        P("ctx", "exp"),
    )
    return jax.shard_map(
        body,
        mesh=mesh,
        in_specs=placed,
        out_specs=(
            P("ctx", "exp"),
            P("ctx", "exp"),
            P("ctx", "exp"),
            P("exp", None, "ctx"),
            P("exp", "ctx", None),
        ),
        check_vma=False,
    )
```

time: 655 us -> 278 us (0.42)
  waiting for transfers between devices: 379 us -> 133 us
  blocking collectives: 104 us -> 34 us
  local copies, waits for them, and re-layouts: 73.3 us -> 6.02 us
  other arithmetic: 32.8 us -> 0 us
  starting transfers between devices: 24.5 us -> 57.3 us
  Pallas kernels: 0 us -> 28.4 us
  between operations: 14.5 us -> 0.82 us
    all_gather x4 -> x0, waiting for transfers between devices: 191 us -> none  [the longest x2 91.5 us: carried_in(): lax.all_gather(part.astype(kind), axis)]
    reduce_scatter x2 -> x0, waiting for transfers between devices: 178 us -> none  [the longest x1 99.2 us: body(): lax.psum_scatter(jnp.dot(row_piece, matrix_down, preferred_element_type=j...]
    all_to_all x2 -> x9, waiting for transfers between devices: 9.83 us -> 133 us  [swap(): return lax.all_to_all(a, axis, split_axis=0, concat_axis=0, tiled=True)]
    dynamic_slice x128 -> x0, local copies, waits for them, and re-layouts: 57.5 us -> none  [step(): part[at].astype(own.dtype)]
    psum x2 -> x0, blocking collectives: 46.5 us -> none  [the longest x1 24.8 us: body(): square_sum = lax.psum(jnp.sum(mixed_wide * mixed_wide, axis=1), 'exp')]
    all_to_all x2 -> x9, starting transfers between devices: 24.1 us -> 57.3 us  [swap(): return lax.all_to_all(a, axis, split_axis=0, concat_axis=0, tiled=True)]
    pallas_call x0 -> x12, Pallas kernels: none -> 28.4 us  [call(): pl.pallas_call(kernel, out_shape=outs, in_specs=[pl.BlockSpec(memory_spac...]
    all_gather x1 -> x0, blocking collectives: 24.1 us -> none  [carried_in(): lax.all_gather(part.astype(kind), axis)]
  transfers between devices with their start and end apart: 8 -> 9, of which waited for: 7 -> 9; matrix products, arithmetic and copies ran while one was open for 8% -> 5% of each run, Pallas kernels for 0% -> 8%
where the time goes in v1:
time: 278 us; the launch traced here: 276 us
  waiting for transfers between devices  133 us (48%)
  starting transfers between devices  57.3 us (21%)
  blocking collectives  34 us (12%)
  Pallas kernels  28.4 us (10%)
  matrix products  16.6 us (6%)
  local copies, waits for them, and re-layouts  6.02 us (2%)
    all_to_all x9, waiting for transfers between devices, swap(): return lax.all_to_all(a, axis, split_axis=0, concat_axis=0, tiled=True)  133 us
    all_to_all x9, starting transfers between devices, swap(): return lax.all_to_all(a, axis, split_axis=0, concat_axis=0, tiled=True)  57.3 us
    all_to_all x1, blocking collectives, swap(): return lax.all_to_all(a, axis, split_axis=0, concat_axis=0, tiled=True)  34 us
    pallas_call x12, Pallas kernels, call(): pl.pallas_call(kernel, out_shape=outs, in_specs=[pl.BlockSpec(memory_spac...  28.4 us
    dot_general x2, matrix products, mm_t(): lax.dot_general(a, b, (((0,), (0,)), ((), ())), preferred_element_type=f32)  6.71 us
    unnamed x29, local copies, waits for them, and re-layouts  6.02 us
  transfers between devices with their start and end apart: 9, of which 9 were waited for; matrix products, arithmetic and copies ran while one was open for 5% of the time, Pallas kernels for 8%

profile of v1, /device:TPU:1, one launch (start us, length us, event | category | flops | bytes accessed | tf_op | source)
XLA Modules:
  0.0 276.5 jit_solution(15922611374572904709)
XLA Ops:
  0.6 0.0 copy-start
  0.6 0.0 copy-start.11
  0.7 0.0 copy-start.10
  0.7 1.5 copy.17.decay_ref
  2.2 2.5 shard_map.155
  4.7 10.4 %all-to-all-start = ((bf16[32,144,128]{2,1,0:T(8,128)(2,1)}), bf16[32,144,128]{2,1,0:T(8,128)(2,1)S(1)}, u32[]{:S(2)}, u32[]{:S(2)}) async-start(bf16[32,144,128]{2,1,0:T(8,128)(2,1)} %get-tuple-element.23), calls=%async_computation | async-start | bytes 2359296 | tf_op jit(solution)/shard_map/all_to_all | solution.py:304
  15.1 0.0 copy-done.11
  15.1 0.7 copy.19.weight_ref
  15.8 0.0 copy-done.10
  15.8 0.7 copy.18.ids_ref
  16.6 2.0 shard_map.157
  18.6 14.9 %all-to-all-done.states_ref = bf16[32,144,128]{2,1,0:T(8,128)(2,1)S(1)} async-done(((bf16[32,144,128]{2,1,0:T(8,128)(2,1)}), bf16[32,144,128]{2,1,0:T(8,128)(2,1)S(1)}, u32[]{:S(2)}, u32[]{:S(2)}) %all-to-all-start) | async-done | bytes 1179680 | tf_op jit(solution)/shard_map/all_to_all | solution.py:304
  33.6 0.0 copy-start.3
  33.6 13.0 %all-to-all-start.2 = ((bf16[16,32,128]{2,1,0:T(8,128)(2,1)}), bf16[16,32,128]{2,1,0:T(8,128)(2,1)S(1)}, u32[]{:S(2)}, u32[]{:S(2)}) async-start(bf16[16,32,128]{2,1,0:T(8,128)(2,1)} %get-tuple-element.28), calls=%async_computation.2 | async-start | bytes 262144 | tf_op jit(solution)/shard_map/all_to_all | solution.py:304
  46.5 2.0 shard_map.156
  48.5 0.0 copy-done.3
  48.5 2.8 shard_map.158
  51.2 7.4 %all-to-all-done.2.in_ref = bf16[16,32,128]{2,1,0:T(8,128)(2,1)S(1)} async-done(((bf16[16,32,128]{2,1,0:T(8,128)(2,1)}), bf16[16,32,128]{2,1,0:T(8,128)(2,1)S(1)}, u32[]{:S(2)}, u32[]{:S(2)}) %all-to-all-start.2) | async-done | bytes 131104 | tf_op jit(solution)/shard_map/all_to_all | solution.py:304
  58.6 0.0 copy-start.6
  58.6 6.5 %all-to-all-start.1 = ((bf16[16,16,128]{2,1,0:T(8,128)(2,1)}), bf16[16,16,128]{2,1,0:T(8,128)(2,1)S(1)}, u32[]{:S(2)}, u32[]{:S(2)}) async-start(bf16[16,16,128]{2,1,0:T(8,128)(2,1)} %get-tuple-element.27), calls=%async_computation.1 | async-start | bytes 131072 | tf_op jit(solution)/shard_map/all_to_all | solution.py:304
  65.1 0.0 copy-done.6
  65.1 2.8 %shard_map.159 = (bf16[32,16,2048]{2,1,0:T(8,128)(2,1)}, f32[1,2048]{1,0:T(1,128)}) custom-call(bf16[16,32,128]{2,1,0:T(8,128)(2,1)} %copy-done.6), custom_call_target="tpu_custom_call" | custom-call | tf_op jit(solution)/shard_map/pallas_call | solution.py:60
  67.9 8.8 %all-to-all-done.1.in_ref = bf16[16,16,128]{2,1,0:T(8,128)(2,1)S(1)} async-done(((bf16[16,16,128]{2,1,0:T(8,128)(2,1)}), bf16[16,16,128]{2,1,0:T(8,128)(2,1)S(1)}, u32[]{:S(2)}, u32[]{:S(2)}) %all-to-all-start.1) | async-done | bytes 65568 | tf_op jit(solution)/shard_map/all_to_all | solution.py:304
  76.7 0.0 copy-start.9
  76.7 0.6 copy-done.9
  77.3 2.8 %shard_map.160 = (bf16[32,16,2048]{2,1,0:T(8,128)(2,1)}, bf16[16,2048]{1,0:T(8,128)(2,1)}, f32[16,128]{1,0:T(8,128)}) custom-call(bf16[16,16,128]{2,1,0:T(8,128)(2,1)} %copy-done.9, f32[1,2048]{1,0:T(1,128)} %get-tuple-element.29.gain_ref), custom_call_target="tpu_custom_call" | custom-call | tf_op jit(solution)/shard_map/pallas_call | solution.py:60
  80.1 34.0 %all_to_all.50 = bf16[32,16,2048]{2,1,0:T(8,128)(2,1)S(1)} all-to-all(bf16[32,16,2048]{2,1,0:T(8,128)(2,1)} %get-tuple-element.30), channel_id=1, replica_groups=mesh['ctx'=32,'exp'=16] {'ctx'}, dimensions={0} | all-to-all | bytes 4194304 | tf_op jit(solution)/shard_map/all_to_all | solution.py:304
  114.1 0.0 copy-start.5
  114.1 4.6 %all-to-all-start.6 = ((bf16[32,16,2048]{2,1,0:T(8,128)(2,1)}), bf16[32,16,2048]{2,1,0:T(8,128)(2,1)}, u32[]{:S(2)}, u32[]{:S(2)}) async-start(bf16[32,16,2048]{2,1,0:T(8,128)(2,1)} %get-tuple-element.33), calls=%async_computation.6 | async-start | bytes 4194304 | tf_op jit(solution)/shard_map/all_to_all | solution.py:304
  118.7 0.0 copy-done.5
  118.7 0.0 copy-done
  118.7 1.5 fusion.7
  120.2 26.8 %all-to-all-done.6 = bf16[32,16,2048]{2,1,0:T(8,128)(2,1)} async-done(((bf16[32,16,2048]{2,1,0:T(8,128)(2,1)}), bf16[32,16,2048]{2,1,0:T(8,128)(2,1)}, u32[]{:S(2)}, u32[]{:S(2)}) %all-to-all-start.6) | async-done | bytes 2097184 | tf_op jit(solution)/shard_map/all_to_all | solution.py:304
  147.0 2.7 fusion.3
  149.8 2.1 convolution_convert_fusion
  151.9 4.5 %all-to-all-start.7 = ((bf16[32,16,2048]{2,1,0:T(8,128)(2,1)}), bf16[32,16,2048]{2,1,0:T(8,128)(2,1)S(1)}, u32[]{:S(2)}, u32[]{:S(2)}) async-start(bf16[32,16,2048]{2,1,0:T(8,128)(2,1)} %bitcast.28), calls=%async_computation.7 | async-start | bytes 4194304 | tf_op jit(solution)/shard_map/all_to_all | solution.py:304
  156.4 3.5 %convolution_convert_fusion.1 = bf16[512,2048]{1,0:T(8,128)(2,1)} fusion(bf16[1,256,2048]{2,1,0:T(8,128)(2,1)} %param.22, f32[512,256]{1,0:T(8,128)} %fusion.7), kind=kOutput, calls=%fused_computation.1 | convolution fusion | flops 538574848 | bytes 3670016 | tf_op jit(solution)/shard_map/dot_general | solution.py:20
  159.9 24.9 %all-to-all-done.7.parts_ref = bf16[32,16,2048]{2,1,0:T(8,128)(2,1)S(1)} async-done(((bf16[32,16,2048]{2,1,0:T(8,128)(2,1)}), bf16[32,16,2048]{2,1,0:T(8,128)(2,1)S(1)}, u32[]{:S(2)}, u32[]{:S(2)}) %all-to-all-start.7) | async-done | bytes 2097184 | tf_op jit(solution)/shard_map/all_to_all | solution.py:304
  184.8 0.0 copy-start.2
  184.8 1.4 copy-done.2
  186.2 4.5 %all-to-all-start.4 = ((bf16[32,16,2048]{2,1,0:T(8,128)(2,1)}), bf16[32,16,2048]{2,1,0:T(8,128)(2,1)S(1)}, u32[]{:S(2)}, u32[]{:S(2)}) async-start(bf16[32,16,2048]{2,1,0:T(8,128)(2,1)} %bitcast.31), calls=%async_computation.4 | async-start | bytes 4194304 | tf_op jit(solution)/shard_map/all_to_all | solution.py:304
  190.7 2.8 shard_map.163
  193.5 25.7 %all-to-all-done.4.parts_ref = bf16[32,16,2048]{2,1,0:T(8,128)(2,1)S(1)} async-done(((bf16[32,16,2048]{2,1,0:T(8,128)(2,1)}), bf16[32,16,2048]{2,1,0:T(8,128)(2,1)S(1)}, u32[]{:S(2)}, u32[]{:S(2)}) %all-to-all-start.4) | async-done | bytes 2097184 | tf_op jit(solution)/shard_map/all_to_all | solution.py:304
  219.2 0.0 copy-start.1
  219.2 3.5 %all-to-all-start.8 = ((bf16[16,16,128]{2,1,0:T(8,128)(2,1)}), bf16[16,16,128]{2,1,0:T(8,128)(2,1)S(1)}, u32[]{:S(2)}, u32[]{:S(2)}) async-start(bf16[16,16,128]{2,1,0:T(8,128)(2,1)} %shard_map.163), calls=%async_computation.8 | async-start | bytes 131072 | tf_op jit(solution)/shard_map/all_to_all | solution.py:304
  222.7 0.0 copy-done.1
  222.7 2.5 shard_map.161
  225.2 9.1 %all-to-all-done.8.rows_ref = bf16[16,16,128]{2,1,0:T(8,128)(2,1)S(1)} async-done(((bf16[16,16,128]{2,1,0:T(8,128)(2,1)}), bf16[16,16,128]{2,1,0:T(8,128)(2,1)S(1)}, u32[]{:S(2)}, u32[]{:S(2)}) %all-to-all-start.8) | async-done | bytes 65568 | tf_op jit(solution)/shard_map/all_to_all | solution.py:304
  234.3 0.0 copy-start.8
  234.3 3.8 %all-to-all-start.5 = ((bf16[16,16,128]{2,1,0:T(8,128)(2,1)}), bf16[16,16,128]{2,1,0:T(8,128)(2,1)S(1)}, u32[]{:S(2)}, u32[]{:S(2)}) async-start(bf16[16,16,128]{2,1,0:T(8,128)(2,1)} %shard_map.161), calls=%async_computation.5 | async-start | bytes 131072 | tf_op jit(solution)/shard_map/all_to_all | solution.py:304
  238.2 0.0 copy-done.8
  238.2 2.4 shard_map.164
  240.6 9.1 %all-to-all-done.5.rows_ref = bf16[16,16,128]{2,1,0:T(8,128)(2,1)S(1)} async-done(((bf16[16,16,128]{2,1,0:T(8,128)(2,1)}), bf16[16,16,128]{2,1,0:T(8,128)(2,1)S(1)}, u32[]{:S(2)}, u32[]{:S(2)}) %all-to-all-start.5) | async-done | bytes 65568 | tf_op jit(solution)/shard_map/all_to_all | solution.py:304
  249.7 6.5 %all-to-all-start.9 = ((bf16[32,128,128]{2,1,0:T(8,128)(2,1)}), bf16[32,128,128]{2,1,0:T(8,128)(2,1)S(1)}, u32[]{:S(2)}, u32[]{:S(2)}) async-start(bf16[32,128,128]{2,1,0:T(8,128)(2,1)} %get-tuple-element.37), calls=%async_computation.9 | async-start | bytes 2097152 | tf_op jit(solution)/shard_map/all_to_all | solution.py:304
  256.3 0.0 copy-start.12
  256.3 3.4 %fusion = bf16[1,2048,256]{2,1,0:T(8,128)(2,1)} fusion(bf16[512,2048]{1,0:T(8,128)(2,1)} %bitcast.30, bf16[512,256]{1,0:T(8,128)(2,1)S(1)} %fusion.3), kind=kOutput, calls=%fused_computation.4 | convolution fusion | flops 537395200 | bytes 3407872 | tf_op jit(solution)/shard_map/dot_general | solution.py:24
  259.7 0.0 copy-done.7
  259.7 0.0 copy-done.12
  259.7 3.3 %fusion.1 = bf16[1,256,2048]{2,1,0:T(8,128)(2,1)} fusion(bf16[512,2048]{1,0:T(8,128)(2,1)} %bitcast.8, f32[512,256]{1,0:T(8,128)S(1)} %copy-done.12), kind=kOutput, calls=%fused_computation.5 | convolution fusion | flops 538050560 | bytes 3670016 | tf_op jit(solution)/shard_map/dot_general | solution.py:24
  263.0 1.8 shard_map.165.local_ref
  264.8 1.7 shard_map.162
  266.5 6.7 %all-to-all-done.9.states_ref = bf16[32,128,128]{2,1,0:T(8,128)(2,1)S(1)} async-done(((bf16[32,128,128]{2,1,0:T(8,128)(2,1)}), bf16[32,128,128]{2,1,0:T(8,128)(2,1)S(1)}, u32[]{:S(2)}, u32[]{:S(2)}) %all-to-all-start.9) | async-done | bytes 1048608 | tf_op jit(solution)/shard_map/all_to_all | solution.py:304
  273.3 1.0 copy-done.4
  274.2 2.3 shard_map.166
  (2 shorter events, 0.0 us)
Async XLA Ops:
  0.6 118.0 %copy-start = (bf16[1,2048,256]{2,1,0:T(8,128)(2,1)S(1)}, bf16[1,2048,256]{2,1,0:T(8,128)(2,1)}, u32[]{:S(2)}) copy-start(bf16[1,2048,256]{2,1,0:T(8,128)(2,1)} %param.21) | copy-start | bytes 3145732
  0.6 14.5 %copy-start.11 = (f32[128,2]{0,1:T(2,128)S(1)}, f32[128,2]{0,1:T(2,128)}, u32[]{:S(2)}) copy-start(f32[128,2]{0,1:T(2,128)} %param.19) | copy-start | bytes 3076
  0.7 15.2 %copy-start.10 = (s32[128,2]{0,1:T(2,128)S(1)}, s32[128,2]{0,1:T(2,128)}, u32[]{:S(2)}) copy-start(s32[128,2]{0,1:T(2,128)} %param.20) | copy-start | bytes 3076
  4.7 28.9 %all-to-all-start = ((bf16[32,144,128]{2,1,0:T(8,128)(2,1)}), bf16[32,144,128]{2,1,0:T(8,128)(2,1)S(1)}, u32[]{:S(2)}, u32[]{:S(2)}) async-start(bf16[32,144,128]{2,1,0:T(8,128)(2,1)} %get-tuple-element.23), calls=%async_computation | async-start | bytes 2359296 | tf_op jit(solution)/shard_map/all_to_all | solution.py:304
  33.6 14.9 %copy-start.3 = (bf16[32,144,128]{2,1,0:T(8,128)(2,1)}, bf16[32,144,128]{2,1,0:T(8,128)(2,1)S(1)}, u32[]{:S(2)}) copy-start(bf16[32,144,128]{2,1,0:T(8,128)(2,1)S(1)} %all-to-all-done.states_ref) | copy-start | bytes 3538948
  33.6 25.1 %all-to-all-start.2 = ((bf16[16,32,128]{2,1,0:T(8,128)(2,1)}), bf16[16,32,128]{2,1,0:T(8,128)(2,1)S(1)}, u32[]{:S(2)}, u32[]{:S(2)}) async-start(bf16[16,32,128]{2,1,0:T(8,128)(2,1)} %get-tuple-element.28), calls=%async_computation.2 | async-start | bytes 262144 | tf_op jit(solution)/shard_map/all_to_all | solution.py:304
  58.6 6.5 %copy-start.6 = (bf16[16,32,128]{2,1,0:T(8,128)(2,1)}, bf16[16,32,128]{2,1,0:T(8,128)(2,1)S(1)}, u32[]{:S(2)}) copy-start(bf16[16,32,128]{2,1,0:T(8,128)(2,1)S(1)} %all-to-all-done.2.in_ref) | copy-start | bytes 393220
  58.6 18.1 %all-to-all-start.1 = ((bf16[16,16,128]{2,1,0:T(8,128)(2,1)}), bf16[16,16,128]{2,1,0:T(8,128)(2,1)S(1)}, u32[]{:S(2)}, u32[]{:S(2)}) async-start(bf16[16,16,128]{2,1,0:T(8,128)(2,1)} %get-tuple-element.27), calls=%async_computation.1 | async-start | bytes 131072 | tf_op jit(solution)/shard_map/all_to_all | solution.py:304
  76.7 0.6 copy-start.9
  114.1 4.6 %copy-start.5 = (bf16[32,16,2048]{2,1,0:T(8,128)(2,1)}, bf16[32,16,2048]{2,1,0:T(8,128)(2,1)S(1)}, u32[]{:S(2)}) copy-start(bf16[32,16,2048]{2,1,0:T(8,128)(2,1)S(1)} %all_to_all.50) | copy-start | bytes 6291460
  114.1 32.9 %all-to-all-start.6 = ((bf16[32,16,2048]{2,1,0:T(8,128)(2,1)}), bf16[32,16,2048]{2,1,0:T(8,128)(2,1)}, u32[]{:S(2)}, u32[]{:S(2)}) async-start(bf16[32,16,2048]{2,1,0:T(8,128)(2,1)} %get-tuple-element.33), calls=%async_computation.6 | async-start | bytes 4194304 | tf_op jit(solution)/shard_map/all_to_all | solution.py:304
  151.9 32.9 %all-to-all-start.7 = ((bf16[32,16,2048]{2,1,0:T(8,128)(2,1)}), bf16[32,16,2048]{2,1,0:T(8,128)(2,1)S(1)}, u32[]{:S(2)}, u32[]{:S(2)}) async-start(bf16[32,16,2048]{2,1,0:T(8,128)(2,1)} %bitcast.28), calls=%async_computation.7 | async-start | bytes 4194304 | tf_op jit(solution)/shard_map/all_to_all | solution.py:304
  184.8 1.4 copy-start.2
  186.2 32.9 %all-to-all-start.4 = ((bf16[32,16,2048]{2,1,0:T(8,128)(2,1)}), bf16[32,16,2048]{2,1,0:T(8,128)(2,1)S(1)}, u32[]{:S(2)}, u32[]{:S(2)}) async-start(bf16[32,16,2048]{2,1,0:T(8,128)(2,1)} %bitcast.31), calls=%async_computation.4 | async-start | bytes 4194304 | tf_op jit(solution)/shard_map/all_to_all | solution.py:304
  219.2 3.5 %copy-start.1 = (bf16[32,16,2048]{2,1,0:T(8,128)(2,1)}, bf16[32,16,2048]{2,1,0:T(8,128)(2,1)S(1)}, u32[]{:S(2)}) copy-start(bf16[32,16,2048]{2,1,0:T(8,128)(2,1)S(1)} %all-to-all-done.4.parts_ref) | copy-start | bytes 6291460
  219.2 15.1 %all-to-all-start.8 = ((bf16[16,16,128]{2,1,0:T(8,128)(2,1)}), bf16[16,16,128]{2,1,0:T(8,128)(2,1)S(1)}, u32[]{:S(2)}, u32[]{:S(2)}) async-start(bf16[16,16,128]{2,1,0:T(8,128)(2,1)} %shard_map.163), calls=%async_computation.8 | async-start | bytes 131072 | tf_op jit(solution)/shard_map/all_to_all | solution.py:304
  234.3 3.9 %copy-start.8 = (bf16[16,16,128]{2,1,0:T(8,128)(2,1)}, bf16[16,16,128]{2,1,0:T(8,128)(2,1)S(1)}, u32[]{:S(2)}) copy-start(bf16[16,16,128]{2,1,0:T(8,128)(2,1)S(1)} %all-to-all-done.8.rows_ref) | copy-start | bytes 196612
  234.3 15.4 %all-to-all-start.5 = ((bf16[16,16,128]{2,1,0:T(8,128)(2,1)}), bf16[16,16,128]{2,1,0:T(8,128)(2,1)S(1)}, u32[]{:S(2)}, u32[]{:S(2)}) async-start(bf16[16,16,128]{2,1,0:T(8,128)(2,1)} %shard_map.161), calls=%async_computation.5 | async-start | bytes 131072 | tf_op jit(solution)/shard_map/all_to_all | solution.py:304
  249.7 9.9 %copy-start.7 = (bf16[16,16,128]{2,1,0:T(8,128)(2,1)}, bf16[16,16,128]{2,1,0:T(8,128)(2,1)S(1)}, u32[]{:S(2)}) copy-start(bf16[16,16,128]{2,1,0:T(8,128)(2,1)S(1)} %all-to-all-done.5.rows_ref) | copy-start | bytes 196612
  249.7 23.5 %all-to-all-start.9 = ((bf16[32,128,128]{2,1,0:T(8,128)(2,1)}), bf16[32,128,128]{2,1,0:T(8,128)(2,1)S(1)}, u32[]{:S(2)}, u32[]{:S(2)}) async-start(bf16[32,128,128]{2,1,0:T(8,128)(2,1)} %get-tuple-element.37), calls=%async_computation.9 | async-start | bytes 2097152 | tf_op jit(solution)/shard_map/all_to_all | solution.py:304
  256.3 3.4 %copy-start.12 = (f32[512,256]{1,0:T(8,128)S(1)}, f32[512,256]{1,0:T(8,128)}, u32[]{:S(2)}) copy-start(f32[512,256]{1,0:T(8,128)} %fusion.7) | copy-start | bytes 1572868
  273.3 1.0 copy-start.4

commit v2 on v1

--- a/solution.py
+++ b/solution.py
@@ -183,7 +183,7 @@
     return total
 
 
-def mixed_kernel(me_ref, states_ref, c_ref, cum_ref, local_ref, table_ref, mixed_ref, rows_ref, later_ref):
+def mixed_kernel(me_ref, states_ref, c_ref, cum_ref, local_ref, table_ref, early_ref, mixed_ref, pay_ref, later_ref):
     blocks = states_ref.shape[0]
     states = c_ref.shape[1]
     me = me_ref[0]
@@ -198,73 +198,93 @@
     total = local_ref[...] + jnp.exp(cum_ref[...]) * (mm(c, high) + mm(c, low))
     mixed = total.astype(bf16)
     mixed_ref[...] = mixed
-    rows_ref[...] = mm(table_ref[...], mixed).astype(bf16).reshape(rows_ref.shape)
+    experts, total_rows, features = pay_ref.shape
+    capacity = table_ref.shape[0] // experts
+    pay_ref[:, :capacity, :] = (
+        mm(table_ref[...], mixed).astype(bf16).reshape(experts, capacity, features)
+    )
+    pay_ref[:, capacity:, :] = early_ref[...]
     mask = ones_where((between < source) & (between > me))
     sums = mm(mask, parts[0]) + mm(mask, parts[1]) + mm(mask, parts[2])
     later_ref[...] = jnp.where(which > me, jnp.exp(sums), 0.0)
 
 
-def cot_kernel(in_ref, out_ref, gain_ref):
-    peers, capacity, features = in_ref.shape[0], out_ref.shape[1], in_ref.shape[2]
-    for e in range(peers):
-        here = slice(e * features, (e + 1) * features)
-        piece = in_ref[e, :capacity, :]
-        for j in range(out_ref.shape[0]):
-            out_ref[j, :, here] = piece
-        extra = in_ref[e, capacity : 2 * capacity, :].astype(f32)
-        gain_ref[:, here] = jnp.sum(extra, axis=0, keepdims=True)
-
-
-def norm_kernel(in_ref, gain_ref, out_ref, raw_ref, inv_ref):
-    peers, capacity, features = in_ref.shape
+def norm_kernel(in_ref, out_ref, raw_ref, inv_ref, gain_ref):
+    peers, _, features = in_ref.shape
+    capacity = raw_ref.shape[0]
     square = jnp.zeros((capacity, features), f32)
     for e in range(peers):
-        piece = in_ref[e].astype(f32)
+        piece = in_ref[e, :capacity, :].astype(f32)
         square = square + piece * piece
     inv = lax.rsqrt(jnp.sum(square, axis=1, keepdims=True) / D + epsilon)
     inv_ref[...] = jnp.broadcast_to(inv, inv_ref.shape)
     for e in range(peers):
         here = slice(e * features, (e + 1) * features)
-        piece = in_ref[e]
+        piece = in_ref[e, :capacity, :]
+        cot = in_ref[e, capacity : 2 * capacity, :]
+        gain = jnp.sum(in_ref[e, 2 * capacity :, :].astype(f32), axis=0, keepdims=True)
+        gain_ref[:, here] = gain
         raw_ref[:, here] = piece
-        normed = (piece.astype(f32) * inv * gain_ref[:, here]).astype(bf16)
+        normed = (piece.astype(f32) * inv * gain).astype(bf16)
         for j in range(out_ref.shape[0]):
-            out_ref[j, :, here] = normed
-
-
-def grad_rows_kernel(parts_ref, raw_ref, inv_ref, gain_ref, out_ref):
-    peers, capacity, features = out_ref.shape
+            out_ref[j, :capacity, here] = normed
+            out_ref[j, capacity:, here] = cot
+
+
+def expert_kernel(rows_ref, in_ref, in_peer_ref, down_ref, down_peer_ref, parts_ref, mine_ref, peer_ref):
+    chips, both, width = rows_ref.shape
+    capacity = both // 2
+    count = chips * capacity
+    rows = rows_ref[:, :capacity, :].reshape(count, width)
+    cot = rows_ref[:, capacity:, :].reshape(count, width)
+    d_total = None
+    out_total = None
+    for wide, narrow, kept in ((in_ref, down_ref, mine_ref), (in_peer_ref, down_peer_ref, peer_ref)):
+        hidden = mm(rows, wide[...])
+        d_act = mm_nt(cot, narrow[...])
+        sigmoid_h = 1.0 / (1.0 + jnp.exp(-hidden))
+        activated = (hidden * sigmoid_h).astype(bf16)
+        d_hidden = (d_act * sigmoid_h * (1.0 + hidden * (1.0 - sigmoid_h))).astype(bf16)
+        kept[0] = activated
+        kept[1] = d_hidden
+        d_part = mm_nt(d_hidden, wide[...])
+        out_part = mm(activated, narrow[...])
+        d_total = d_part if d_total is None else d_total + d_part
+        out_total = out_part if out_total is None else out_total + out_part
+    parts_ref[:, :capacity, :] = d_total.astype(bf16).reshape(chips, capacity, width)
+    parts_ref[:, capacity:, :] = out_total.astype(bf16).reshape(chips, capacity, width)
+
+
+def return_kernel(parts_ref, raw_ref, inv_ref, gain_ref, out_ref):
+    peers, both, features = out_ref.shape
+    capacity = both // 2
     total = parts_ref[0].astype(f32)
     for j in range(1, parts_ref.shape[0]):
         total = total + parts_ref[j].astype(f32)
-    total = total.astype(bf16).astype(f32)
-    scaled = gain_ref[...] * total
+    d_rows = total[:capacity].astype(bf16).astype(f32)
+    out_rows = total[capacity:]
+    scaled = gain_ref[...] * d_rows
     raw = raw_ref[...].astype(f32)
     inv = inv_ref[:, 0:1]
     inner = jnp.sum(scaled * raw, axis=1, keepdims=True)
     result = inv * scaled - raw * (inv * inv * inv * inner / D)
     for e in range(peers):
-        out_ref[e] = result[:, e * features : (e + 1) * features].astype(bf16)
-
-
-def out_rows_kernel(parts_ref, out_ref):
-    peers, capacity, features = out_ref.shape
-    total = parts_ref[0].astype(f32)
-    for j in range(1, parts_ref.shape[0]):
-        total = total + parts_ref[j].astype(f32)
-    for e in range(peers):
-        out_ref[e] = total[:, e * features : (e + 1) * features].astype(bf16)
+        here = slice(e * features, (e + 1) * features)
+        out_ref[e, :capacity, :] = result[:, here].astype(bf16)
+        out_ref[e, capacity:, :] = out_rows[:, here].astype(bf16)
 
 
 def block_out_kernel(rows_ref, from_ref, weight_ref, mixed_ref, out_ref):
-    rows = rows_ref[...].reshape(from_ref.shape[2], rows_ref.shape[2])
+    half = rows_ref.shape[1] // 2
+    rows = rows_ref[:, half:, :].reshape(from_ref.shape[2], rows_ref.shape[2])
     total = mixed_ref[...].astype(f32)
     extra = weight_ref[:, 0:1] * mm(from_ref[0], rows) + weight_ref[:, 1:2] * mm(from_ref[1], rows)
     out_ref[...] = (total + extra).astype(bf16)
 
 
 def cot_state_kernel(rows_ref, from_ref, grad_ref, c_ref, cum_ref, residual_ref, wide_ref, pay_ref):
-    rows = rows_ref[...].reshape(from_ref.shape[2], rows_ref.shape[2])
+    half = rows_ref.shape[1] // 2
+    rows = rows_ref[:, :half, :].reshape(from_ref.shape[2], rows_ref.shape[2])
     table = from_ref[0] + from_ref[1]
     total = grad_ref[...].astype(f32) + mm(table, rows)
     wide_ref[...] = total
@@ -300,8 +320,10 @@
     out_ref[...] = (local_ref[...] + tail * (mm(b, high) + mm(b, low))).astype(bf16)
 
 
-def swap(a, axis):
-    return lax.all_to_all(a, axis, split_axis=0, concat_axis=0, tiled=True)
+def swap(a, axis, groups=None):
+    return lax.all_to_all(
+        a, axis, split_axis=0, concat_axis=0, tiled=True, axis_index_groups=groups
+    )
 
 
 def body(
@@ -330,12 +352,21 @@
     matrix_in = weight_in[0]
     matrix_down = weight_down[0]
 
+    chips = blocks // 2
+    same_core = [[2 * chip + core for chip in range(chips)] for core in range(2)]
+    partners = [(i, i ^ 1) for i in range(blocks)]
+
+    def partner(a):
+        return lax.ppermute(a, "ctx", partners)
+
     state_pay, cum = call(
         state_kernel,
         (shape_of((blocks, states + 16, features), bf16), shape_of((tokens, features), f32)),
         ssd_input, state_in, log_decay,
     )
     state_all = swap(state_pay, "ctx")
+    peer_in = partner(matrix_in)
+    peer_down = partner(matrix_down)
 
     to_rows, from_rows, cot_pay = call(
         route_kernel,
@@ -346,59 +377,60 @@
         ),
         expert_ids, expert_ids.T, route_weight, out_grad, norm_gain.reshape(1, features),
     )
-    cot_arrived = swap(cot_pay, "exp")
     local, back = call(
         local_kernel,
         (shape_of((tokens, features), f32), shape_of((2, heads, tokens, tokens), bf16)),
         ssd_input, state_in, state_out, cum, skip, residual,
     )
-    cot_spread, gain = call(
-        cot_kernel,
-        (shape_of((blocks, capacity, D), bf16), shape_of((1, D), f32)),
-        cot_arrived,
-    )
-    cot_rows = swap(cot_spread, "ctx").reshape(blocks * capacity, D)
-    d_act = mm_nt(cot_rows, matrix_down)
-
-    mixed, mixed_rows, later = call(
+    mixed, rows_pay, later = call(
         mixed_kernel,
         (
             shape_of((tokens, features), bf16),
-            shape_of((experts, capacity, features), bf16),
+            shape_of((experts, 3 * capacity, features), bf16),
             shape_of((blocks, features), f32),
         ),
-        me, state_all, state_out, cum, local, to_rows,
+        me, state_all, state_out, cum, local, to_rows, cot_pay,
         smem=(0,),
     )
-    arrived = swap(mixed_rows, "exp")
-    normed_spread, raw, inv = call(
+    arrived = swap(rows_pay, "exp")
+    spread, raw, inv, gain = call(
         norm_kernel,
         (
-            shape_of((blocks, capacity, D), bf16),
+            shape_of((chips, 2 * capacity, D), bf16),
             shape_of((capacity, D), bf16),
             shape_of((capacity, 128), f32),
-        ),
-        arrived, gain,
-    )
-    expert_rows = swap(normed_spread, "ctx").reshape(blocks * capacity, D)
-
-    hidden = mm(expert_rows, matrix_in)
-    sigmoid_h = jax.nn.sigmoid(hidden)
-    d_hidden = (d_act * sigmoid_h * (1.0 + hidden * (1.0 - sigmoid_h))).astype(bf16)
-    d_parts = mm_nt(d_hidden, matrix_in).astype(bf16).reshape(blocks, capacity, D)
-    d_all = swap(d_parts, "ctx")
-    activated = (hidden * sigmoid_h).astype(bf16)
-    out_parts = mm(activated, matrix_down).astype(bf16).reshape(blocks, capacity, D)
-    out_all = swap(out_parts, "ctx")
-    grad_down = mm_t(activated, cot_rows).astype(bf16)
-    grad_in = mm_t(expert_rows, d_hidden).astype(bf16)
-
-    d_back = call(
-        grad_rows_kernel, shape_of((experts, capacity, features), bf16), d_all, raw, inv, gain
-    )
-    d_returned = swap(d_back, "exp")
-    out_back = call(out_rows_kernel, shape_of((experts, capacity, features), bf16), out_all)
-    out_returned = swap(out_back, "exp")
+            shape_of((1, D), f32),
+        ),
+        arrived,
+    )
+    expert_rows = swap(spread, "ctx", same_core)
+
+    units = matrix_in.shape[1]
+    count = chips * capacity
+    parts, mine, peer = call(
+        expert_kernel,
+        (
+            shape_of((chips, 2 * capacity, D), bf16),
+            shape_of((2, count, units), bf16),
+            shape_of((2, count, units), bf16),
+        ),
+        expert_rows, matrix_in, peer_in, matrix_down, peer_down,
+    )
+    parts_all = swap(parts, "ctx", same_core)
+    peer_rows = partner(expert_rows)
+    peer_units = partner(peer)
+    all_rows = jnp.concatenate([expert_rows[:, :capacity], peer_rows[:, :capacity]]).reshape(-1, D)
+    all_cot = jnp.concatenate([expert_rows[:, capacity:], peer_rows[:, capacity:]]).reshape(-1, D)
+    all_units = jnp.concatenate([mine, peer_units], axis=1)
+    grad_down = mm_t(all_units[0], all_cot).astype(bf16)
+    grad_in = mm_t(all_rows, all_units[1]).astype(bf16)
+
+    back_pay = call(
+        return_kernel,
+        shape_of((experts, 2 * capacity, features), bf16),
+        parts_all, raw, inv, gain,
+    )
+    returned = swap(back_pay, "exp")
 
     grad_residual, wide, cot_pay_state = call(
         cot_state_kernel,
@@ -407,14 +439,14 @@
             shape_of((tokens, features), f32),
             shape_of((blocks, states, features), bf16),
         ),
-        d_returned, from_rows, out_grad, state_out, cum,
+        returned, from_rows, out_grad, state_out, cum,
     )
     cot_states = swap(cot_pay_state, "ctx")
     back_local = call(
         back_local_kernel, shape_of((tokens, features), f32), wide, back, skip
     )
     block_out = call(
-        block_out_kernel, shape_of((tokens, features), bf16), out_returned, from_rows, route_weight, mixed
+        block_out_kernel, shape_of((tokens, features), bf16), returned, from_rows, route_weight, mixed
     )
     grad_input = call(
         final_kernel, shape_of((tokens, features), bf16), cot_states, later, state_in, cum, back_local

time: 278 us -> 195 us (0.70)
  waiting for transfers between devices: 133 us -> 59.7 us
  matrix products: 16.6 us -> 5.35 us
  blocking collectives: 34 us -> 26.3 us
  local copies, waits for them, and re-layouts: 6.02 us -> 12.9 us
    all_to_all x9 -> x5, waiting for transfers between devices: 133 us -> 57.7 us  [swap(): lax.all_to_all(a, axis, split_axis=0, concat_axis=0, tiled=True, axis_ind...]
    ppermute x0 -> x4, starting transfers between devices: none -> 15.9 us  [partner(): return lax.ppermute(a, 'ctx', partners)]
    all_to_all x9 -> x5, starting transfers between devices: 57.3 us -> 43 us  [swap(): lax.all_to_all(a, axis, split_axis=0, concat_axis=0, tiled=True, axis_ind...]
    dot_general x4 -> x0, matrix products: 9.9 us -> none  [the longest x2 5.01 us: mm(): return jnp.dot(a, b, preferred_element_type=f32)]
    all_to_all x1, blocking collectives: 34 us -> 26.3 us  [swap(): lax.all_to_all(a, axis, split_axis=0, concat_axis=0, tiled=True, axis_ind...]
    slice x0 -> x2, local copies, waits for them, and re-layouts: none -> 3.28 us  [the longest x1 1.83 us: body(): peer_rows[:, capacity:]]
    unnamed x29 -> x30, local copies, waits for them, and re-layouts: 6.02 us -> 8.95 us
    pallas_call x12 -> x11, Pallas kernels: 28.4 us -> 29.7 us  [call(): pl.pallas_call(kernel, out_shape=outs, in_specs=[pl.BlockSpec(memory_spac...]
  transfers between devices with their start and end apart: 9 -> 9, of which waited for: 9 -> 7; matrix products, arithmetic and copies ran while one was open for 5% -> 6% of each run, Pallas kernels for 8% -> 7%
where the time goes in v2:
time: 195 us; the launch traced here: 194 us
  waiting for transfers between devices  59.7 us (31%)
  starting transfers between devices  58.9 us (30%)
  Pallas kernels  29.7 us (15%)
  blocking collectives  26.3 us (13%)
  local copies, waits for them, and re-layouts  12.9 us (7%)
  matrix products  5.35 us (3%)
    all_to_all x5, waiting for transfers between devices, swap(): lax.all_to_all(a, axis, split_axis=0, concat_axis=0, tiled=True, axis_ind...  57.7 us
    all_to_all x5, starting transfers between devices, swap(): lax.all_to_all(a, axis, split_axis=0, concat_axis=0, tiled=True, axis_ind...  43 us
    pallas_call x11, Pallas kernels, call(): pl.pallas_call(kernel, out_shape=outs, in_specs=[pl.BlockSpec(memory_spac...  29.7 us
    all_to_all x1, blocking collectives, swap(): lax.all_to_all(a, axis, split_axis=0, concat_axis=0, tiled=True, axis_ind...  26.3 us
    ppermute x4, starting transfers between devices, partner(): return lax.ppermute(a, 'ctx', partners)  15.9 us
    unnamed x30, local copies, waits for them, and re-layouts  8.95 us
    dot_general x2, matrix products, mm_t(): lax.dot_general(a, b, (((0,), (0,)), ((), ())), preferred_element_type=f32)  5.35 us
  transfers between devices with their start and end apart: 9, of which 7 were waited for; matrix products, arithmetic and copies ran while one was open for 6% of the time, Pallas kernels for 7%

profile of v2, /device:TPU:1, one launch (start us, length us, event | category | flops | bytes accessed | tf_op | source)
XLA Modules:
  0.0 194.1 jit_solution(17969258750340382550)
XLA Ops:
  0.6 0.0 copy-start.11
  0.6 0.0 copy-start.10
  0.7 1.4 copy.17.decay_ref
  2.1 2.5 %shard_map.155 = (bf16[32,144,128]{2,1,0:T(8,128)(2,1)}, f32[128,128]{1,0:T(8,128)}) custom-call(bf16[128,128]{1,0:T(8,128)(2,1)} %x_ref.3, bf16[128,128]{1,0:T(8,128)(2,1)} %b_ref.5, f32[128,4]{1,0:T(8,128)} %copy.17.decay_ref), custom_call_target="tpu_custom_call" | custom-call | tf_op jit(solution)/shard_map/pallas_call | solution.py:60
  4.6 10.4 %all-to-all-start = ((bf16[32,144,128]{2,1,0:T(8,128)(2,1)}), bf16[32,144,128]{2,1,0:T(8,128)(2,1)S(1)}, u32[]{:S(2)}, u32[]{:S(2)}) async-start(bf16[32,144,128]{2,1,0:T(8,128)(2,1)} %get-tuple-element.25), calls=%async_computation | async-start | bytes 2359296 | tf_op jit(solution)/shard_map/all_to_all | solution.py:324
  15.0 0.0 copy-done.11
  15.0 0.7 copy.19.weight_ref
  15.7 0.0 copy-done.10
  15.7 0.7 copy.18.ids_ref
  16.5 1.9 %shard_map.156 = (f32[128,128]{1,0:T(8,128)}, bf16[2,4,128,128]{3,2,1,0:T(8,128)(2,1)}) custom-call(bf16[128,128]{1,0:T(8,128)(2,1)} %x_ref.3, bf16[128,128]{1,0:T(8,128)(2,1)} %b_ref.5, bf16[128,128]{1,0:T(8,128)(2,1)} %c_ref.5, f32[128,128]{1,0:T(8,128)} %get-tuple-element.26.cum_ref, f32[1,4]{1,0:T(1,128)} %bitcast.27, bf16[128,128]{1,0:T(8,128)(2,1)} %residual_ref.1), custom_call_target="tpu_custom_call" | custom-call | tf_op jit(solution)/shard_map/pallas_call | solution.py:60
  18.4 2.0 %shard_map.157 = (bf16[256,128]{1,0:T(8,128)(2,1)}, bf16[2,128,256]{2,1,0:T(8,128)(2,1)}, bf16[16,32,128]{2,1,0:T(8,128)(2,1)}) custom-call(s32[128,2]{1,0:T(8,128)} %copy.18.ids_ref, s32[2,128]{1,0:T(2,128)} %bitcast.26, f32[128,2]{1,0:T(8,128)} %copy.19.weight_ref, bf16[128,128]{1,0:T(8,128)(2,1)} %grad_ref.3, f32[1,128]{1,0:T(1,128)} %bitcast.29), custom_call_target="tpu_custom_call" | custom-call | tf_op jit(solution)/shard_map/pallas_call | solution.py:60
  20.5 13.0 %all-to-all-done.states_ref = bf16[32,144,128]{2,1,0:T(8,128)(2,1)S(1)} async-done(((bf16[32,144,128]{2,1,0:T(8,128)(2,1)}), bf16[32,144,128]{2,1,0:T(8,128)(2,1)S(1)}, u32[]{:S(2)}, u32[]{:S(2)}) %all-to-all-start) | async-done | bytes 1179680 | tf_op jit(solution)/shard_map/all_to_all | solution.py:324
  33.5 0.0 copy-start.2
  33.5 1.0 copy-done.2
  34.5 2.8 %shard_map.158 = (bf16[128,128]{1,0:T(8,128)(2,1)}, bf16[16,48,128]{2,1,0:T(8,128)(2,1)}, f32[32,128]{1,0:T(8,128)}) custom-call(s32[1]{0:T(128)} %bitcast.me_ref, bf16[32,144,128]{2,1,0:T(8,128)(2,1)} %copy-done.2, bf16[128,128]{1,0:T(8,128)(2,1)} %c_ref.5, f32[128,128]{1,0:T(8,128)} %get-tuple-element.26.cum_ref, f32[128,128]{1,0:T(8,128)} %get-tuple-element.27.local_ref, ...), custom_call_target="tpu_custom_call" | custom-call | tf_op jit(solution)/shard_map/pallas_call | solution.py:60
  37.3 26.3 %all_to_all.30.in_ref = bf16[16,48,128]{2,1,0:T(8,128)(2,1)} all-to-all(bf16[16,48,128]{2,1,0:T(8,128)(2,1)} %get-tuple-element.30), channel_id=1, replica_groups=mesh['ctx'=32,'exp'=16] {'exp'}, dimensions={0} | all-to-all | bytes 393216 | tf_op jit(solution)/shard_map/all_to_all | solution.py:324
  63.6 2.8 %shard_map.159 = (bf16[16,32,2048]{2,1,0:T(8,128)(2,1)}, bf16[16,2048]{1,0:T(8,128)(2,1)}, f32[16,128]{1,0:T(8,128)}, f32[1,2048]{1,0:T(1,128)}) custom-call(bf16[16,48,128]{2,1,0:T(8,128)(2,1)} %all_to_all.30.in_ref), custom_call_target="tpu_custom_call" | custom-call | tf_op jit(solution)/shard_map/pallas_call | solution.py:60
  66.3 0.0 copy-start.7
  66.3 3.9 %all-to-all-start.2 = ((bf16[16,32,2048]{2,1,0:T(8,128)(2,1)}), bf16[16,32,2048]{2,1,0:T(8,128)(2,1)S(1)}, u32[]{:S(2)}, u32[]{:S(2)}) async-start(bf16[16,32,2048]{2,1,0:T(8,128)(2,1)} %get-tuple-element.31), calls=%async_computation.2 | async-start | bytes 4194304 | tf_op jit(solution)/shard_map/all_to_all | solution.py:324
  70.2 0.0 copy-done.7
  70.2 5.5 %collective-permute-start = (bf16[2048,256]{1,0:T(8,128)(2,1)S(1)}, bf16[2048,256]{1,0:T(8,128)(2,1)S(1)}, u32[]{:S(2)}, u32[]{:S(2)}) collective-permute-start(bf16[2048,256]{1,0:T(8,128)(2,1)S(1)} %bitcast.23), channel_id=1, source_target_pairs={{0,16},{16,0},{32,48},{48,32},{64,80},{80,64},{96,112},{112,96},{1... | collective-permute-start | bytes 3145736 | tf_op jit(solution)/shard_map/ppermute | solution.py:360
  75.7 1.9 collective-permute-start.1
  77.6 0.3 collective-permute-done.in_peer_ref
  77.9 0.0 copy-start.8
  78.0 1.0 copy-done.8
  78.9 1.7 collective-permute-done.1.down_peer_ref
  80.6 14.8 %all-to-all-done.2.rows_ref = bf16[16,32,2048]{2,1,0:T(8,128)(2,1)S(1)} async-done(((bf16[16,32,2048]{2,1,0:T(8,128)(2,1)}), bf16[16,32,2048]{2,1,0:T(8,128)(2,1)S(1)}, u32[]{:S(2)}, u32[]{:S(2)}) %all-to-all-start.2) | async-done | bytes 2097184 | tf_op jit(solution)/shard_map/all_to_all | solution.py:324
  95.3 0.0 copy-start
  95.3 1.3 copy-done
  96.7 6.7 %shard_map.160 = (bf16[16,32,2048]{2,1,0:T(8,128)(2,1)}, bf16[2,256,256]{2,1,0:T(8,128)(2,1)}, bf16[2,256,256]{2,1,0:T(8,128)(2,1)}) custom-call(bf16[16,32,2048]{2,1,0:T(8,128)(2,1)} %copy-done, bf16[2048,256]{1,0:T(8,128)(2,1)} %bitcast.22, bf16[2048,256]{1,0:T(8,128)(2,1)} %copy-done.8, bf16[256,2048]{1,0:T(8,128)(2,1)} %bitcast.25, ...), custom_call_target="tpu_custom_call" | custom-call | tf_op jit(solution)/shard_map/pallas_call | solution.py:60
  103.4 0.0 copy-start.1
  103.4 0.0 copy-start.12
  103.4 6.0 %all-to-all-start.3 = ((bf16[16,32,2048]{2,1,0:T(8,128)(2,1)}), bf16[16,32,2048]{2,1,0:T(8,128)(2,1)}, u32[]{:S(2)}, u32[]{:S(2)}) async-start(bf16[16,32,2048]{2,1,0:T(8,128)(2,1)} %get-tuple-element.32), calls=%async_computation.3 | async-start | bytes 4194304 | tf_op jit(solution)/shard_map/all_to_all | solution.py:324
  109.4 0.0 copy-done.1
  109.4 6.6 %collective-permute-start.2 = (bf16[16,32,2048]{2,1,0:T(8,128)(2,1)S(1)}, bf16[16,32,2048]{2,1,0:T(8,128)(2,1)}, u32[]{:S(2)}, u32[]{:S(2)}) collective-permute-start(bf16[16,32,2048]{2,1,0:T(8,128)(2,1)S(1)} %copy-done.1), channel_id=1, source_target_pairs={{0,16},{16,0},{32,48},{48,32},{64,80},{80,64},{96,112},{112,96},{1... | collective-permute-start | bytes 6291464 | tf_op jit(solution)/shard_map/ppermute | solution.py:360
  116.0 0.0 copy-done.12
  116.0 1.9 collective-permute-start.3
  117.9 15.5 %all-to-all-done.3.parts_ref = bf16[16,32,2048]{2,1,0:T(8,128)(2,1)} async-done(((bf16[16,32,2048]{2,1,0:T(8,128)(2,1)}), bf16[16,32,2048]{2,1,0:T(8,128)(2,1)}, u32[]{:S(2)}, u32[]{:S(2)}) %all-to-all-start.3) | async-done | bytes 2097184 | tf_op jit(solution)/shard_map/all_to_all | solution.py:324
  133.4 2.7 %shard_map.161 = bf16[16,32,128]{2,1,0:T(8,128)(2,1)} custom-call(bf16[16,32,2048]{2,1,0:T(8,128)(2,1)} %all-to-all-done.3.parts_ref, bf16[16,2048]{1,0:T(8,128)(2,1)} %get-tuple-element.33.raw_ref, f32[16,128]{1,0:T(8,128)} %get-tuple-element.34.inv_ref, f32[1,2048]{1,0:T(1,128)} %get-tuple-element.35.gain_ref), custom_call_target="tpu_custom_call" | custom-call | tf_op jit(solution)/shard_map/pallas_call | solution.py:60
  136.1 12.6 %all-to-all-start.4 = ((bf16[16,32,128]{2,1,0:T(8,128)(2,1)}), bf16[16,32,128]{2,1,0:T(8,128)(2,1)S(1)}, u32[]{:S(2)}, u32[]{:S(2)}) async-start(bf16[16,32,128]{2,1,0:T(8,128)(2,1)} %shard_map.161), calls=%async_computation.4 | async-start | bytes 262144 | tf_op jit(solution)/shard_map/all_to_all | solution.py:324
  148.7 0.0 copy-start.9
  148.7 1.5 fusion.2
  150.2 0.0 copy-done.9
  150.2 0.7 constant_dynamic-update-slice_fusion.1
  150.9 0.0 collective-permute-done.3
  150.9 0.7 constant_dynamic-update-slice_fusion
  151.6 9.1 %all-to-all-done.4.rows_ref = bf16[16,32,128]{2,1,0:T(8,128)(2,1)S(1)} async-done(((bf16[16,32,128]{2,1,0:T(8,128)(2,1)}), bf16[16,32,128]{2,1,0:T(8,128)(2,1)S(1)}, u32[]{:S(2)}, u32[]{:S(2)}) %all-to-all-start.4) | async-done | bytes 131104 | tf_op jit(solution)/shard_map/all_to_all | solution.py:324
  160.7 0.7 copy-done.6
  161.4 2.4 %shard_map.163 = (bf16[128,128]{1,0:T(8,128)(2,1)}, f32[128,128]{1,0:T(8,128)}, bf16[32,128,128]{2,1,0:T(8,128)(2,1)}) custom-call(bf16[16,32,128]{2,1,0:T(8,128)(2,1)} %copy-done.6, bf16[2,128,256]{2,1,0:T(8,128)(2,1)} %get-tuple-element.36.from_ref, bf16[128,128]{1,0:T(8,128)(2,1)} %grad_ref.3, bf16[128,128]{1,0:T(8,128)(2,1)} %c_ref.5, ...), custom_call_target="tpu_custom_call" | custom-call | tf_op jit(solution)/shard_map/pallas_call | solution.py:60
  163.8 10.2 %all-to-all-start.5 = ((bf16[32,128,128]{2,1,0:T(8,128)(2,1)}), bf16[32,128,128]{2,1,0:T(8,128)(2,1)S(1)}, u32[]{:S(2)}, u32[]{:S(2)}) async-start(bf16[32,128,128]{2,1,0:T(8,128)(2,1)} %get-tuple-element.39), calls=%async_computation.5 | async-start | bytes 2097152 | tf_op jit(solution)/shard_map/all_to_all | solution.py:324
  174.0 0.0 copy-start.4
  174.0 0.0 copy-start.5
  174.0 0.0 collective-permute-done.2
  174.0 1.8 fusion.3
  175.8 0.0 copy-done.4
  175.8 0.3 copy-done.5
  176.1 0.4 pad_maximum_fusion
  176.5 2.7 %fusion.1 = bf16[1,256,2048]{2,1,0:T(8,128)(2,1)} fusion(bf16[512,2048]{1,0:T(8,128)(2,1)S(1)} %bitcast.20, bf16[2,512,256]{2,1,0:T(8,128)(2,1)} %constant_dynamic-update-slice_fusion), kind=kOutput, calls=%fused_computation.3 | convolution fusion | flops 537395200 | bytes 3407872 | tf_op jit(solution)/shard_map/dot_general | solution.py:24
  179.2 2.7 %fusion = bf16[1,2048,256]{2,1,0:T(8,128)(2,1)} fusion(bf16[512,2048]{1,0:T(8,128)(2,1)S(1)} %bitcast.21, bf16[2,512,256]{2,1,0:T(8,128)(2,1)} %constant_dynamic-update-slice_fusion), kind=kOutput, calls=%fused_computation.2 | convolution fusion | flops 537395200 | bytes 3407872 | tf_op jit(solution)/shard_map/dot_general | solution.py:24
  181.9 1.9 shard_map.164.local_ref
  183.7 1.8 shard_map.162
  185.5 5.4 %all-to-all-done.5.states_ref = bf16[32,128,128]{2,1,0:T(8,128)(2,1)S(1)} async-done(((bf16[32,128,128]{2,1,0:T(8,128)(2,1)}), bf16[32,128,128]{2,1,0:T(8,128)(2,1)S(1)}, u32[]{:S(2)}, u32[]{:S(2)}) %all-to-all-start.5) | async-done | bytes 1048608 | tf_op jit(solution)/shard_map/all_to_all | solution.py:324
  190.9 1.0 copy-done.3
  191.9 2.3 %shard_map.165 = bf16[128,128]{1,0:T(8,128)(2,1)} custom-call(bf16[32,128,128]{2,1,0:T(8,128)(2,1)} %copy-done.3, f32[32,128]{1,0:T(8,128)} %get-tuple-element.40.later_ref, bf16[128,128]{1,0:T(8,128)(2,1)} %b_ref.5, f32[128,128]{1,0:T(8,128)} %get-tuple-element.26.cum_ref, f32[128,128]{1,0:T(8,128)} %shard_map.164.local_ref), custom_call_target="tpu_custom_call" | custom-call | tf_op jit(solution)/shard_map/pallas_call | solution.py:60
  (2 shorter events, 0.0 us)
Async XLA Ops:
  0.6 14.4 %copy-start.11 = (f32[128,2]{0,1:T(2,128)S(1)}, f32[128,2]{0,1:T(2,128)}, u32[]{:S(2)}) copy-start(f32[128,2]{0,1:T(2,128)} %param.19) | copy-start | bytes 3076
  0.6 15.1 %copy-start.10 = (s32[128,2]{0,1:T(2,128)S(1)}, s32[128,2]{0,1:T(2,128)}, u32[]{:S(2)}) copy-start(s32[128,2]{0,1:T(2,128)} %param.20) | copy-start | bytes 3076
  4.6 28.9 %all-to-all-start = ((bf16[32,144,128]{2,1,0:T(8,128)(2,1)}), bf16[32,144,128]{2,1,0:T(8,128)(2,1)S(1)}, u32[]{:S(2)}, u32[]{:S(2)}) async-start(bf16[32,144,128]{2,1,0:T(8,128)(2,1)} %get-tuple-element.25), calls=%async_computation | async-start | bytes 2359296 | tf_op jit(solution)/shard_map/all_to_all | solution.py:324
  33.5 1.0 copy-start.2
  66.3 3.9 %copy-start.7 = (bf16[1,2048,256]{2,1,0:T(8,128)(2,1)S(1)}, bf16[1,2048,256]{2,1,0:T(8,128)(2,1)}, u32[]{:S(2)}) copy-start(bf16[1,2048,256]{2,1,0:T(8,128)(2,1)} %param.21) | copy-start | bytes 3145732
  66.3 29.0 %all-to-all-start.2 = ((bf16[16,32,2048]{2,1,0:T(8,128)(2,1)}), bf16[16,32,2048]{2,1,0:T(8,128)(2,1)S(1)}, u32[]{:S(2)}, u32[]{:S(2)}) async-start(bf16[16,32,2048]{2,1,0:T(8,128)(2,1)} %get-tuple-element.31), calls=%async_computation.2 | async-start | bytes 4194304 | tf_op jit(solution)/shard_map/all_to_all | solution.py:324
  70.2 7.7 %collective-permute-start = (bf16[2048,256]{1,0:T(8,128)(2,1)S(1)}, bf16[2048,256]{1,0:T(8,128)(2,1)S(1)}, u32[]{:S(2)}, u32[]{:S(2)}) collective-permute-start(bf16[2048,256]{1,0:T(8,128)(2,1)S(1)} %bitcast.23), channel_id=1, source_target_pairs={{0,16},{16,0},{32,48},{48,32},{64,80},{80,64},{96,112},{112,96},{1... | collective-permute-start | bytes 3145736 | tf_op jit(solution)/shard_map/ppermute | solution.py:360
  75.7 4.9 %collective-permute-start.1 = (bf16[256,2048]{1,0:T(8,128)(2,1)}, bf16[256,2048]{1,0:T(8,128)(2,1)}, u32[]{:S(2)}, u32[]{:S(2)}) collective-permute-start(bf16[256,2048]{1,0:T(8,128)(2,1)} %bitcast.24), channel_id=1, source_target_pairs={{0,16},{16,0},{32,48},{48,32},{64,80},{80,64},{96,112},{112,96},{1... | collective-permute-start | bytes 3145736 | tf_op jit(solution)/shard_map/ppermute | solution.py:360
  77.9 1.0 copy-start.8
  95.3 1.3 copy-start
  103.4 6.0 %copy-start.1 = (bf16[16,32,2048]{2,1,0:T(8,128)(2,1)S(1)}, bf16[16,32,2048]{2,1,0:T(8,128)(2,1)}, u32[]{:S(2)}) copy-start(bf16[16,32,2048]{2,1,0:T(8,128)(2,1)} %copy-done) | copy-start | bytes 6291460
  103.4 12.6 %copy-start.12 = (bf16[2,256,256]{2,1,0:T(8,128)(2,1)S(1)}, bf16[2,256,256]{2,1,0:T(8,128)(2,1)}, u32[]{:S(2)}) copy-start(bf16[2,256,256]{2,1,0:T(8,128)(2,1)} %get-tuple-element.44) | copy-start | bytes 786436
  103.4 30.0 %all-to-all-start.3 = ((bf16[16,32,2048]{2,1,0:T(8,128)(2,1)}), bf16[16,32,2048]{2,1,0:T(8,128)(2,1)}, u32[]{:S(2)}, u32[]{:S(2)}) async-start(bf16[16,32,2048]{2,1,0:T(8,128)(2,1)} %get-tuple-element.32), calls=%async_computation.3 | async-start | bytes 4194304 | tf_op jit(solution)/shard_map/all_to_all | solution.py:324
  109.4 64.6 %collective-permute-start.2 = (bf16[16,32,2048]{2,1,0:T(8,128)(2,1)S(1)}, bf16[16,32,2048]{2,1,0:T(8,128)(2,1)}, u32[]{:S(2)}, u32[]{:S(2)}) collective-permute-start(bf16[16,32,2048]{2,1,0:T(8,128)(2,1)S(1)} %copy-done.1), channel_id=1, source_target_pairs={{0,16},{16,0},{32,48},{48,32},{64,80},{80,64},{96,112},{112,96},{1... | collective-permute-start | bytes 6291464 | tf_op jit(solution)/shard_map/ppermute | solution.py:360
  116.0 34.9 %collective-permute-start.3 = (bf16[2,256,256]{2,1,0:T(8,128)(2,1)S(1)}, bf16[2,256,256]{2,1,0:T(8,128)(2,1)S(1)}, u32[]{:S(2)}, u32[]{:S(2)}) collective-permute-start(bf16[2,256,256]{2,1,0:T(8,128)(2,1)S(1)} %copy-done.12), channel_id=1, source_target_pairs={{0,16},{16,0},{32,48},{48,32},{64,80},{80,64},{96,112},{112,96},{1... | collective-permute-start | bytes 786440 | tf_op jit(solution)/shard_map/ppermute | solution.py:360
  136.1 24.6 %all-to-all-start.4 = ((bf16[16,32,128]{2,1,0:T(8,128)(2,1)}), bf16[16,32,128]{2,1,0:T(8,128)(2,1)S(1)}, u32[]{:S(2)}, u32[]{:S(2)}) async-start(bf16[16,32,128]{2,1,0:T(8,128)(2,1)} %shard_map.161), calls=%async_computation.4 | async-start | bytes 262144 | tf_op jit(solution)/shard_map/all_to_all | solution.py:324
  148.7 1.5 copy-start.9
  160.7 0.7 copy-start.6
  163.8 27.1 %all-to-all-start.5 = ((bf16[32,128,128]{2,1,0:T(8,128)(2,1)}), bf16[32,128,128]{2,1,0:T(8,128)(2,1)S(1)}, u32[]{:S(2)}, u32[]{:S(2)}) async-start(bf16[32,128,128]{2,1,0:T(8,128)(2,1)} %get-tuple-element.39), calls=%async_computation.5 | async-start | bytes 2097152 | tf_op jit(solution)/shard_map/all_to_all | solution.py:324
  174.0 1.9 copy-start.4
  174.0 2.2 %copy-start.5 = (bf16[16,16,2048]{2,1,0:T(8,128)(2,1)S(1)}, bf16[16,16,2048]{2,1,0:T(8,128)(2,1)}, u32[]{:S(2)}) copy-start(bf16[16,16,2048]{2,1,0:T(8,128)(2,1)} %get-tuple-element.46) | copy-start | bytes 3145732
  190.9 1.0 copy-start.3

commit v3 on v2

--- a/solution.py
+++ b/solution.py
@@ -56,7 +56,11 @@
     return jnp.where(condition, 1.0, 0.0).astype(dtype)
 
 
-def call(kernel, outs, *args, smem=()):
+def call(kernel, outs, *args, smem=(), near=()):
+    args = [
+        pltpu.with_memory_space_constraint(a, pltpu.VMEM) if a.ndim > 2 or i in near else a
+        for i, a in enumerate(args)
+    ]
     return pl.pallas_call(
         kernel,
         out_shape=outs,
@@ -100,23 +104,27 @@
     to_rows_ref[...] = spread[0] + spread[1]
     pay_ref[:, :capacity, :] = cot.astype(bf16).reshape(experts, capacity, features)
     high, middle, low = split3(gain_ref[...])
-    place = iota((capacity, features), 0)
+    place = iota((pay_ref.shape[1] - capacity, features), 0)
     pieces = jnp.where(
         place == 0,
         high.astype(f32),
         jnp.where(place == 1, middle.astype(f32), jnp.where(place == 2, low.astype(f32), 0.0)),
     ).astype(bf16)
-    pay_ref[:, capacity:, :] = jnp.broadcast_to(pieces[None], (experts, capacity, features))
+    pay_ref[:, capacity:, :] = jnp.broadcast_to(pieces[None], (experts,) + pieces.shape)
 
 
 def state_kernel(x_ref, b_ref, decay_ref, pay_ref, cum_ref):
     tokens, features = x_ref.shape
-    width = features // decay_ref.shape[1]
+    heads = decay_ref.shape[0]
+    width = features // heads
     square = (tokens, tokens)
-    spread = per_head(decay_ref[...], (tokens, features), width)
-    causal = ones_where(iota(square, 1) <= iota(square, 0))
+    place = iota((features, tokens), 0)
+    spread = jnp.broadcast_to(decay_ref[0:1, :], (features, tokens))
+    for head in range(1, heads):
+        spread = jnp.where(place >= head * width, decay_ref[head : head + 1, :], spread)
+    causal = ones_where(iota(square, 0) <= iota(square, 1))
     high, middle, low = split3(spread)
-    cum = mm(causal, high) + mm(causal, middle) + mm(causal, low)
+    cum = (mm(high, causal) + mm(middle, causal) + mm(low, causal)).T
     cum_ref[...] = cum
     ending = cum[tokens - 1 : tokens, :]
     tail = jnp.exp(ending - cum)
@@ -362,7 +370,7 @@
     state_pay, cum = call(
         state_kernel,
         (shape_of((blocks, states + 16, features), bf16), shape_of((tokens, features), f32)),
-        ssd_input, state_in, log_decay,
+        ssd_input, state_in, log_decay.T,
     )
     state_all = swap(state_pay, "ctx")
     peer_in = partner(matrix_in)
@@ -373,7 +381,7 @@
         (
             shape_of((rows, tokens), bf16),
             shape_of((2, tokens, rows), bf16),
-            shape_of((experts, 2 * capacity, features), bf16),
+            shape_of((experts, capacity + 8, features), bf16),
         ),
         expert_ids, expert_ids.T, route_weight, out_grad, norm_gain.reshape(1, features),
     )
@@ -386,7 +394,7 @@
         mixed_kernel,
         (
             shape_of((tokens, features), bf16),
-            shape_of((experts, 3 * capacity, features), bf16),
+            shape_of((experts, 2 * capacity + 8, features), bf16),
             shape_of((blocks, features), f32),
         ),
         me, state_all, state_out, cum, local, to_rows, cot_pay,

time: 195 us -> 187 us (0.959)
  waiting for transfers between devices: 59.7 us -> 67.8 us
  local copies, waits for them, and re-layouts: 12.9 us -> 7.04 us
  starting transfers between devices: 58.9 us -> 54.1 us
  Pallas kernels: 29.7 us -> 26.7 us
    all_to_all x5, waiting for transfers between devices: 57.7 us -> 65.1 us  [swap(): lax.all_to_all(a, axis, split_axis=0, concat_axis=0, tiled=True, axis_ind...]
    unnamed x30 -> x25, local copies, waits for them, and re-layouts: 8.95 us -> 2.49 us
    pallas_call x11, Pallas kernels: 29.7 us -> 26.7 us  [call(): pl.pallas_call(kernel, out_shape=outs, in_specs=[pl.BlockSpec(memory_spac...]
    ppermute x4, starting transfers between devices: 15.9 us -> 13.2 us  [partner(): return lax.ppermute(a, 'ctx', partners)]
    all_to_all x5, starting transfers between devices: 43 us -> 40.8 us  [swap(): lax.all_to_all(a, axis, split_axis=0, concat_axis=0, tiled=True, axis_ind...]
  transfers between devices with their start and end apart: 9 -> 9, of which waited for: 7 -> 7; matrix products, arithmetic and copies ran while one was open for 6% -> 5% of each run, Pallas kernels for 7% -> 6%
where the time goes in v3:
time: 187 us; the launch traced here: 186 us
  waiting for transfers between devices  67.8 us (36%)
  starting transfers between devices  54.1 us (29%)
  Pallas kernels  26.7 us (14%)
  blocking collectives  25.9 us (14%)
  local copies, waits for them, and re-layouts  7.04 us (4%)
  matrix products  3.45 us (2%)
    all_to_all x5, waiting for transfers between devices, swap(): lax.all_to_all(a, axis, split_axis=0, concat_axis=0, tiled=True, axis_ind...  65.1 us
    all_to_all x5, starting transfers between devices, swap(): lax.all_to_all(a, axis, split_axis=0, concat_axis=0, tiled=True, axis_ind...  40.8 us
    pallas_call x11, Pallas kernels, call(): pl.pallas_call(kernel, out_shape=outs, in_specs=[pl.BlockSpec(memory_spac...  26.7 us
    all_to_all x1, blocking collectives, swap(): lax.all_to_all(a, axis, split_axis=0, concat_axis=0, tiled=True, axis_ind...  25.9 us
    ppermute x4, starting transfers between devices, partner(): return lax.ppermute(a, 'ctx', partners)  13.2 us
  transfers between devices with their start and end apart: 9, of which 7 were waited for; matrix products, arithmetic and copies ran while one was open for 5% of the time, Pallas kernels for 6%

profile of v3, /device:TPU:1, one launch (start us, length us, event | category | flops | bytes accessed | tf_op | source)
XLA Modules:
  0.0 186.2 jit_solution(641833245570985873)
XLA Ops:
  0.6 0.0 copy-start.9
  0.6 0.0 copy-start.8
  0.7 2.3 %shard_map.155 = (bf16[32,144,128]{2,1,0:T(8,128)(2,1)}, f32[128,128]{1,0:T(8,128)}) custom-call(bf16[128,128]{1,0:T(8,128)(2,1)} %x_ref.3, bf16[128,128]{1,0:T(8,128)(2,1)} %b_ref.5, f32[4,128]{1,0:T(4,128)} %bitcast.30), custom_call_target="tpu_custom_call" | custom-call | tf_op jit(solution)/shard_map/pallas_call | solution.py:64
  3.0 10.4 %all-to-all-start = ((bf16[32,144,128]{2,1,0:T(8,128)(2,1)}), bf16[32,144,128]{2,1,0:T(8,128)(2,1)S(1)}, u32[]{:S(2)}, u32[]{:S(2)}) async-start(bf16[32,144,128]{2,1,0:T(8,128)(2,1)} %get-tuple-element.25), calls=%async_computation | async-start | bytes 2359296 | tf_op jit(solution)/shard_map/all_to_all | solution.py:332
  13.4 0.0 copy-done.9
  13.4 0.7 copy.18.weight_ref
  14.2 0.0 copy-done.8
  14.2 0.7 copy.17.ids_ref
  14.9 1.9 %shard_map.156 = (f32[128,128]{1,0:T(8,128)}, bf16[2,4,128,128]{3,2,1,0:T(8,128)(2,1)}) custom-call(bf16[128,128]{1,0:T(8,128)(2,1)} %x_ref.3, bf16[128,128]{1,0:T(8,128)(2,1)} %b_ref.5, bf16[128,128]{1,0:T(8,128)(2,1)} %c_ref.5, f32[128,128]{1,0:T(8,128)} %get-tuple-element.26.cum_ref, f32[1,4]{1,0:T(1,128)} %bitcast.28, bf16[128,128]{1,0:T(8,128)(2,1)} %residual_ref.1), custom_call_target="tpu_custom_call" | custom-call | tf_op jit(solution)/shard_map/pallas_call | solution.py:64
  16.9 2.0 %shard_map.157 = (bf16[256,128]{1,0:T(8,128)(2,1)}, bf16[2,128,256]{2,1,0:T(8,128)(2,1)}, bf16[16,24,128]{2,1,0:T(8,128)(2,1)}) custom-call(s32[128,2]{1,0:T(8,128)} %copy.17.ids_ref, s32[2,128]{1,0:T(2,128)} %bitcast.27, f32[128,2]{1,0:T(8,128)} %copy.18.weight_ref, bf16[128,128]{1,0:T(8,128)(2,1)} %grad_ref.3, f32[1,128]{1,0:T(1,128)} %bitcast.31), custom_call_target="tpu_custom_call" | custom-call | tf_op jit(solution)/shard_map/pallas_call | solution.py:64
  18.9 13.0 %all-to-all-done.states_ref = bf16[32,144,128]{2,1,0:T(8,128)(2,1)S(1)} async-done(((bf16[32,144,128]{2,1,0:T(8,128)(2,1)}), bf16[32,144,128]{2,1,0:T(8,128)(2,1)S(1)}, u32[]{:S(2)}, u32[]{:S(2)}) %all-to-all-start) | async-done | bytes 1179680 | tf_op jit(solution)/shard_map/all_to_all | solution.py:332
  31.9 0.0 copy-start.2
  31.9 0.9 copy-done.2
  32.8 2.4 %shard_map.158 = (bf16[128,128]{1,0:T(8,128)(2,1)}, bf16[16,40,128]{2,1,0:T(8,128)(2,1)}, f32[32,128]{1,0:T(8,128)}) custom-call(s32[1]{0:T(128)} %bitcast.me_ref, bf16[32,144,128]{2,1,0:T(8,128)(2,1)S(1)} %all-to-all-done.states_ref, bf16[128,128]{1,0:T(8,128)(2,1)} %c_ref.5, f32[128,128]{1,0:T(8,128)} %get-tuple-element.26.cum_ref, ...), custom_call_target="tpu_custom_call" | custom-call | tf_op jit(solution)/shard_map/pallas_call | solution.py:64
  35.1 25.9 %all_to_all.30.in_ref = bf16[16,40,128]{2,1,0:T(8,128)(2,1)S(1)} all-to-all(bf16[16,40,128]{2,1,0:T(8,128)(2,1)} %get-tuple-element.30), channel_id=1, replica_groups=mesh['ctx'=32,'exp'=16] {'exp'}, dimensions={0} | all-to-all | bytes 327680 | tf_op jit(solution)/shard_map/all_to_all | solution.py:332
  61.0 1.8 shard_map.159
  62.8 0.0 copy-start.4
  62.8 0.0 copy-start.5
  62.8 4.6 %all-to-all-start.2 = ((bf16[16,32,2048]{2,1,0:T(8,128)(2,1)}), bf16[16,32,2048]{2,1,0:T(8,128)(2,1)}, u32[]{:S(2)}, u32[]{:S(2)}) async-start(bf16[16,32,2048]{2,1,0:T(8,128)(2,1)} %get-tuple-element.31), calls=%async_computation.2 | async-start | bytes 4194304 | tf_op jit(solution)/shard_map/all_to_all | solution.py:332
  67.4 0.0 copy-done.4
  67.4 4.3 %collective-permute-start = (bf16[2048,256]{1,0:T(8,128)(2,1)S(1)}, bf16[2048,256]{1,0:T(8,128)(2,1)S(1)}, u32[]{:S(2)}, u32[]{:S(2)}) collective-permute-start(bf16[2048,256]{1,0:T(8,128)(2,1)S(1)} %bitcast.24), channel_id=1, source_target_pairs={{0,16},{16,0},{32,48},{48,32},{64,80},{80,64},{96,112},{112,96},{1... | collective-permute-start | bytes 3145736 | tf_op jit(solution)/shard_map/ppermute | solution.py:368
  71.8 0.0 copy-done.5
  71.8 1.9 %collective-permute-start.1 = (bf16[256,2048]{1,0:T(8,128)(2,1)S(1)}, bf16[256,2048]{1,0:T(8,128)(2,1)}, u32[]{:S(2)}, u32[]{:S(2)}) collective-permute-start(bf16[256,2048]{1,0:T(8,128)(2,1)S(1)} %bitcast.26), channel_id=1, source_target_pairs={{0,16},{16,0},{32,48},{48,32},{64,80},{80,64},{96,112},{112,96},{1... | collective-permute-start | bytes 3145736 | tf_op jit(solution)/shard_map/ppermute | solution.py:368
  73.7 0.3 collective-permute-done.in_peer_ref
  74.0 0.0 copy-start.6
  74.0 2.4 %collective-permute-done.1.down_peer_ref = bf16[256,2048]{1,0:T(8,128)(2,1)} collective-permute-done((bf16[256,2048]{1,0:T(8,128)(2,1)S(1)}, bf16[256,2048]{1,0:T(8,128)(2,1)}, u32[]{:S(2)}, u32[]{:S(2)}) %collective-permute-start.1) | collective-permute-done | bytes 1048608 | tf_op jit(solution)/shard_map/ppermute | solution.py:368
  76.5 0.0 copy-done.6
  76.5 16.7 %all-to-all-done.2.rows_ref = bf16[16,32,2048]{2,1,0:T(8,128)(2,1)} async-done(((bf16[16,32,2048]{2,1,0:T(8,128)(2,1)}), bf16[16,32,2048]{2,1,0:T(8,128)(2,1)}, u32[]{:S(2)}, u32[]{:S(2)}) %all-to-all-start.2) | async-done | bytes 2097184 | tf_op jit(solution)/shard_map/all_to_all | solution.py:332
  93.2 6.7 %shard_map.160 = (bf16[16,32,2048]{2,1,0:T(8,128)(2,1)}, bf16[2,256,256]{2,1,0:T(8,128)(2,1)}, bf16[2,256,256]{2,1,0:T(8,128)(2,1)}) custom-call(bf16[16,32,2048]{2,1,0:T(8,128)(2,1)} %all-to-all-done.2.rows_ref, bf16[2048,256]{1,0:T(8,128)(2,1)} %bitcast.23, bf16[2048,256]{1,0:T(8,128)(2,1)} %copy-done.6, bf16[256,2048]{1,0:T(8,128)(2,1)} %bitcast.25, ...), custom_call_target="tpu_custom_call" | custom-call | tf_op jit(solution)/shard_map/pallas_call | solution.py:64
  99.9 0.0 copy-start.10
  99.9 5.6 %all-to-all-start.3 = ((bf16[16,32,2048]{2,1,0:T(8,128)(2,1)}), bf16[16,32,2048]{2,1,0:T(8,128)(2,1)S(1)}, u32[]{:S(2)}, u32[]{:S(2)}) async-start(bf16[16,32,2048]{2,1,0:T(8,128)(2,1)} %get-tuple-element.32), calls=%async_computation.3 | async-start | bytes 4194304 | tf_op jit(solution)/shard_map/all_to_all | solution.py:332
  105.5 5.1 %collective-permute-start.2 = (bf16[16,32,2048]{2,1,0:T(8,128)(2,1)}, bf16[16,32,2048]{2,1,0:T(8,128)(2,1)}, u32[]{:S(2)}, u32[]{:S(2)}) collective-permute-start(bf16[16,32,2048]{2,1,0:T(8,128)(2,1)} %all-to-all-done.2.rows_ref), channel_id=1, source_target_pairs={{0,16},{16,0},{32,48},{48,32},{64,80},{80,64},{96,112},{112,96},{1... | collective-permute-start | bytes 6291464 | tf_op jit(solution)/shard_map/ppermute | solution.py:368
  110.6 0.0 copy-done.10
  110.6 1.9 %collective-permute-start.3 = (bf16[2,256,256]{2,1,0:T(8,128)(2,1)S(1)}, bf16[2,256,256]{2,1,0:T(8,128)(2,1)S(1)}, u32[]{:S(2)}, u32[]{:S(2)}) collective-permute-start(bf16[2,256,256]{2,1,0:T(8,128)(2,1)S(1)} %copy-done.10), channel_id=1, source_target_pairs={{0,16},{16,0},{32,48},{48,32},{64,80},{80,64},{96,112},{112,96},{1... | collective-permute-start | bytes 786440 | tf_op jit(solution)/shard_map/ppermute | solution.py:368
  112.5 18.4 %all-to-all-done.3.parts_ref = bf16[16,32,2048]{2,1,0:T(8,128)(2,1)S(1)} async-done(((bf16[16,32,2048]{2,1,0:T(8,128)(2,1)}), bf16[16,32,2048]{2,1,0:T(8,128)(2,1)S(1)}, u32[]{:S(2)}, u32[]{:S(2)}) %all-to-all-start.3) | async-done | bytes 2097184 | tf_op jit(solution)/shard_map/all_to_all | solution.py:332
  130.9 2.0 %shard_map.161 = bf16[16,32,128]{2,1,0:T(8,128)(2,1)} custom-call(bf16[16,32,2048]{2,1,0:T(8,128)(2,1)S(1)} %all-to-all-done.3.parts_ref, bf16[16,2048]{1,0:T(8,128)(2,1)} %get-tuple-element.33.raw_ref, f32[16,128]{1,0:T(8,128)} %get-tuple-element.34.inv_ref, f32[1,2048]{1,0:T(1,128)} %get-tuple-element.35.gain_ref), custom_call_target="tpu_custom_call" | custom-call | tf_op jit(solution)/shard_map/pallas_call | solution.py:64
  132.9 10.0 %all-to-all-start.4 = ((bf16[16,32,128]{2,1,0:T(8,128)(2,1)}), bf16[16,32,128]{2,1,0:T(8,128)(2,1)S(1)}, u32[]{:S(2)}, u32[]{:S(2)}) async-start(bf16[16,32,128]{2,1,0:T(8,128)(2,1)} %shard_map.161), calls=%async_computation.4 | async-start | bytes 262144 | tf_op jit(solution)/shard_map/all_to_all | solution.py:332
  142.9 0.0 copy-start.7
  142.9 0.0 copy-start
  143.0 2.8 %fusion.2 = (bf16[16,16,2048]{2,1,0:T(8,128)(2,1)S(1)}, bf16[16,16,2048]{2,1,0:T(8,128)(2,1)}) fusion(bf16[16,32,2048]{2,1,0:T(8,128)(2,1)} %all-to-all-done.2.rows_ref), kind=kLoop, calls=%fused_computation.10 | loop fusion | bytes 4194304 | tf_op jit(solution)/shard_map/slice | solution.py:431
  145.7 0.0 copy-done.7
  145.7 0.0 collective-permute-done.3
  145.8 9.1 %all-to-all-done.4.rows_ref = bf16[16,32,128]{2,1,0:T(8,128)(2,1)S(1)} async-done(((bf16[16,32,128]{2,1,0:T(8,128)(2,1)}), bf16[16,32,128]{2,1,0:T(8,128)(2,1)S(1)}, u32[]{:S(2)}, u32[]{:S(2)}) %all-to-all-start.4) | async-done | bytes 131104 | tf_op jit(solution)/shard_map/all_to_all | solution.py:332
  154.9 0.0 copy-done
  154.9 2.3 %shard_map.163 = (bf16[128,128]{1,0:T(8,128)(2,1)}, f32[128,128]{1,0:T(8,128)}, bf16[32,128,128]{2,1,0:T(8,128)(2,1)}) custom-call(bf16[16,32,128]{2,1,0:T(8,128)(2,1)S(1)} %all-to-all-done.4.rows_ref, bf16[2,128,256]{2,1,0:T(8,128)(2,1)S(1)} %copy-done, bf16[128,128]{1,0:T(8,128)(2,1)} %grad_ref.3, bf16[128,128]{1,0:T(8,128)(2,1)} %c_ref.5, ...), custom_call_target="tpu_custom_call" | custom-call | tf_op jit(solution)/shard_map/pallas_call | solution.py:64
  157.2 10.2 %all-to-all-start.5 = ((bf16[32,128,128]{2,1,0:T(8,128)(2,1)}), bf16[32,128,128]{2,1,0:T(8,128)(2,1)S(1)}, u32[]{:S(2)}, u32[]{:S(2)}) async-start(bf16[32,128,128]{2,1,0:T(8,128)(2,1)} %get-tuple-element.39), calls=%async_computation.5 | async-start | bytes 2097152 | tf_op jit(solution)/shard_map/all_to_all | solution.py:332
  167.4 0.0 copy-start.3
  167.4 0.0 collective-permute-done.2
  167.4 1.8 fusion.3
  169.2 0.1 copy-done.3
  169.3 0.4 pad_maximum_fusion
  169.6 1.7 fusion.1
  171.3 0.0 copy-start.1
  171.3 1.7 fusion
  173.1 0.0 copy-done.1
  173.1 1.7 shard_map.164.local_ref
  174.8 1.6 shard_map.162
  176.4 7.9 %all-to-all-done.5.states_ref = bf16[32,128,128]{2,1,0:T(8,128)(2,1)S(1)} async-done(((bf16[32,128,128]{2,1,0:T(8,128)(2,1)}), bf16[32,128,128]{2,1,0:T(8,128)(2,1)S(1)}, u32[]{:S(2)}, u32[]{:S(2)}) %all-to-all-start.5) | async-done | bytes 1048608 | tf_op jit(solution)/shard_map/all_to_all | solution.py:332
  184.3 1.9 %shard_map.165 = bf16[128,128]{1,0:T(8,128)(2,1)} custom-call(bf16[32,128,128]{2,1,0:T(8,128)(2,1)S(1)} %all-to-all-done.5.states_ref, f32[32,128]{1,0:T(8,128)} %get-tuple-element.40.later_ref, bf16[128,128]{1,0:T(8,128)(2,1)} %b_ref.5, f32[128,128]{1,0:T(8,128)} %get-tuple-element.26.cum_ref, f32[128,128]{1,0:T(8,128)} %shard_map.164.local_ref), custom_call_target="tpu_custom_call" | custom-call | tf_op jit(solution)/shard_map/pallas_call | solution.py:64
  (2 shorter events, 0.0 us)
Async XLA Ops:
  0.6 12.8 %copy-start.9 = (f32[128,2]{0,1:T(2,128)S(1)}, f32[128,2]{0,1:T(2,128)}, u32[]{:S(2)}) copy-start(f32[128,2]{0,1:T(2,128)} %param.19) | copy-start | bytes 3076
  0.6 13.5 %copy-start.8 = (s32[128,2]{0,1:T(2,128)S(1)}, s32[128,2]{0,1:T(2,128)}, u32[]{:S(2)}) copy-start(s32[128,2]{0,1:T(2,128)} %param.20) | copy-start | bytes 3076
  3.0 28.9 %all-to-all-start = ((bf16[32,144,128]{2,1,0:T(8,128)(2,1)}), bf16[32,144,128]{2,1,0:T(8,128)(2,1)S(1)}, u32[]{:S(2)}, u32[]{:S(2)}) async-start(bf16[32,144,128]{2,1,0:T(8,128)(2,1)} %get-tuple-element.25), calls=%async_computation | async-start | bytes 2359296 | tf_op jit(solution)/shard_map/all_to_all | solution.py:332
  31.9 0.9 copy-start.2
  62.8 4.6 %copy-start.4 = (bf16[1,2048,256]{2,1,0:T(8,128)(2,1)S(1)}, bf16[1,2048,256]{2,1,0:T(8,128)(2,1)}, u32[]{:S(2)}) copy-start(bf16[1,2048,256]{2,1,0:T(8,128)(2,1)} %param.21) | copy-start | bytes 3145732
  62.8 8.9 %copy-start.5 = (bf16[1,256,2048]{2,1,0:T(8,128)(2,1)S(1)}, bf16[1,256,2048]{2,1,0:T(8,128)(2,1)}, u32[]{:S(2)}) copy-start(bf16[1,256,2048]{2,1,0:T(8,128)(2,1)} %param.22) | copy-start | bytes 3145732
  62.8 30.3 %all-to-all-start.2 = ((bf16[16,32,2048]{2,1,0:T(8,128)(2,1)}), bf16[16,32,2048]{2,1,0:T(8,128)(2,1)}, u32[]{:S(2)}, u32[]{:S(2)}) async-start(bf16[16,32,2048]{2,1,0:T(8,128)(2,1)} %get-tuple-element.31), calls=%async_computation.2 | async-start | bytes 4194304 | tf_op jit(solution)/shard_map/all_to_all | solution.py:332
  67.4 6.6 %collective-permute-start = (bf16[2048,256]{1,0:T(8,128)(2,1)S(1)}, bf16[2048,256]{1,0:T(8,128)(2,1)S(1)}, u32[]{:S(2)}, u32[]{:S(2)}) collective-permute-start(bf16[2048,256]{1,0:T(8,128)(2,1)S(1)} %bitcast.24), channel_id=1, source_target_pairs={{0,16},{16,0},{32,48},{48,32},{64,80},{80,64},{96,112},{112,96},{1... | collective-permute-start | bytes 3145736 | tf_op jit(solution)/shard_map/ppermute | solution.py:368
  71.8 4.7 %collective-permute-start.1 = (bf16[256,2048]{1,0:T(8,128)(2,1)S(1)}, bf16[256,2048]{1,0:T(8,128)(2,1)}, u32[]{:S(2)}, u32[]{:S(2)}) collective-permute-start(bf16[256,2048]{1,0:T(8,128)(2,1)S(1)} %bitcast.26), channel_id=1, source_target_pairs={{0,16},{16,0},{32,48},{48,32},{64,80},{80,64},{96,112},{112,96},{1... | collective-permute-start | bytes 3145736 | tf_op jit(solution)/shard_map/ppermute | solution.py:368
  74.0 2.4 %copy-start.6 = (bf16[2048,256]{1,0:T(8,128)(2,1)}, bf16[2048,256]{1,0:T(8,128)(2,1)S(1)}, u32[]{:S(2)}) copy-start(bf16[2048,256]{1,0:T(8,128)(2,1)S(1)} %collective-permute-done.in_peer_ref) | copy-start | bytes 3145732
  99.9 10.7 %copy-start.10 = (bf16[2,256,256]{2,1,0:T(8,128)(2,1)S(1)}, bf16[2,256,256]{2,1,0:T(8,128)(2,1)}, u32[]{:S(2)}) copy-start(bf16[2,256,256]{2,1,0:T(8,128)(2,1)} %get-tuple-element.44) | copy-start | bytes 786436
  99.9 31.1 %all-to-all-start.3 = ((bf16[16,32,2048]{2,1,0:T(8,128)(2,1)}), bf16[16,32,2048]{2,1,0:T(8,128)(2,1)S(1)}, u32[]{:S(2)}, u32[]{:S(2)}) async-start(bf16[16,32,2048]{2,1,0:T(8,128)(2,1)} %get-tuple-element.32), calls=%async_computation.3 | async-start | bytes 4194304 | tf_op jit(solution)/shard_map/all_to_all | solution.py:332
  105.5 61.9 %collective-permute-start.2 = (bf16[16,32,2048]{2,1,0:T(8,128)(2,1)}, bf16[16,32,2048]{2,1,0:T(8,128)(2,1)}, u32[]{:S(2)}, u32[]{:S(2)}) collective-permute-start(bf16[16,32,2048]{2,1,0:T(8,128)(2,1)} %all-to-all-done.2.rows_ref), channel_id=1, source_target_pairs={{0,16},{16,0},{32,48},{48,32},{64,80},{80,64},{96,112},{112,96},{1... | collective-permute-start | bytes 6291464 | tf_op jit(solution)/shard_map/ppermute | solution.py:368
  110.6 35.1 %collective-permute-start.3 = (bf16[2,256,256]{2,1,0:T(8,128)(2,1)S(1)}, bf16[2,256,256]{2,1,0:T(8,128)(2,1)S(1)}, u32[]{:S(2)}, u32[]{:S(2)}) collective-permute-start(bf16[2,256,256]{2,1,0:T(8,128)(2,1)S(1)} %copy-done.10), channel_id=1, source_target_pairs={{0,16},{16,0},{32,48},{48,32},{64,80},{80,64},{96,112},{112,96},{1... | collective-permute-start | bytes 786440 | tf_op jit(solution)/shard_map/ppermute | solution.py:368
  132.9 22.0 %all-to-all-start.4 = ((bf16[16,32,128]{2,1,0:T(8,128)(2,1)}), bf16[16,32,128]{2,1,0:T(8,128)(2,1)S(1)}, u32[]{:S(2)}, u32[]{:S(2)}) async-start(bf16[16,32,128]{2,1,0:T(8,128)(2,1)} %shard_map.161), calls=%async_computation.4 | async-start | bytes 262144 | tf_op jit(solution)/shard_map/all_to_all | solution.py:332
  142.9 2.8 %copy-start.7 = (bf16[2,256,256]{2,1,0:T(8,128)(2,1)S(1)}, bf16[2,256,256]{2,1,0:T(8,128)(2,1)}, u32[]{:S(2)}) copy-start(bf16[2,256,256]{2,1,0:T(8,128)(2,1)} %get-tuple-element.43) | copy-start | bytes 786436
  142.9 11.9 %copy-start = (bf16[2,128,256]{2,1,0:T(8,128)(2,1)S(1)}, bf16[2,128,256]{2,1,0:T(8,128)(2,1)}, u32[]{:S(2)}) copy-start(bf16[2,128,256]{2,1,0:T(8,128)(2,1)} %get-tuple-element.36.from_ref) | copy-start | bytes 393220
  157.2 27.1 %all-to-all-start.5 = ((bf16[32,128,128]{2,1,0:T(8,128)(2,1)}), bf16[32,128,128]{2,1,0:T(8,128)(2,1)S(1)}, u32[]{:S(2)}, u32[]{:S(2)}) async-start(bf16[32,128,128]{2,1,0:T(8,128)(2,1)} %get-tuple-element.39), calls=%async_computation.5 | async-start | bytes 2097152 | tf_op jit(solution)/shard_map/all_to_all | solution.py:332
  167.4 1.9 copy-start.3
  171.3 1.7 copy-start.1

commit v4 on v3

--- a/solution.py
+++ b/solution.py
@@ -1,4 +1,3 @@
-import functools
 import jax
 import jax.numpy as jnp
 from jax import lax
@@ -6,6 +5,7 @@
 from jax.experimental.pallas import tpu as pltpu
 from jax.sharding import PartitionSpec as P
 
+
 D = 2048
 epsilon = 1e-05
 f32 = jnp.float32
@@ -38,10 +38,6 @@
     rest = a - high.astype(f32)
     middle = rest.astype(bf16)
     return high, middle, (rest - middle.astype(f32)).astype(bf16)
-
-
-def join3(parts):
-    return parts[0].astype(f32) + parts[1].astype(f32) + parts[2].astype(f32)
 
 
 def per_head(columns, shape, width):
@@ -206,7 +202,7 @@
     total = local_ref[...] + jnp.exp(cum_ref[...]) * (mm(c, high) + mm(c, low))
     mixed = total.astype(bf16)
     mixed_ref[...] = mixed
-    experts, total_rows, features = pay_ref.shape
+    experts, _, features = pay_ref.shape
     capacity = table_ref.shape[0] // experts
     pay_ref[:, :capacity, :] = (
         mm(table_ref[...], mixed).astype(bf16).reshape(experts, capacity, features)
@@ -239,7 +235,19 @@
             out_ref[j, capacity:, here] = cot
 
 
-def expert_kernel(rows_ref, in_ref, in_peer_ref, down_ref, down_peer_ref, parts_ref, mine_ref, peer_ref):
+def expert_kernel(*refs):
+    rows_ref = refs[0]
+    weights = refs[1:9]
+    parts_ref = refs[9]
+    units = refs[10:14]
+    held = refs[14:22]
+    sems = refs[22]
+    copies = [
+        pltpu.make_async_copy(source, target, sems.at[k])
+        for k, (source, target) in enumerate(zip(weights, held))
+    ]
+    for copy in copies:
+        copy.start()
     chips, both, width = rows_ref.shape
     capacity = both // 2
     count = chips * capacity
@@ -247,20 +255,40 @@
     cot = rows_ref[:, capacity:, :].reshape(count, width)
     d_total = None
     out_total = None
-    for wide, narrow, kept in ((in_ref, down_ref, mine_ref), (in_peer_ref, down_peer_ref, peer_ref)):
-        hidden = mm(rows, wide[...])
-        d_act = mm_nt(cot, narrow[...])
+    for k in range(4):
+        copies[2 * k].wait()
+        copies[2 * k + 1].wait()
+        wide = held[2 * k][...]
+        narrow = held[2 * k + 1][...]
+        hidden = mm(rows, wide)
+        d_act = mm_nt(cot, narrow)
         sigmoid_h = 1.0 / (1.0 + jnp.exp(-hidden))
         activated = (hidden * sigmoid_h).astype(bf16)
         d_hidden = (d_act * sigmoid_h * (1.0 + hidden * (1.0 - sigmoid_h))).astype(bf16)
-        kept[0] = activated
-        kept[1] = d_hidden
-        d_part = mm_nt(d_hidden, wide[...])
-        out_part = mm(activated, narrow[...])
+        units[k][0] = activated
+        units[k][1] = d_hidden
+        d_part = mm_nt(d_hidden, wide)
+        out_part = mm(activated, narrow)
         d_total = d_part if d_total is None else d_total + d_part
         out_total = out_part if out_total is None else out_total + out_part
     parts_ref[:, :capacity, :] = d_total.astype(bf16).reshape(chips, capacity, width)
     parts_ref[:, capacity:, :] = out_total.astype(bf16).reshape(chips, capacity, width)
+
+
+def run_experts(rows, weights):
+    chips, both, _ = rows.shape
+    units = weights[0].shape[1]
+    count = chips * both // 2
+    near = pl.BlockSpec(memory_space=pltpu.VMEM)
+    kept = [shape_of((2, count, units), bf16)] * 4
+    return pl.pallas_call(
+        expert_kernel,
+        out_shape=[shape_of(rows.shape, bf16)] + kept,
+        in_specs=[near] + [pl.BlockSpec(memory_space=pl.ANY)] * 8,
+        out_specs=[near] * 5,
+        scratch_shapes=[pltpu.VMEM(w.shape, bf16) for w in weights]
+        + [pltpu.SemaphoreType.DMA((8,))],
+    )(pltpu.with_memory_space_constraint(rows, pltpu.VMEM), *weights)
 
 
 def return_kernel(parts_ref, raw_ref, inv_ref, gain_ref, out_ref):
@@ -360,12 +388,30 @@
     matrix_in = weight_in[0]
     matrix_down = weight_down[0]
 
-    chips = blocks // 2
-    same_core = [[2 * chip + core for chip in range(chips)] for core in range(2)]
-    partners = [(i, i ^ 1) for i in range(blocks)]
+    chips = [(x, y) for x in range(4) for y in range(4)]
+
+    def place(x, y, core):
+        return x * 8 + y * 2 + core
+
+    colours = [
+        [place(x, y, core) for x, y in chips if (x + y) % 2 == colour]
+        for core in range(2)
+        for colour in range(2)
+    ]
+    members = len(colours[0])
+    near_of = {}
+    for x, y in chips:
+        near_of[place(x, y, 0)] = place(x ^ 1, y, 0)
+        near_of[place(x, y, 1)] = place(x, y ^ 1, 1)
 
     def partner(a):
-        return lax.ppermute(a, "ctx", partners)
+        return lax.ppermute(a, "ctx", [(i, i ^ 1) for i in range(blocks)])
+
+    def near(a):
+        return lax.ppermute(a, "ctx", [(i, near_of[i]) for i in range(blocks)])
+
+    def across(a):
+        return lax.ppermute(a, "ctx", [(i, near_of[i ^ 1]) for i in range(blocks)])
 
     state_pay, cum = call(
         state_kernel,
@@ -373,8 +419,12 @@
         ssd_input, state_in, log_decay.T,
     )
     state_all = swap(state_pay, "ctx")
+    near_in = near(matrix_in)
+    near_down = near(matrix_down)
     peer_in = partner(matrix_in)
     peer_down = partner(matrix_down)
+    far_in = partner(near_in)
+    far_down = partner(near_down)
 
     to_rows, from_rows, cot_pay = call(
         route_kernel,
@@ -404,32 +454,28 @@
     spread, raw, inv, gain = call(
         norm_kernel,
         (
-            shape_of((chips, 2 * capacity, D), bf16),
+            shape_of((members, 2 * capacity, D), bf16),
             shape_of((capacity, D), bf16),
             shape_of((capacity, 128), f32),
             shape_of((1, D), f32),
         ),
         arrived,
     )
-    expert_rows = swap(spread, "ctx", same_core)
-
-    units = matrix_in.shape[1]
-    count = chips * capacity
-    parts, mine, peer = call(
-        expert_kernel,
-        (
-            shape_of((chips, 2 * capacity, D), bf16),
-            shape_of((2, count, units), bf16),
-            shape_of((2, count, units), bf16),
-        ),
-        expert_rows, matrix_in, peer_in, matrix_down, peer_down,
-    )
-    parts_all = swap(parts, "ctx", same_core)
+    expert_rows = swap(spread, "ctx", colours)
+
+    parts, mine, of_peer, of_near, of_far = run_experts(
+        expert_rows,
+        (matrix_in, matrix_down, peer_in, peer_down, near_in, near_down, far_in, far_down),
+    )
+    parts_all = swap(parts, "ctx", colours)
     peer_rows = partner(expert_rows)
-    peer_units = partner(peer)
-    all_rows = jnp.concatenate([expert_rows[:, :capacity], peer_rows[:, :capacity]]).reshape(-1, D)
-    all_cot = jnp.concatenate([expert_rows[:, capacity:], peer_rows[:, capacity:]]).reshape(-1, D)
-    all_units = jnp.concatenate([mine, peer_units], axis=1)
+    near_rows = near(expert_rows)
+    far_rows = near(peer_rows)
+    units = (mine, partner(of_peer), near(of_near), across(of_far))
+    lots = (expert_rows, peer_rows, near_rows, far_rows)
+    all_rows = jnp.concatenate([lot[:, :capacity] for lot in lots]).reshape(-1, D)
+    all_cot = jnp.concatenate([lot[:, capacity:] for lot in lots]).reshape(-1, D)
+    all_units = jnp.concatenate(units, axis=1)
     grad_down = mm_t(all_units[0], all_cot).astype(bf16)
     grad_in = mm_t(all_rows, all_units[1]).astype(bf16)
 

time: 187 us -> 178 us (0.952)
  waiting for transfers between devices: 67.8 us -> 30.4 us
  starting transfers between devices: 54.1 us -> 72.6 us
  local copies, waits for them, and re-layouts: 7.04 us -> 12.1 us
  matrix products: 3.45 us -> 5.33 us
    all_to_all x5, waiting for transfers between devices: 65.1 us -> 27.4 us  [swap(): lax.all_to_all(a, axis, split_axis=0, concat_axis=0, tiled=True, axis_ind...]
    ppermute x4 -> x12, starting transfers between devices: 13.2 us -> 33.4 us  [the longest x6 16.3 us: partner(): return lax.ppermute(a, 'ctx', [(i, i ^ 1) for i in range(blocks)])]
    pallas_call x0 -> x1, Pallas kernels: none -> 9.17 us  [run_experts(): pl.pallas_call(expert_kernel, out_shape=[shape_of(rows.shape, bf16)] + ke...]
    pallas_call x11 -> x10, Pallas kernels: 26.7 us -> 19.4 us  [call(): pl.pallas_call(kernel, out_shape=outs, in_specs=[pl.BlockSpec(memory_spac...]
    slice x2 -> x4, local copies, waits for them, and re-layouts: 4.53 us -> 6.75 us  [body(): lot[:, capacity:]]
    unnamed x25 -> x35, local copies, waits for them, and re-layouts: 2.49 us -> 4.68 us
    dot_general x2, matrix products: 3.45 us -> 5.33 us  [mm_t(): lax.dot_general(a, b, (((0,), (0,)), ((), ())), preferred_element_type=f32)]
  transfers between devices with their start and end apart: 9 -> 17, of which waited for: 7 -> 5; matrix products, arithmetic and copies ran while one was open for 5% -> 10% of each run, Pallas kernels for 6% -> 14%
where the time goes in v4:
time: 178 us; the launch traced here: 176 us
  starting transfers between devices  72.6 us (41%)
  waiting for transfers between devices  30.4 us (17%)
  Pallas kernels  28.5 us (16%)
  blocking collectives  25.9 us (15%)
  local copies, waits for them, and re-layouts  12.1 us (7%)
  matrix products  5.33 us (3%)
    all_to_all x5, starting transfers between devices, swap(): lax.all_to_all(a, axis, split_axis=0, concat_axis=0, tiled=True, axis_ind...  39.2 us
    all_to_all x5, waiting for transfers between devices, swap(): lax.all_to_all(a, axis, split_axis=0, concat_axis=0, tiled=True, axis_ind...  27.4 us
    all_to_all x1, blocking collectives, swap(): lax.all_to_all(a, axis, split_axis=0, concat_axis=0, tiled=True, axis_ind...  25.9 us
    pallas_call x10, Pallas kernels, call(): pl.pallas_call(kernel, out_shape=outs, in_specs=[pl.BlockSpec(memory_spac...  19.4 us
    ppermute x6, starting transfers between devices, partner(): return lax.ppermute(a, 'ctx', [(i, i ^ 1) for i in range(blocks)])  16.3 us
    ppermute x5, starting transfers between devices, near(): return lax.ppermute(a, 'ctx', [(i, near_of[i]) for i in range(blocks)])  13.1 us
    pallas_call x1, Pallas kernels, run_experts(): pl.pallas_call(expert_kernel, out_shape=[shape_of(rows.shape, bf16)] + ke...  9.17 us
    slice x4, local copies, waits for them, and re-layouts, body(): lot[:, capacity:]  6.75 us
  transfers between devices with their start and end apart: 17, of which 5 were waited for; matrix products, arithmetic and copies ran while one was open for 10% of the time, Pallas kernels for 14%

profile of v4, /device:TPU:1, one launch (start us, length us, event | category | flops | bytes accessed | tf_op | source)
XLA Modules:
  0.0 176.4 jit_solution(1081087061400613504)
XLA Ops:
  0.6 0.0 copy-start.7
  0.6 0.0 copy-start.8
  0.7 0.0 copy-start.10
  0.7 2.5 %shard_map.155 = (bf16[32,144,128]{2,1,0:T(8,128)(2,1)}, f32[128,128]{1,0:T(8,128)}) custom-call(bf16[128,128]{1,0:T(8,128)(2,1)} %x_ref.3, bf16[128,128]{1,0:T(8,128)(2,1)} %b_ref.5, f32[4,128]{1,0:T(4,128)} %bitcast.32), custom_call_target="tpu_custom_call" | custom-call | tf_op jit(solution)/shard_map/pallas_call | solution.py:60
  3.1 10.4 %all-to-all-start = ((bf16[32,144,128]{2,1,0:T(8,128)(2,1)}), bf16[32,144,128]{2,1,0:T(8,128)(2,1)S(1)}, u32[]{:S(2)}, u32[]{:S(2)}) async-start(bf16[32,144,128]{2,1,0:T(8,128)(2,1)} %get-tuple-element.27), calls=%async_computation | async-start | bytes 2359296 | tf_op jit(solution)/shard_map/all_to_all | solution.py:360
  13.6 3.3 %collective-permute-start.2 = (bf16[2048,256]{1,0:T(8,128)(2,1)S(1)}, bf16[2048,256]{1,0:T(8,128)(2,1)}, u32[]{:S(2)}, u32[]{:S(2)}) collective-permute-start(bf16[2048,256]{1,0:T(8,128)(2,1)S(1)} %bitcast.24), channel_id=1, source_target_pairs={{0,128},{16,48},{32,160},{48,16},{64,192},{80,112},{96,224},{112,8... | collective-permute-start | bytes 3145736 | tf_op jit(solution)/shard_map/ppermute | solution.py:411
  16.9 2.0 %collective-permute-start.3 = (bf16[256,2048]{1,0:T(8,128)(2,1)S(1)}, bf16[256,2048]{1,0:T(8,128)(2,1)}, u32[]{:S(2)}, u32[]{:S(2)}) collective-permute-start(bf16[256,2048]{1,0:T(8,128)(2,1)S(1)} %bitcast.27), channel_id=1, source_target_pairs={{0,128},{16,48},{32,160},{48,16},{64,192},{80,112},{96,224},{112,8... | collective-permute-start | bytes 3145736 | tf_op jit(solution)/shard_map/ppermute | solution.py:411
  18.9 0.7 copy.18.weight_ref
  19.7 0.7 copy.17.ids_ref
  20.4 2.0 %shard_map.156 = (f32[128,128]{1,0:T(8,128)}, bf16[2,4,128,128]{3,2,1,0:T(8,128)(2,1)}) custom-call(bf16[128,128]{1,0:T(8,128)(2,1)} %x_ref.3, bf16[128,128]{1,0:T(8,128)(2,1)} %b_ref.5, bf16[128,128]{1,0:T(8,128)(2,1)} %c_ref.5, f32[128,128]{1,0:T(8,128)} %get-tuple-element.28.cum_ref, f32[1,4]{1,0:T(1,128)} %bitcast.30, bf16[128,128]{1,0:T(8,128)(2,1)} %residual_ref.1), custom_call_target="tpu_custom_call" | custom-call | tf_op jit(solution)/shard_map/pallas_call | solution.py:60
  22.3 2.0 %shard_map.157 = (bf16[256,128]{1,0:T(8,128)(2,1)}, bf16[2,128,256]{2,1,0:T(8,128)(2,1)}, bf16[16,24,128]{2,1,0:T(8,128)(2,1)}) custom-call(s32[128,2]{1,0:T(8,128)} %copy.17.ids_ref, s32[2,128]{1,0:T(2,128)} %bitcast.29, f32[128,2]{1,0:T(8,128)} %copy.18.weight_ref, bf16[128,128]{1,0:T(8,128)(2,1)} %grad_ref.3, f32[1,128]{1,0:T(1,128)} %bitcast.33), custom_call_target="tpu_custom_call" | custom-call | tf_op jit(solution)/shard_map/pallas_call | solution.py:60
  24.4 7.7 %all-to-all-done.states_ref = bf16[32,144,128]{2,1,0:T(8,128)(2,1)S(1)} async-done(((bf16[32,144,128]{2,1,0:T(8,128)(2,1)}), bf16[32,144,128]{2,1,0:T(8,128)(2,1)S(1)}, u32[]{:S(2)}, u32[]{:S(2)}) %all-to-all-start) | async-done | bytes 1179680 | tf_op jit(solution)/shard_map/all_to_all | solution.py:360
  32.0 0.9 copy-done.2
  32.9 2.4 %shard_map.158 = (bf16[128,128]{1,0:T(8,128)(2,1)}, bf16[16,40,128]{2,1,0:T(8,128)(2,1)}, f32[32,128]{1,0:T(8,128)}) custom-call(s32[1]{0:T(128)} %bitcast.me_ref, bf16[32,144,128]{2,1,0:T(8,128)(2,1)S(1)} %all-to-all-done.states_ref, bf16[128,128]{1,0:T(8,128)(2,1)} %c_ref.5, f32[128,128]{1,0:T(8,128)} %get-tuple-element.28.cum_ref, ...), custom_call_target="tpu_custom_call" | custom-call | tf_op jit(solution)/shard_map/pallas_call | solution.py:60
  35.3 25.9 %all_to_all.30.in_ref = bf16[16,40,128]{2,1,0:T(8,128)(2,1)S(1)} all-to-all(bf16[16,40,128]{2,1,0:T(8,128)(2,1)} %get-tuple-element.32), channel_id=1, replica_groups=mesh['ctx'=32,'exp'=16] {'exp'}, dimensions={0} | all-to-all | bytes 327680 | tf_op jit(solution)/shard_map/all_to_all | solution.py:360
  61.2 1.2 shard_map.159
  62.4 3.6 %all-to-all-start.2 = ((bf16[8,32,2048]{2,1,0:T(8,128)(2,1)}), bf16[8,32,2048]{2,1,0:T(8,128)(2,1)S(1)}, u32[]{:S(2)}, u32[]{:S(2)}) async-start(bf16[8,32,2048]{2,1,0:T(8,128)(2,1)} %get-tuple-element.33), calls=%async_computation.2 | async-start | bytes 2097152 | tf_op jit(solution)/shard_map/all_to_all | solution.py:360
  65.9 4.3 %collective-permute-start = (bf16[2048,256]{1,0:T(8,128)(2,1)S(1)}, bf16[2048,256]{1,0:T(8,128)(2,1)}, u32[]{:S(2)}, u32[]{:S(2)}) collective-permute-start(bf16[2048,256]{1,0:T(8,128)(2,1)S(1)} %bitcast.25), channel_id=1, source_target_pairs={{0,16},{16,0},{32,48},{48,32},{64,80},{80,64},{96,112},{112,96},{1... | collective-permute-start | bytes 3145736 | tf_op jit(solution)/shard_map/ppermute | solution.py:408
  70.3 1.9 %collective-permute-start.1 = (bf16[256,2048]{1,0:T(8,128)(2,1)S(1)}, bf16[256,2048]{1,0:T(8,128)(2,1)}, u32[]{:S(2)}, u32[]{:S(2)}) collective-permute-start(bf16[256,2048]{1,0:T(8,128)(2,1)S(1)} %bitcast.28), channel_id=1, source_target_pairs={{0,16},{16,0},{32,48},{48,32},{64,80},{80,64},{96,112},{112,96},{1... | collective-permute-start | bytes 3145736 | tf_op jit(solution)/shard_map/ppermute | solution.py:408
  72.2 0.0 collective-permute-done.2.refs_5_
  72.2 2.4 %collective-permute-start.4 = (bf16[2048,256]{1,0:T(8,128)(2,1)}, bf16[2048,256]{1,0:T(8,128)(2,1)}, u32[]{:S(2)}, u32[]{:S(2)}) collective-permute-start(bf16[2048,256]{1,0:T(8,128)(2,1)} %collective-permute-done.2.refs_5_), channel_id=1, source_target_pairs={{0,16},{16,0},{32,48},{48,32},{64,80},{80,64},{96,112},{112,96},{1... | collective-permute-start | bytes 3145736 | tf_op jit(solution)/shard_map/ppermute | solution.py:408
  74.6 0.0 collective-permute-done.3.refs_6_
  74.6 1.9 %collective-permute-start.5 = (bf16[256,2048]{1,0:T(8,128)(2,1)}, bf16[256,2048]{1,0:T(8,128)(2,1)}, u32[]{:S(2)}, u32[]{:S(2)}) collective-permute-start(bf16[256,2048]{1,0:T(8,128)(2,1)} %collective-permute-done.3.refs_6_), channel_id=1, source_target_pairs={{0,16},{16,0},{32,48},{48,32},{64,80},{80,64},{96,112},{112,96},{1... | collective-permute-start | bytes 3145736 | tf_op jit(solution)/shard_map/ppermute | solution.py:408
  76.6 6.2 %all-to-all-done.2.refs_0_ = bf16[8,32,2048]{2,1,0:T(8,128)(2,1)S(1)} async-done(((bf16[8,32,2048]{2,1,0:T(8,128)(2,1)}), bf16[8,32,2048]{2,1,0:T(8,128)(2,1)S(1)}, u32[]{:S(2)}, u32[]{:S(2)}) %all-to-all-start.2) | async-done | bytes 1048608 | tf_op jit(solution)/shard_map/all_to_all | solution.py:360
  82.8 3.8 %collective-permute-start.6 = (bf16[8,32,2048]{2,1,0:T(8,128)(2,1)S(1)}, bf16[8,32,2048]{2,1,0:T(8,128)(2,1)}, u32[]{:S(2)}, u32[]{:S(2)}) collective-permute-start(bf16[8,32,2048]{2,1,0:T(8,128)(2,1)S(1)} %all-to-all-done.2.refs_0_), channel_id=1, source_target_pairs={{0,16},{16,0},{32,48},{48,32},{64,80},{80,64},{96,112},{112,96},{1... | collective-permute-start | bytes 3145736 | tf_op jit(solution)/shard_map/ppermute | solution.py:408
  86.6 0.0 collective-permute-done.refs_3_
  86.6 0.0 collective-permute-done.1.refs_4_
  86.6 0.0 collective-permute-done.4.refs_7_
  86.7 0.0 collective-permute-done.5.refs_8_
  86.7 9.2 %shard_map.160 = (bf16[8,32,2048]{2,1,0:T(8,128)(2,1)}, bf16[2,128,256]{2,1,0:T(8,128)(2,1)}, bf16[2,128,256]{2,1,0:T(8,128)(2,1)}, bf16[2,128,256]{2,1,0:T(8,128)(2,1)}, bf16[2,128,256]{2,1,0:T(8,128)(2,1)}) custom-call(bf16[8,32,2048]{2,1,0:T(8,128)(2,1)S(1)} %all-to-all-done.2.refs_0_, bf16[2048,256]{1,0:T(8,128)(2,1)} %bitcast.23, ...), custom_call_target="tpu_custom_call" | custom-call | tf_op jit(solution)/shard_map/pallas_call | solution.py:284
  95.9 0.0 copy-start.9
  95.9 3.7 %all-to-all-start.3 = ((bf16[8,32,2048]{2,1,0:T(8,128)(2,1)}), bf16[8,32,2048]{2,1,0:T(8,128)(2,1)S(1)}, u32[]{:S(2)}, u32[]{:S(2)}) async-start(bf16[8,32,2048]{2,1,0:T(8,128)(2,1)} %get-tuple-element.34), calls=%async_computation.3 | async-start | bytes 2097152 | tf_op jit(solution)/shard_map/all_to_all | solution.py:360
  99.6 1.9 %collective-permute-start.9 = (bf16[2,128,256]{2,1,0:T(8,128)(2,1)S(1)}, bf16[2,128,256]{2,1,0:T(8,128)(2,1)S(1)}, u32[]{:S(2)}, u32[]{:S(2)}) collective-permute-start(bf16[2,128,256]{2,1,0:T(8,128)(2,1)S(1)} %copy-done.14), channel_id=1, source_target_pairs={{0,16},{16,0},{32,48},{48,32},{64,80},{80,64},{96,112},{112,96},{1... | collective-permute-start | bytes 393224 | tf_op jit(solution)/shard_map/ppermute | solution.py:408
  101.5 1.9 %collective-permute-start.10 = (bf16[2,128,256]{2,1,0:T(8,128)(2,1)S(1)}, bf16[2,128,256]{2,1,0:T(8,128)(2,1)S(1)}, u32[]{:S(2)}, u32[]{:S(2)}) collective-permute-start(bf16[2,128,256]{2,1,0:T(8,128)(2,1)S(1)} %copy-done.13), channel_id=1, source_target_pairs={{0,128},{16,48},{32,160},{48,16},{64,192},{80,112},{96,224},{112,8... | collective-permute-start | bytes 393224 | tf_op jit(solution)/shard_map/ppermute | solution.py:411
  103.5 4.0 %collective-permute-start.11 = (bf16[2,128,256]{2,1,0:T(8,128)(2,1)S(1)}, bf16[2,128,256]{2,1,0:T(8,128)(2,1)S(1)}, u32[]{:S(2)}, u32[]{:S(2)}) collective-permute-start(bf16[2,128,256]{2,1,0:T(8,128)(2,1)S(1)} %copy-done.12), channel_id=1, source_target_pairs={{0,48},{16,128},{32,16},{48,160},{64,112},{80,192},{96,80},{112,22... | collective-permute-start | bytes 393224 | tf_op jit(solution)/shard_map/ppermute | solution.py:414
  107.5 2.7 %collective-permute-start.7 = (bf16[8,32,2048]{2,1,0:T(8,128)(2,1)S(1)}, bf16[8,32,2048]{2,1,0:T(8,128)(2,1)}, u32[]{:S(2)}, u32[]{:S(2)}) collective-permute-start(bf16[8,32,2048]{2,1,0:T(8,128)(2,1)S(1)} %all-to-all-done.2.refs_0_), channel_id=1, source_target_pairs={{0,128},{16,48},{32,160},{48,16},{64,192},{80,112},{96,224},{112,8... | collective-permute-start | bytes 3145736 | tf_op jit(solution)/shard_map/ppermute | solution.py:411
  110.2 0.9 fusion.2
  111.1 0.7 constant_dynamic-update-slice_fusion.3
  111.8 0.7 constant_dynamic-update-slice_fusion.2
  112.5 0.0 collective-permute-done.10
  112.5 0.7 constant_dynamic-update-slice_fusion.1
  113.2 0.0 collective-permute-done.6
  113.2 3.2 %collective-permute-start.8 = (bf16[8,32,2048]{2,1,0:T(8,128)(2,1)}, bf16[8,32,2048]{2,1,0:T(8,128)(2,1)}, u32[]{:S(2)}, u32[]{:S(2)}) collective-permute-start(bf16[8,32,2048]{2,1,0:T(8,128)(2,1)} %collective-permute-done.6), channel_id=1, source_target_pairs={{0,128},{16,48},{32,160},{48,16},{64,192},{80,112},{96,224},{112,8... | collective-permute-start | bytes 3145736 | tf_op jit(solution)/shard_map/ppermute | solution.py:411
  116.3 3.0 %collective-permute-done.11 = bf16[2,128,256]{2,1,0:T(8,128)(2,1)S(1)} collective-permute-done((bf16[2,128,256]{2,1,0:T(8,128)(2,1)S(1)}, bf16[2,128,256]{2,1,0:T(8,128)(2,1)S(1)}, u32[]{:S(2)}, u32[]{:S(2)}) %collective-permute-start.11) | collective-permute-done | bytes 131104 | tf_op jit(solution)/shard_map/ppermute | solution.py:414
  119.4 0.7 constant_dynamic-update-slice_fusion
  120.0 1.8 %shard_map.161 = bf16[16,32,128]{2,1,0:T(8,128)(2,1)} custom-call(bf16[8,32,2048]{2,1,0:T(8,128)(2,1)S(1)} %all-to-all-done.3.parts_ref, bf16[16,2048]{1,0:T(8,128)(2,1)} %get-tuple-element.35.raw_ref, f32[16,128]{1,0:T(8,128)} %get-tuple-element.36.inv_ref, f32[1,2048]{1,0:T(1,128)} %get-tuple-element.37.gain_ref), custom_call_target="tpu_custom_call" | custom-call | tf_op jit(solution)/shard_map/pallas_call | solution.py:60
  121.9 8.3 %all-to-all-start.4 = ((bf16[16,32,128]{2,1,0:T(8,128)(2,1)}), bf16[16,32,128]{2,1,0:T(8,128)(2,1)S(1)}, u32[]{:S(2)}, u32[]{:S(2)}) async-start(bf16[16,32,128]{2,1,0:T(8,128)(2,1)} %shard_map.161), calls=%async_computation.4 | async-start | bytes 262144 | tf_op jit(solution)/shard_map/all_to_all | solution.py:360
  130.2 2.1 %fusion.3 = (bf16[8,16,2048]{2,1,0:T(8,128)(2,1)S(1)}, bf16[8,16,2048]{2,1,0:T(8,128)(2,1)}) fusion(bf16[8,32,2048]{2,1,0:T(8,128)(2,1)} %collective-permute-done.6), kind=kLoop, calls=%fused_computation.13 | loop fusion | bytes 2097152 | tf_op jit(solution)/shard_map/slice | solution.py:477
  132.4 0.0 collective-permute-done.7
  132.4 2.3 %fusion.4 = (bf16[8,16,2048]{2,1,0:T(8,128)(2,1)}, bf16[8,16,2048]{2,1,0:T(8,128)(2,1)}) fusion(bf16[8,32,2048]{2,1,0:T(8,128)(2,1)} %collective-permute-done.7), kind=kLoop, calls=%fused_computation.14 | loop fusion | bytes 2097152 | tf_op jit(solution)/shard_map/slice | solution.py:477
  134.7 7.5 %all-to-all-done.4.rows_ref = bf16[16,32,128]{2,1,0:T(8,128)(2,1)S(1)} async-done(((bf16[16,32,128]{2,1,0:T(8,128)(2,1)}), bf16[16,32,128]{2,1,0:T(8,128)(2,1)S(1)}, u32[]{:S(2)}, u32[]{:S(2)}) %all-to-all-start.4) | async-done | bytes 131104 | tf_op jit(solution)/shard_map/all_to_all | solution.py:360
  142.2 2.3 %shard_map.163 = (bf16[128,128]{1,0:T(8,128)(2,1)}, f32[128,128]{1,0:T(8,128)}, bf16[32,128,128]{2,1,0:T(8,128)(2,1)}) custom-call(bf16[16,32,128]{2,1,0:T(8,128)(2,1)S(1)} %all-to-all-done.4.rows_ref, bf16[2,128,256]{2,1,0:T(8,128)(2,1)S(1)} %copy-done, bf16[128,128]{1,0:T(8,128)(2,1)} %grad_ref.3, bf16[128,128]{1,0:T(8,128)(2,1)} %c_ref.5, ...), custom_call_target="tpu_custom_call" | custom-call | tf_op jit(solution)/shard_map/pallas_call | solution.py:60
  144.5 13.2 %all-to-all-start.5 = ((bf16[32,128,128]{2,1,0:T(8,128)(2,1)}), bf16[32,128,128]{2,1,0:T(8,128)(2,1)S(1)}, u32[]{:S(2)}, u32[]{:S(2)}) async-start(bf16[32,128,128]{2,1,0:T(8,128)(2,1)} %get-tuple-element.41), calls=%async_computation.5 | async-start | bytes 2097152 | tf_op jit(solution)/shard_map/all_to_all | solution.py:360
  157.7 1.7 shard_map.164.local_ref
  159.4 1.6 shard_map.162
  161.0 0.0 collective-permute-done.8
  161.0 1.4 fusion.5
  162.4 0.1 copy-done.5
  162.5 0.2 copy-done.6
  162.7 0.5 pad_maximum_fusion
  163.2 2.7 %fusion.1 = bf16[1,256,2048]{2,1,0:T(8,128)(2,1)} fusion(bf16[512,2048]{1,0:T(8,128)(2,1)S(1)} %bitcast.21, bf16[2,512,256]{2,1,0:T(8,128)(2,1)} %constant_dynamic-update-slice_fusion), kind=kOutput, calls=%fused_computation.3 | convolution fusion | flops 537395200 | bytes 3407872 | tf_op jit(solution)/shard_map/dot_general | solution.py:24
  165.9 2.7 %fusion = bf16[1,2048,256]{2,1,0:T(8,128)(2,1)} fusion(bf16[512,2048]{1,0:T(8,128)(2,1)S(1)} %bitcast.22, bf16[2,512,256]{2,1,0:T(8,128)(2,1)} %constant_dynamic-update-slice_fusion), kind=kOutput, calls=%fused_computation.2 | convolution fusion | flops 537395200 | bytes 3407872 | tf_op jit(solution)/shard_map/dot_general | solution.py:24
  168.6 6.0 %all-to-all-done.5.states_ref = bf16[32,128,128]{2,1,0:T(8,128)(2,1)S(1)} async-done(((bf16[32,128,128]{2,1,0:T(8,128)(2,1)}), bf16[32,128,128]{2,1,0:T(8,128)(2,1)S(1)}, u32[]{:S(2)}, u32[]{:S(2)}) %all-to-all-start.5) | async-done | bytes 1048608 | tf_op jit(solution)/shard_map/all_to_all | solution.py:360
  174.6 1.9 %shard_map.165 = bf16[128,128]{1,0:T(8,128)(2,1)} custom-call(bf16[32,128,128]{2,1,0:T(8,128)(2,1)S(1)} %all-to-all-done.5.states_ref, f32[32,128]{1,0:T(8,128)} %get-tuple-element.42.later_ref, bf16[128,128]{1,0:T(8,128)(2,1)} %b_ref.5, f32[128,128]{1,0:T(8,128)} %get-tuple-element.28.cum_ref, f32[128,128]{1,0:T(8,128)} %shard_map.164.local_ref), custom_call_target="tpu_custom_call" | custom-call | tf_op jit(solution)/shard_map/pallas_call | solution.py:60
  (25 shorter events, 0.1 us)
Async XLA Ops:
  0.6 12.9 %copy-start.7 = (bf16[1,2048,256]{2,1,0:T(8,128)(2,1)S(1)}, bf16[1,2048,256]{2,1,0:T(8,128)(2,1)}, u32[]{:S(2)}) copy-start(bf16[1,2048,256]{2,1,0:T(8,128)(2,1)} %param.21) | copy-start | bytes 3145732
  0.6 16.2 %copy-start.8 = (bf16[1,256,2048]{2,1,0:T(8,128)(2,1)S(1)}, bf16[1,256,2048]{2,1,0:T(8,128)(2,1)}, u32[]{:S(2)}) copy-start(bf16[1,256,2048]{2,1,0:T(8,128)(2,1)} %param.22) | copy-start | bytes 3145732
  0.7 18.2 %copy-start.11 = (f32[128,2]{0,1:T(2,128)S(1)}, f32[128,2]{0,1:T(2,128)}, u32[]{:S(2)}) copy-start(f32[128,2]{0,1:T(2,128)} %param.19) | copy-start | bytes 3076
  0.7 19.0 %copy-start.10 = (s32[128,2]{0,1:T(2,128)S(1)}, s32[128,2]{0,1:T(2,128)}, u32[]{:S(2)}) copy-start(s32[128,2]{0,1:T(2,128)} %param.20) | copy-start | bytes 3076
  3.1 28.9 %all-to-all-start = ((bf16[32,144,128]{2,1,0:T(8,128)(2,1)}), bf16[32,144,128]{2,1,0:T(8,128)(2,1)S(1)}, u32[]{:S(2)}, u32[]{:S(2)}) async-start(bf16[32,144,128]{2,1,0:T(8,128)(2,1)} %get-tuple-element.27), calls=%async_computation | async-start | bytes 2359296 | tf_op jit(solution)/shard_map/all_to_all | solution.py:360
  13.6 58.6 %collective-permute-start.2 = (bf16[2048,256]{1,0:T(8,128)(2,1)S(1)}, bf16[2048,256]{1,0:T(8,128)(2,1)}, u32[]{:S(2)}, u32[]{:S(2)}) collective-permute-start(bf16[2048,256]{1,0:T(8,128)(2,1)S(1)} %bitcast.24), channel_id=1, source_target_pairs={{0,128},{16,48},{32,160},{48,16},{64,192},{80,112},{96,224},{112,8... | collective-permute-start | bytes 3145736 | tf_op jit(solution)/shard_map/ppermute | solution.py:411
  16.9 57.8 %collective-permute-start.3 = (bf16[256,2048]{1,0:T(8,128)(2,1)S(1)}, bf16[256,2048]{1,0:T(8,128)(2,1)}, u32[]{:S(2)}, u32[]{:S(2)}) collective-permute-start(bf16[256,2048]{1,0:T(8,128)(2,1)S(1)} %bitcast.27), channel_id=1, source_target_pairs={{0,128},{16,48},{32,160},{48,16},{64,192},{80,112},{96,224},{112,8... | collective-permute-start | bytes 3145736 | tf_op jit(solution)/shard_map/ppermute | solution.py:411
  32.0 0.9 copy-start.2
  62.4 20.5 %all-to-all-start.2 = ((bf16[8,32,2048]{2,1,0:T(8,128)(2,1)}), bf16[8,32,2048]{2,1,0:T(8,128)(2,1)S(1)}, u32[]{:S(2)}, u32[]{:S(2)}) async-start(bf16[8,32,2048]{2,1,0:T(8,128)(2,1)} %get-tuple-element.33), calls=%async_computation.2 | async-start | bytes 2097152 | tf_op jit(solution)/shard_map/all_to_all | solution.py:360
  65.9 20.7 %collective-permute-start = (bf16[2048,256]{1,0:T(8,128)(2,1)S(1)}, bf16[2048,256]{1,0:T(8,128)(2,1)}, u32[]{:S(2)}, u32[]{:S(2)}) collective-permute-start(bf16[2048,256]{1,0:T(8,128)(2,1)S(1)} %bitcast.25), channel_id=1, source_target_pairs={{0,16},{16,0},{32,48},{48,32},{64,80},{80,64},{96,112},{112,96},{1... | collective-permute-start | bytes 3145736 | tf_op jit(solution)/shard_map/ppermute | solution.py:408
  70.3 16.4 %collective-permute-start.1 = (bf16[256,2048]{1,0:T(8,128)(2,1)S(1)}, bf16[256,2048]{1,0:T(8,128)(2,1)}, u32[]{:S(2)}, u32[]{:S(2)}) collective-permute-start(bf16[256,2048]{1,0:T(8,128)(2,1)S(1)} %bitcast.28), channel_id=1, source_target_pairs={{0,16},{16,0},{32,48},{48,32},{64,80},{80,64},{96,112},{112,96},{1... | collective-permute-start | bytes 3145736 | tf_op jit(solution)/shard_map/ppermute | solution.py:408
  72.2 14.4 %collective-permute-start.4 = (bf16[2048,256]{1,0:T(8,128)(2,1)}, bf16[2048,256]{1,0:T(8,128)(2,1)}, u32[]{:S(2)}, u32[]{:S(2)}) collective-permute-start(bf16[2048,256]{1,0:T(8,128)(2,1)} %collective-permute-done.2.refs_5_), channel_id=1, source_target_pairs={{0,16},{16,0},{32,48},{48,32},{64,80},{80,64},{96,112},{112,96},{1... | collective-permute-start | bytes 3145736 | tf_op jit(solution)/shard_map/ppermute | solution.py:408
  74.6 12.0 %collective-permute-start.5 = (bf16[256,2048]{1,0:T(8,128)(2,1)}, bf16[256,2048]{1,0:T(8,128)(2,1)}, u32[]{:S(2)}, u32[]{:S(2)}) collective-permute-start(bf16[256,2048]{1,0:T(8,128)(2,1)} %collective-permute-done.3.refs_6_), channel_id=1, source_target_pairs={{0,16},{16,0},{32,48},{48,32},{64,80},{80,64},{96,112},{112,96},{1... | collective-permute-start | bytes 3145736 | tf_op jit(solution)/shard_map/ppermute | solution.py:408
  82.8 30.3 %collective-permute-start.6 = (bf16[8,32,2048]{2,1,0:T(8,128)(2,1)S(1)}, bf16[8,32,2048]{2,1,0:T(8,128)(2,1)}, u32[]{:S(2)}, u32[]{:S(2)}) collective-permute-start(bf16[8,32,2048]{2,1,0:T(8,128)(2,1)S(1)} %all-to-all-done.2.refs_0_), channel_id=1, source_target_pairs={{0,16},{16,0},{32,48},{48,32},{64,80},{80,64},{96,112},{112,96},{1... | collective-permute-start | bytes 3145736 | tf_op jit(solution)/shard_map/ppermute | solution.py:408
  95.8 3.8 %copy-start.14 = (bf16[2,128,256]{2,1,0:T(8,128)(2,1)S(1)}, bf16[2,128,256]{2,1,0:T(8,128)(2,1)}, u32[]{:S(2)}) copy-start(bf16[2,128,256]{2,1,0:T(8,128)(2,1)} %get-tuple-element.46) | copy-start | bytes 393220
  95.9 5.7 %copy-start.13 = (bf16[2,128,256]{2,1,0:T(8,128)(2,1)S(1)}, bf16[2,128,256]{2,1,0:T(8,128)(2,1)}, u32[]{:S(2)}) copy-start(bf16[2,128,256]{2,1,0:T(8,128)(2,1)} %get-tuple-element.47) | copy-start | bytes 393220
  95.9 7.6 %copy-start.12 = (bf16[2,128,256]{2,1,0:T(8,128)(2,1)S(1)}, bf16[2,128,256]{2,1,0:T(8,128)(2,1)}, u32[]{:S(2)}) copy-start(bf16[2,128,256]{2,1,0:T(8,128)(2,1)} %get-tuple-element.48) | copy-start | bytes 393220
  95.9 15.3 %copy-start.9 = (bf16[2,128,256]{2,1,0:T(8,128)(2,1)S(1)}, bf16[2,128,256]{2,1,0:T(8,128)(2,1)}, u32[]{:S(2)}) copy-start(bf16[2,128,256]{2,1,0:T(8,128)(2,1)} %get-tuple-element.45) | copy-start | bytes 393220
  95.9 24.1 %all-to-all-start.3 = ((bf16[8,32,2048]{2,1,0:T(8,128)(2,1)}), bf16[8,32,2048]{2,1,0:T(8,128)(2,1)S(1)}, u32[]{:S(2)}, u32[]{:S(2)}) async-start(bf16[8,32,2048]{2,1,0:T(8,128)(2,1)} %get-tuple-element.34), calls=%async_computation.3 | async-start | bytes 2097152 | tf_op jit(solution)/shard_map/all_to_all | solution.py:360
  99.6 12.2 %collective-permute-start.9 = (bf16[2,128,256]{2,1,0:T(8,128)(2,1)S(1)}, bf16[2,128,256]{2,1,0:T(8,128)(2,1)S(1)}, u32[]{:S(2)}, u32[]{:S(2)}) collective-permute-start(bf16[2,128,256]{2,1,0:T(8,128)(2,1)S(1)} %copy-done.14), channel_id=1, source_target_pairs={{0,16},{16,0},{32,48},{48,32},{64,80},{80,64},{96,112},{112,96},{1... | collective-permute-start | bytes 393224 | tf_op jit(solution)/shard_map/ppermute | solution.py:408
  101.5 10.9 %collective-permute-start.10 = (bf16[2,128,256]{2,1,0:T(8,128)(2,1)S(1)}, bf16[2,128,256]{2,1,0:T(8,128)(2,1)S(1)}, u32[]{:S(2)}, u32[]{:S(2)}) collective-permute-start(bf16[2,128,256]{2,1,0:T(8,128)(2,1)S(1)} %copy-done.13), channel_id=1, source_target_pairs={{0,128},{16,48},{32,160},{48,16},{64,192},{80,112},{96,224},{112,8... | collective-permute-start | bytes 393224 | tf_op jit(solution)/shard_map/ppermute | solution.py:411
  103.5 15.9 %collective-permute-start.11 = (bf16[2,128,256]{2,1,0:T(8,128)(2,1)S(1)}, bf16[2,128,256]{2,1,0:T(8,128)(2,1)S(1)}, u32[]{:S(2)}, u32[]{:S(2)}) collective-permute-start(bf16[2,128,256]{2,1,0:T(8,128)(2,1)S(1)} %copy-done.12), channel_id=1, source_target_pairs={{0,48},{16,128},{32,16},{48,160},{64,112},{80,192},{96,80},{112,22... | collective-permute-start | bytes 393224 | tf_op jit(solution)/shard_map/ppermute | solution.py:414
  107.5 24.8 %collective-permute-start.7 = (bf16[8,32,2048]{2,1,0:T(8,128)(2,1)S(1)}, bf16[8,32,2048]{2,1,0:T(8,128)(2,1)}, u32[]{:S(2)}, u32[]{:S(2)}) collective-permute-start(bf16[8,32,2048]{2,1,0:T(8,128)(2,1)S(1)} %all-to-all-done.2.refs_0_), channel_id=1, source_target_pairs={{0,128},{16,48},{32,160},{48,16},{64,192},{80,112},{96,224},{112,8... | collective-permute-start | bytes 3145736 | tf_op jit(solution)/shard_map/ppermute | solution.py:411
  113.2 47.9 %collective-permute-start.8 = (bf16[8,32,2048]{2,1,0:T(8,128)(2,1)}, bf16[8,32,2048]{2,1,0:T(8,128)(2,1)}, u32[]{:S(2)}, u32[]{:S(2)}) collective-permute-start(bf16[8,32,2048]{2,1,0:T(8,128)(2,1)} %collective-permute-done.6), channel_id=1, source_target_pairs={{0,128},{16,48},{32,160},{48,16},{64,192},{80,112},{96,224},{112,8... | collective-permute-start | bytes 3145736 | tf_op jit(solution)/shard_map/ppermute | solution.py:411
  121.9 20.3 %all-to-all-start.4 = ((bf16[16,32,128]{2,1,0:T(8,128)(2,1)}), bf16[16,32,128]{2,1,0:T(8,128)(2,1)S(1)}, u32[]{:S(2)}, u32[]{:S(2)}) async-start(bf16[16,32,128]{2,1,0:T(8,128)(2,1)} %shard_map.161), calls=%async_computation.4 | async-start | bytes 262144 | tf_op jit(solution)/shard_map/all_to_all | solution.py:360
  130.2 12.0 %copy-start = (bf16[2,128,256]{2,1,0:T(8,128)(2,1)S(1)}, bf16[2,128,256]{2,1,0:T(8,128)(2,1)}, u32[]{:S(2)}) copy-start(bf16[2,128,256]{2,1,0:T(8,128)(2,1)} %get-tuple-element.38.from_ref) | copy-start | bytes 393220
  132.4 25.3 %copy-start.1 = (bf16[2,4,128,128]{3,2,1,0:T(8,128)(2,1)S(1)}, bf16[2,4,128,128]{3,2,1,0:T(8,128)(2,1)}, u32[]{:S(2)}) copy-start(bf16[2,4,128,128]{3,2,1,0:T(8,128)(2,1)} %get-tuple-element.44.back_ref) | copy-start | bytes 786436
  144.5 18.0 %copy-start.3 = (bf16[8,16,2048]{2,1,0:T(8,128)(2,1)S(1)}, bf16[8,16,2048]{2,1,0:T(8,128)(2,1)}, u32[]{:S(2)}) copy-start(bf16[8,16,2048]{2,1,0:T(8,128)(2,1)} %get-tuple-element.50) | copy-start | bytes 1572868
  144.5 30.1 %all-to-all-start.5 = ((bf16[32,128,128]{2,1,0:T(8,128)(2,1)}), bf16[32,128,128]{2,1,0:T(8,128)(2,1)S(1)}, u32[]{:S(2)}, u32[]{:S(2)}) async-start(bf16[32,128,128]{2,1,0:T(8,128)(2,1)} %get-tuple-element.41), calls=%async_computation.5 | async-start | bytes 2097152 | tf_op jit(solution)/shard_map/all_to_all | solution.py:360
  161.0 1.4 copy-start.4
  161.0 1.5 copy-start.5
  161.0 1.7 copy-start.6

commit v5 on v4

--- a/solution.py
+++ b/solution.py
@@ -54,7 +54,9 @@
 
 def call(kernel, outs, *args, smem=(), near=()):
     args = [
-        pltpu.with_memory_space_constraint(a, pltpu.VMEM) if a.ndim > 2 or i in near else a
+        pltpu.with_memory_space_constraint(a, pltpu.VMEM)
+        if near is not None and (a.ndim > 2 or i in near)
+        else a
         for i, a in enumerate(args)
     ]
     return pl.pallas_call(
@@ -235,60 +237,104 @@
             out_ref[j, capacity:, here] = cot
 
 
-def expert_kernel(*refs):
-    rows_ref = refs[0]
-    weights = refs[1:9]
-    parts_ref = refs[9]
-    units = refs[10:14]
-    held = refs[14:22]
-    sems = refs[22]
+def pack_kernel(in_ref, down_ref, out_ref):
+    units = down_ref.shape[0]
+    for k in range(in_ref.shape[0] // units):
+        here = slice(k * units, (k + 1) * units)
+        out_ref[0, :, here] = in_ref[here, :]
+    out_ref[1] = down_ref[...]
+
+
+def pack_units(out_ref, lot, activated, d_hidden):
+    units = activated.shape[1]
+    capacity = out_ref.shape[1] // 2
+    for k in range(activated.shape[0] // capacity):
+        rows = slice(k * capacity, (k + 1) * capacity)
+        here = slice(k * units, (k + 1) * units)
+        out_ref[lot, :capacity, here] = activated[rows, :]
+        out_ref[lot, capacity:, here] = d_hidden[rows, :]
+
+
+def expert_kernel(rows_ref, own_ref, peer_ref, near_ref, far_ref, parts_ref, mine_ref, send_ref, held, sems):
     copies = [
-        pltpu.make_async_copy(source, target, sems.at[k])
-        for k, (source, target) in enumerate(zip(weights, held))
+        pltpu.make_async_copy(source, held.at[k], sems.at[k])
+        for k, source in enumerate((own_ref, peer_ref, near_ref, far_ref))
     ]
     for copy in copies:
         copy.start()
     chips, both, width = rows_ref.shape
     capacity = both // 2
     count = chips * capacity
+    units = held.shape[2]
+    blocks = [slice(k * units, (k + 1) * units) for k in range(width // units)]
     rows = rows_ref[:, :capacity, :].reshape(count, width)
     cot = rows_ref[:, capacity:, :].reshape(count, width)
-    d_total = None
+    send_ref[:chips] = rows_ref[...]
+    d_total = [None] * len(blocks)
     out_total = None
     for k in range(4):
-        copies[2 * k].wait()
-        copies[2 * k + 1].wait()
-        wide = held[2 * k][...]
-        narrow = held[2 * k + 1][...]
-        hidden = mm(rows, wide)
+        copies[k].wait()
+        wide = [held[k, 0, :, here] for here in blocks]
+        narrow = held[k, 1]
+        hidden = mm(rows[:, blocks[0]], wide[0])
+        for here, piece in zip(blocks[1:], wide[1:]):
+            hidden = hidden + mm(rows[:, here], piece)
         d_act = mm_nt(cot, narrow)
         sigmoid_h = 1.0 / (1.0 + jnp.exp(-hidden))
         activated = (hidden * sigmoid_h).astype(bf16)
         d_hidden = (d_act * sigmoid_h * (1.0 + hidden * (1.0 - sigmoid_h))).astype(bf16)
-        units[k][0] = activated
-        units[k][1] = d_hidden
-        d_part = mm_nt(d_hidden, wide)
+        if k == 0:
+            mine_ref[0] = activated
+            mine_ref[1] = d_hidden
+        else:
+            pack_units(send_ref, chips + k - 1, activated, d_hidden)
+        d_part = [mm_nt(d_hidden, piece) for piece in wide]
         out_part = mm(activated, narrow)
-        d_total = d_part if d_total is None else d_total + d_part
-        out_total = out_part if out_total is None else out_total + out_part
-    parts_ref[:, :capacity, :] = d_total.astype(bf16).reshape(chips, capacity, width)
+        d_total = d_part if k == 0 else [a + b for a, b in zip(d_total, d_part)]
+        out_total = out_part if k == 0 else out_total + out_part
+    for here, piece in zip(blocks, d_total):
+        parts_ref[:, :capacity, here] = piece.astype(bf16).reshape(chips, capacity, units)
     parts_ref[:, capacity:, :] = out_total.astype(bf16).reshape(chips, capacity, width)
 
 
 def run_experts(rows, weights):
-    chips, both, _ = rows.shape
+    chips, both, width = rows.shape
     units = weights[0].shape[1]
     count = chips * both // 2
     near = pl.BlockSpec(memory_space=pltpu.VMEM)
-    kept = [shape_of((2, count, units), bf16)] * 4
     return pl.pallas_call(
         expert_kernel,
-        out_shape=[shape_of(rows.shape, bf16)] + kept,
-        in_specs=[near] + [pl.BlockSpec(memory_space=pl.ANY)] * 8,
-        out_specs=[near] * 5,
-        scratch_shapes=[pltpu.VMEM(w.shape, bf16) for w in weights]
-        + [pltpu.SemaphoreType.DMA((8,))],
+        out_shape=[
+            shape_of(rows.shape, bf16),
+            shape_of((2, count, units), bf16),
+            shape_of((chips + 3, both, width), bf16),
+        ],
+        in_specs=[near] + [pl.BlockSpec(memory_space=pl.ANY)] * 4,
+        out_specs=[near] * 3,
+        scratch_shapes=[
+            pltpu.VMEM((4,) + weights[0].shape, bf16),
+            pltpu.SemaphoreType.DMA((4,)),
+        ],
     )(pltpu.with_memory_space_constraint(rows, pltpu.VMEM), *weights)
+
+
+def weight_grad_kernel(own_ref, mine_ref, peer_ref, near_ref, far_ref, in_ref, down_ref):
+    chips, both, width = own_ref.shape
+    capacity = both // 2
+    count = chips * capacity
+    units = mine_ref.shape[2]
+    lots = [own_ref, peer_ref, near_ref, far_ref]
+    rows = jnp.concatenate([lot[:chips, :capacity, :].reshape(count, width) for lot in lots])
+    cot = jnp.concatenate([lot[:chips, capacity:, :].reshape(count, width) for lot in lots])
+    activated = [mine_ref[0]]
+    d_hidden = [mine_ref[1]]
+    for k, lot in enumerate(lots[1:]):
+        for j in range(count // capacity):
+            here = slice(j * units, (j + 1) * units)
+            activated.append(lot[chips + k, :capacity, here])
+            d_hidden.append(lot[chips + k, capacity:, here])
+    in_ref[...] = mm_t(rows, jnp.concatenate(d_hidden)).astype(bf16)
+    down_ref[...] = mm_t(jnp.concatenate(activated), cot).astype(bf16)
 
 
 def return_kernel(parts_ref, raw_ref, inv_ref, gain_ref, out_ref):
@@ -410,21 +456,18 @@
     def near(a):
         return lax.ppermute(a, "ctx", [(i, near_of[i]) for i in range(blocks)])
 
-    def across(a):
-        return lax.ppermute(a, "ctx", [(i, near_of[i ^ 1]) for i in range(blocks)])
-
     state_pay, cum = call(
         state_kernel,
         (shape_of((blocks, states + 16, features), bf16), shape_of((tokens, features), f32)),
         ssd_input, state_in, log_decay.T,
     )
     state_all = swap(state_pay, "ctx")
-    near_in = near(matrix_in)
-    near_down = near(matrix_down)
-    peer_in = partner(matrix_in)
-    peer_down = partner(matrix_down)
-    far_in = partner(near_in)
-    far_down = partner(near_down)
+    own_w = call(
+        pack_kernel, shape_of((2,) + matrix_down.shape, bf16), matrix_in, matrix_down
+    )
+    near_w = near(own_w)
+    peer_w = partner(own_w)
+    far_w = partner(near_w)
 
     to_rows, from_rows, cot_pay = call(
         route_kernel,
@@ -463,21 +506,17 @@
     )
     expert_rows = swap(spread, "ctx", colours)
 
-    parts, mine, of_peer, of_near, of_far = run_experts(
-        expert_rows,
-        (matrix_in, matrix_down, peer_in, peer_down, near_in, near_down, far_in, far_down),
-    )
+    parts, mine, send = run_experts(expert_rows, (own_w, peer_w, near_w, far_w))
     parts_all = swap(parts, "ctx", colours)
-    peer_rows = partner(expert_rows)
-    near_rows = near(expert_rows)
-    far_rows = near(peer_rows)
-    units = (mine, partner(of_peer), near(of_near), across(of_far))
-    lots = (expert_rows, peer_rows, near_rows, far_rows)
-    all_rows = jnp.concatenate([lot[:, :capacity] for lot in lots]).reshape(-1, D)
-    all_cot = jnp.concatenate([lot[:, capacity:] for lot in lots]).reshape(-1, D)
-    all_units = jnp.concatenate(units, axis=1)
-    grad_down = mm_t(all_units[0], all_cot).astype(bf16)
-    grad_in = mm_t(all_rows, all_units[1]).astype(bf16)
+    peer_lot = partner(send)
+    near_lot = near(send)
+    far_lot = near(peer_lot)
+    grad_in, grad_down = call(
+        weight_grad_kernel,
+        (shape_of(matrix_in.shape, bf16), shape_of(matrix_down.shape, bf16)),
+        expert_rows, mine, peer_lot, near_lot, far_lot,
+        near=None,
+    )
 
     back_pay = call(
         return_kernel,

time: 178 us -> 204 us (1.15)
  waiting for transfers between devices: 30.4 us -> 61.9 us
  blocking collectives: 25.9 us -> 44.8 us
  starting transfers between devices: 72.6 us -> 55.9 us
  local copies, waits for them, and re-layouts: 12.1 us -> 2.38 us
  Pallas kernels: 28.5 us -> 37.1 us
  matrix products: 5.33 us -> 0 us
    all_to_all x1 -> x2, blocking collectives: 25.9 us -> 44.8 us  [swap(): lax.all_to_all(a, axis, split_axis=0, concat_axis=0, tiled=True, axis_ind...]
    ppermute x5 -> x3, waiting for transfers between devices: 0.01 us -> 18.9 us  [near(): return lax.ppermute(a, 'ctx', [(i, near_of[i]) for i in range(blocks)])]
    all_to_all x5 -> x4, waiting for transfers between devices: 27.4 us -> 42.9 us  [swap(): lax.all_to_all(a, axis, split_axis=0, concat_axis=0, tiled=True, axis_ind...]
    all_to_all x5 -> x4, starting transfers between devices: 39.2 us -> 28.8 us  [swap(): lax.all_to_all(a, axis, split_axis=0, concat_axis=0, tiled=True, axis_ind...]
    pallas_call x10 -> x12, Pallas kernels: 19.4 us -> 27.6 us  [call(): pl.pallas_call(kernel, out_shape=outs, in_specs=[pl.BlockSpec(memory_spac...]
    slice x4 -> x0, local copies, waits for them, and re-layouts: 6.75 us -> none  [body(): lot[:, capacity:]]
    dot_general x2 -> x0, matrix products: 5.33 us -> none  [mm_t(): lax.dot_general(a, b, (((0,), (0,)), ((), ())), preferred_element_type=f32)]
    ppermute x1 -> x0, starting transfers between devices: 4.03 us -> none  [across(): return lax.ppermute(a, 'ctx', [(i, near_of[i ^ 1]) for i in range(blocks)])]
  transfers between devices with their start and end apart: 17 -> 10, of which waited for: 5 -> 4; matrix products, arithmetic and copies ran while one was open for 10% -> 1% of each run, Pallas kernels for 14% -> 9%
where the time goes in v5:
time: 204 us; the launch traced here: 203 us
  waiting for transfers between devices  61.9 us (30%)
  starting transfers between devices  55.9 us (27%)
  blocking collectives  44.8 us (22%)
  Pallas kernels  37.1 us (18%)
  local copies, waits for them, and re-layouts  2.38 us (1%)
    all_to_all x2, blocking collectives, swap(): lax.all_to_all(a, axis, split_axis=0, concat_axis=0, tiled=True, axis_ind...  44.8 us
    all_to_all x4, waiting for transfers between devices, swap(): lax.all_to_all(a, axis, split_axis=0, concat_axis=0, tiled=True, axis_ind...  42.9 us
    all_to_all x4, starting transfers between devices, swap(): lax.all_to_all(a, axis, split_axis=0, concat_axis=0, tiled=True, axis_ind...  28.8 us
    pallas_call x12, Pallas kernels, call(): pl.pallas_call(kernel, out_shape=outs, in_specs=[pl.BlockSpec(memory_spac...  27.6 us
    ppermute x3, waiting for transfers between devices, near(): return lax.ppermute(a, 'ctx', [(i, near_of[i]) for i in range(blocks)])  18.9 us
    ppermute x3, starting transfers between devices, partner(): return lax.ppermute(a, 'ctx', [(i, i ^ 1) for i in range(blocks)])  17.7 us
    pallas_call x1, Pallas kernels, run_experts(): pl.pallas_call(expert_kernel, out_shape=[shape_of(rows.shape, bf16), shap...  9.55 us
    ppermute x3, starting transfers between devices, near(): return lax.ppermute(a, 'ctx', [(i, near_of[i]) for i in range(blocks)])  9.43 us
  transfers between devices with their start and end apart: 10, of which 4 were waited for; matrix products, arithmetic and copies ran while one was open for 1% of the time, Pallas kernels for 9%

profile of v5, /device:TPU:1, one launch (start us, length us, event | category | flops | bytes accessed | tf_op | source)
XLA Modules:
  0.0 202.9 jit_solution(14194514957577223202)
XLA Ops:
  0.6 3.1 %shard_map.160.own_ref = bf16[2,256,2048]{2,1,0:T(8,128)(2,1)} custom-call(bf16[2048,256]{1,0:T(8,128)(2,1)} %bitcast.9, bf16[256,2048]{1,0:T(8,128)(2,1)} %bitcast.10), custom_call_target="tpu_custom_call" | custom-call | tf_op jit(solution)/shard_map/pallas_call | solution.py:62
  3.7 0.0 copy-start.4
  3.7 0.0 copy-start.7
  3.7 0.0 copy-start.6
  3.7 4.1 %collective-permute-start.1 = (bf16[2,256,2048]{2,1,0:T(8,128)(2,1)}, bf16[2,256,2048]{2,1,0:T(8,128)(2,1)}, u32[]{:S(2)}, u32[]{:S(2)}) collective-permute-start(bf16[2,256,2048]{2,1,0:T(8,128)(2,1)} %shard_map.160.own_ref), channel_id=1, source_target_pairs={{0,128},{16,48},{32,160},{48,16},{64,192},{80,112},{96,224},{112,8... | collective-permute-start | bytes 6291464 | tf_op jit(solution)/shard_map/ppermute | solution.py:457
  7.9 2.4 %shard_map.155 = (bf16[32,144,128]{2,1,0:T(8,128)(2,1)}, f32[128,128]{1,0:T(8,128)}) custom-call(bf16[128,128]{1,0:T(8,128)(2,1)} %x_ref.3, bf16[128,128]{1,0:T(8,128)(2,1)} %b_ref.5, f32[4,128]{1,0:T(4,128)} %bitcast.14), custom_call_target="tpu_custom_call" | custom-call | tf_op jit(solution)/shard_map/pallas_call | solution.py:62
  10.2 8.3 %all-to-all-start = ((bf16[32,144,128]{2,1,0:T(8,128)(2,1)}), bf16[32,144,128]{2,1,0:T(8,128)(2,1)S(1)}, u32[]{:S(2)}, u32[]{:S(2)}) async-start(bf16[32,144,128]{2,1,0:T(8,128)(2,1)} %get-tuple-element.27), calls=%async_computation | async-start | bytes 2359296 | tf_op jit(solution)/shard_map/all_to_all | solution.py:406
  18.6 0.0 copy-done.4
  18.6 2.3 %collective-permute-start = (bf16[2,256,2048]{2,1,0:T(8,128)(2,1)S(1)}, bf16[2,256,2048]{2,1,0:T(8,128)(2,1)}, u32[]{:S(2)}, u32[]{:S(2)}) collective-permute-start(bf16[2,256,2048]{2,1,0:T(8,128)(2,1)S(1)} %copy-done.4), channel_id=1, source_target_pairs={{0,16},{16,0},{32,48},{48,32},{64,80},{80,64},{96,112},{112,96},{1... | collective-permute-start | bytes 6291464 | tf_op jit(solution)/shard_map/ppermute | solution.py:454
  20.8 18.9 %collective-permute-done.1.near_ref = bf16[2,256,2048]{2,1,0:T(8,128)(2,1)} collective-permute-done((bf16[2,256,2048]{2,1,0:T(8,128)(2,1)}, bf16[2,256,2048]{2,1,0:T(8,128)(2,1)}, u32[]{:S(2)}, u32[]{:S(2)}) %collective-permute-start.1) | collective-permute-done | bytes 2097184 | tf_op jit(solution)/shard_map/ppermute | solution.py:457
  39.8 7.4 %collective-permute-start.2 = (bf16[2,256,2048]{2,1,0:T(8,128)(2,1)}, bf16[2,256,2048]{2,1,0:T(8,128)(2,1)}, u32[]{:S(2)}, u32[]{:S(2)}) collective-permute-start(bf16[2,256,2048]{2,1,0:T(8,128)(2,1)} %collective-permute-done.1.near_ref), channel_id=1, source_target_pairs={{0,16},{16,0},{32,48},{48,32},{64,80},{80,64},{96,112},{112,96},{1... | collective-permute-start | bytes 6291464 | tf_op jit(solution)/shard_map/ppermute | solution.py:454
  47.1 0.0 copy-done.7
  47.2 0.7 copy.18.weight_ref
  47.9 0.0 copy-done.6
  47.9 0.7 copy.17.ids_ref
  48.6 1.9 shard_map.156
  50.6 2.0 shard_map.157
  52.6 0.0 all-to-all-done.states_ref
  52.6 0.0 copy-start.3
  52.6 0.9 copy-done.3
  53.5 2.4 %shard_map.158 = (bf16[128,128]{1,0:T(8,128)(2,1)}, bf16[16,40,128]{2,1,0:T(8,128)(2,1)}, f32[32,128]{1,0:T(8,128)}) custom-call(s32[1]{0:T(128)} %bitcast.me_ref, bf16[32,144,128]{2,1,0:T(8,128)(2,1)S(1)} %all-to-all-done.states_ref, bf16[128,128]{1,0:T(8,128)(2,1)} %c_ref.5, f32[128,128]{1,0:T(8,128)} %get-tuple-element.28.cum_ref, ...), custom_call_target="tpu_custom_call" | custom-call | tf_op jit(solution)/shard_map/pallas_call | solution.py:62
  55.9 25.2 %all_to_all.30.in_ref = bf16[16,40,128]{2,1,0:T(8,128)(2,1)S(1)} all-to-all(bf16[16,40,128]{2,1,0:T(8,128)(2,1)} %get-tuple-element.32), channel_id=1, replica_groups=mesh['ctx'=32,'exp'=16] {'exp'}, dimensions={0} | all-to-all | bytes 327680 | tf_op jit(solution)/shard_map/all_to_all | solution.py:406
  81.0 1.2 shard_map.159
  82.2 3.7 %all-to-all-start.2 = ((bf16[8,32,2048]{2,1,0:T(8,128)(2,1)}), bf16[8,32,2048]{2,1,0:T(8,128)(2,1)S(1)}, u32[]{:S(2)}, u32[]{:S(2)}) async-start(bf16[8,32,2048]{2,1,0:T(8,128)(2,1)} %get-tuple-element.33), calls=%async_computation.2 | async-start | bytes 2097152 | tf_op jit(solution)/shard_map/all_to_all | solution.py:406
  85.9 0.0 collective-permute-done.peer_ref
  85.9 12.6 %all-to-all-done.2.rows_ref.own_ref = bf16[8,32,2048]{2,1,0:T(8,128)(2,1)S(1)} async-done(((bf16[8,32,2048]{2,1,0:T(8,128)(2,1)}), bf16[8,32,2048]{2,1,0:T(8,128)(2,1)S(1)}, u32[]{:S(2)}, u32[]{:S(2)}) %all-to-all-start.2) | async-done | bytes 1048608 | tf_op jit(solution)/shard_map/all_to_all | solution.py:406
  98.5 0.0 copy-start
  98.5 0.0 collective-permute-done.2.far_ref
  98.5 9.5 %shard_map.161 = (bf16[8,32,2048]{2,1,0:T(8,128)(2,1)}, bf16[2,128,256]{2,1,0:T(8,128)(2,1)}, bf16[11,32,2048]{2,1,0:T(8,128)(2,1)}) custom-call(bf16[8,32,2048]{2,1,0:T(8,128)(2,1)S(1)} %all-to-all-done.2.rows_ref.own_ref, bf16[2,256,2048]{2,1,0:T(8,128)(2,1)} %shard_map.160.own_ref, bf16[2,256,2048]{2,1,0:T(8,128)(2,1)} %collective-permute-done.peer_ref, ...), custom_call_target="tpu_custom_call" | custom-call | tf_op jit(solution)/shard_map/pallas_call | solution.py:305
  108.1 0.0 copy-done
  108.1 8.1 %collective-permute-start.3 = (bf16[11,32,2048]{2,1,0:T(8,128)(2,1)}, bf16[11,32,2048]{2,1,0:T(8,128)(2,1)S(1)}, u32[]{:S(2)}, u32[]{:S(2)}) collective-permute-start(bf16[11,32,2048]{2,1,0:T(8,128)(2,1)} %get-tuple-element.46), channel_id=1, source_target_pairs={{0,16},{16,0},{32,48},{48,32},{64,80},{80,64},{96,112},{112,96},{1... | collective-permute-start | bytes 4325384 | tf_op jit(solution)/shard_map/ppermute | solution.py:454
  116.2 0.0 copy-start.1
  116.2 19.6 %all_to_all.31.parts_ref = bf16[8,32,2048]{2,1,0:T(8,128)(2,1)S(1)} all-to-all(bf16[8,32,2048]{2,1,0:T(8,128)(2,1)} %get-tuple-element.34), channel_id=1, replica_groups={{0,64,160,224,256,320,416,480},{32,96,128,192,288,352,384,448},{16,80,1..., dimensions={0} | all-to-all | bytes 2097152 | tf_op jit(solution)/shard_map/all_to_all | solution.py:406
  135.9 1.8 shard_map.162
  137.7 0.0 copy-start.2
  137.7 9.1 %all-to-all-start.4 = ((bf16[16,32,128]{2,1,0:T(8,128)(2,1)}), bf16[16,32,128]{2,1,0:T(8,128)(2,1)S(1)}, u32[]{:S(2)}, u32[]{:S(2)}) async-start(bf16[16,32,128]{2,1,0:T(8,128)(2,1)} %shard_map.162), calls=%async_computation.4 | async-start | bytes 262144 | tf_op jit(solution)/shard_map/all_to_all | solution.py:406
  146.8 1.9 collective-permute-start.4
  148.7 0.0 collective-permute-done.3.peer_ref
  148.7 0.0 copy-start.5
  148.7 3.4 %collective-permute-start.5 = (bf16[11,32,2048]{2,1,0:T(8,128)(2,1)S(1)}, bf16[11,32,2048]{2,1,0:T(8,128)(2,1)}, u32[]{:S(2)}, u32[]{:S(2)}) collective-permute-start(bf16[11,32,2048]{2,1,0:T(8,128)(2,1)S(1)} %collective-permute-done.3.peer_ref), channel_id=1, source_target_pairs={{0,128},{16,48},{32,160},{48,16},{64,192},{80,112},{96,224},{112,8... | collective-permute-start | bytes 4325384 | tf_op jit(solution)/shard_map/ppermute | solution.py:457
  152.1 6.6 %all-to-all-done.4.rows_ref = bf16[16,32,128]{2,1,0:T(8,128)(2,1)S(1)} async-done(((bf16[16,32,128]{2,1,0:T(8,128)(2,1)}), bf16[16,32,128]{2,1,0:T(8,128)(2,1)S(1)}, u32[]{:S(2)}, u32[]{:S(2)}) %all-to-all-start.4) | async-done | bytes 131104 | tf_op jit(solution)/shard_map/all_to_all | solution.py:406
  158.7 0.0 copy-done.1
  158.7 2.3 %shard_map.164 = (bf16[128,128]{1,0:T(8,128)(2,1)}, f32[128,128]{1,0:T(8,128)}, bf16[32,128,128]{2,1,0:T(8,128)(2,1)}) custom-call(bf16[16,32,128]{2,1,0:T(8,128)(2,1)S(1)} %all-to-all-done.4.rows_ref, bf16[2,128,256]{2,1,0:T(8,128)(2,1)S(1)} %copy-done.1, bf16[128,128]{1,0:T(8,128)(2,1)} %grad_ref.3, bf16[128,128]{1,0:T(8,128)(2,1)} %c_ref.5, ...), custom_call_target="tpu_custom_call" | custom-call | tf_op jit(solution)/shard_map/pallas_call | solution.py:62
  161.0 7.7 %all-to-all-start.5 = ((bf16[32,128,128]{2,1,0:T(8,128)(2,1)}), bf16[32,128,128]{2,1,0:T(8,128)(2,1)S(1)}, u32[]{:S(2)}, u32[]{:S(2)}) async-start(bf16[32,128,128]{2,1,0:T(8,128)(2,1)} %get-tuple-element.41), calls=%async_computation.5 | async-start | bytes 2097152 | tf_op jit(solution)/shard_map/all_to_all | solution.py:406
  168.7 0.0 copy-done.2
  168.7 1.7 shard_map.165.local_ref
  170.4 0.0 copy-done.5
  170.4 1.6 shard_map.163
  172.1 23.7 %all-to-all-done.5.states_ref = bf16[32,128,128]{2,1,0:T(8,128)(2,1)S(1)} async-done(((bf16[32,128,128]{2,1,0:T(8,128)(2,1)}), bf16[32,128,128]{2,1,0:T(8,128)(2,1)S(1)}, u32[]{:S(2)}, u32[]{:S(2)}) %all-to-all-start.5) | async-done | bytes 1048608 | tf_op jit(solution)/shard_map/all_to_all | solution.py:406
  195.7 1.9 shard_map.166
  197.6 0.0 collective-permute-done.4.near_ref
  197.6 0.0 collective-permute-done.5.far_ref
  197.6 5.3 %shard_map.167 = (bf16[2048,256]{1,0:T(8,128)(2,1)}, bf16[256,2048]{1,0:T(8,128)(2,1)}) custom-call(bf16[8,32,2048]{2,1,0:T(8,128)(2,1)} %copy-done, bf16[2,128,256]{2,1,0:T(8,128)(2,1)} %get-tuple-element.45.mine_ref, bf16[11,32,2048]{2,1,0:T(8,128)(2,1)} %copy-done.5, bf16[11,32,2048]{2,1,0:T(8,128)(2,1)} %collective-permute-done.4.near_ref, ...), custom_call_target="tpu_custom_call" | custom-call | tf_op jit(solution)/shard_map/pallas_call | solution.py:62
Async XLA Ops:
  3.7 14.9 %copy-start.4 = (bf16[2,256,2048]{2,1,0:T(8,128)(2,1)S(1)}, bf16[2,256,2048]{2,1,0:T(8,128)(2,1)}, u32[]{:S(2)}) copy-start(bf16[2,256,2048]{2,1,0:T(8,128)(2,1)} %shard_map.160.own_ref) | copy-start | bytes 6291460
  3.7 43.4 %copy-start.7 = (f32[128,2]{0,1:T(2,128)S(1)}, f32[128,2]{0,1:T(2,128)}, u32[]{:S(2)}) copy-start(f32[128,2]{0,1:T(2,128)} %param.19) | copy-start | bytes 3076
  3.7 44.2 %copy-start.6 = (s32[128,2]{0,1:T(2,128)S(1)}, s32[128,2]{0,1:T(2,128)}, u32[]{:S(2)}) copy-start(s32[128,2]{0,1:T(2,128)} %param.20) | copy-start | bytes 3076
  3.7 36.1 %collective-permute-start.1 = (bf16[2,256,2048]{2,1,0:T(8,128)(2,1)}, bf16[2,256,2048]{2,1,0:T(8,128)(2,1)}, u32[]{:S(2)}, u32[]{:S(2)}) collective-permute-start(bf16[2,256,2048]{2,1,0:T(8,128)(2,1)} %shard_map.160.own_ref), channel_id=1, source_target_pairs={{0,128},{16,48},{32,160},{48,16},{64,192},{80,112},{96,224},{112,8... | collective-permute-start | bytes 6291464 | tf_op jit(solution)/shard_map/ppermute | solution.py:457
  10.2 42.4 %all-to-all-start = ((bf16[32,144,128]{2,1,0:T(8,128)(2,1)}), bf16[32,144,128]{2,1,0:T(8,128)(2,1)S(1)}, u32[]{:S(2)}, u32[]{:S(2)}) async-start(bf16[32,144,128]{2,1,0:T(8,128)(2,1)} %get-tuple-element.27), calls=%async_computation | async-start | bytes 2359296 | tf_op jit(solution)/shard_map/all_to_all | solution.py:406
  18.6 67.3 %collective-permute-start = (bf16[2,256,2048]{2,1,0:T(8,128)(2,1)S(1)}, bf16[2,256,2048]{2,1,0:T(8,128)(2,1)}, u32[]{:S(2)}, u32[]{:S(2)}) collective-permute-start(bf16[2,256,2048]{2,1,0:T(8,128)(2,1)S(1)} %copy-done.4), channel_id=1, source_target_pairs={{0,16},{16,0},{32,48},{48,32},{64,80},{80,64},{96,112},{112,96},{1... | collective-permute-start | bytes 6291464 | tf_op jit(solution)/shard_map/ppermute | solution.py:454
  39.8 58.7 %collective-permute-start.2 = (bf16[2,256,2048]{2,1,0:T(8,128)(2,1)}, bf16[2,256,2048]{2,1,0:T(8,128)(2,1)}, u32[]{:S(2)}, u32[]{:S(2)}) collective-permute-start(bf16[2,256,2048]{2,1,0:T(8,128)(2,1)} %collective-permute-done.1.near_ref), channel_id=1, source_target_pairs={{0,16},{16,0},{32,48},{48,32},{64,80},{80,64},{96,112},{112,96},{1... | collective-permute-start | bytes 6291464 | tf_op jit(solution)/shard_map/ppermute | solution.py:454
  52.6 0.9 copy-start.3
  82.2 16.3 %all-to-all-start.2 = ((bf16[8,32,2048]{2,1,0:T(8,128)(2,1)}), bf16[8,32,2048]{2,1,0:T(8,128)(2,1)S(1)}, u32[]{:S(2)}, u32[]{:S(2)}) async-start(bf16[8,32,2048]{2,1,0:T(8,128)(2,1)} %get-tuple-element.33), calls=%async_computation.2 | async-start | bytes 2097152 | tf_op jit(solution)/shard_map/all_to_all | solution.py:406
  98.5 9.6 %copy-start = (bf16[8,32,2048]{2,1,0:T(8,128)(2,1)}, bf16[8,32,2048]{2,1,0:T(8,128)(2,1)S(1)}, u32[]{:S(2)}) copy-start(bf16[8,32,2048]{2,1,0:T(8,128)(2,1)S(1)} %all-to-all-done.2.rows_ref.own_ref) | copy-start | bytes 3145732
  108.1 40.6 %collective-permute-start.3 = (bf16[11,32,2048]{2,1,0:T(8,128)(2,1)}, bf16[11,32,2048]{2,1,0:T(8,128)(2,1)S(1)}, u32[]{:S(2)}, u32[]{:S(2)}) collective-permute-start(bf16[11,32,2048]{2,1,0:T(8,128)(2,1)} %get-tuple-element.46), channel_id=1, source_target_pairs={{0,16},{16,0},{32,48},{48,32},{64,80},{80,64},{96,112},{112,96},{1... | collective-permute-start | bytes 4325384 | tf_op jit(solution)/shard_map/ppermute | solution.py:454
  116.2 42.5 %copy-start.1 = (bf16[2,128,256]{2,1,0:T(8,128)(2,1)S(1)}, bf16[2,128,256]{2,1,0:T(8,128)(2,1)}, u32[]{:S(2)}) copy-start(bf16[2,128,256]{2,1,0:T(8,128)(2,1)} %get-tuple-element.38.from_ref) | copy-start | bytes 393220
  137.7 31.0 %copy-start.2 = (bf16[2,4,128,128]{3,2,1,0:T(8,128)(2,1)S(1)}, bf16[2,4,128,128]{3,2,1,0:T(8,128)(2,1)}, u32[]{:S(2)}) copy-start(bf16[2,4,128,128]{3,2,1,0:T(8,128)(2,1)} %get-tuple-element.44.back_ref) | copy-start | bytes 786436
  137.7 21.1 %all-to-all-start.4 = ((bf16[16,32,128]{2,1,0:T(8,128)(2,1)}), bf16[16,32,128]{2,1,0:T(8,128)(2,1)S(1)}, u32[]{:S(2)}, u32[]{:S(2)}) async-start(bf16[16,32,128]{2,1,0:T(8,128)(2,1)} %shard_map.162), calls=%async_computation.4 | async-start | bytes 262144 | tf_op jit(solution)/shard_map/all_to_all | solution.py:406
  146.8 50.8 %collective-permute-start.4 = (bf16[11,32,2048]{2,1,0:T(8,128)(2,1)}, bf16[11,32,2048]{2,1,0:T(8,128)(2,1)}, u32[]{:S(2)}, u32[]{:S(2)}) collective-permute-start(bf16[11,32,2048]{2,1,0:T(8,128)(2,1)} %get-tuple-element.46), channel_id=1, source_target_pairs={{0,128},{16,48},{32,160},{48,16},{64,192},{80,112},{96,224},{112,8... | collective-permute-start | bytes 4325384 | tf_op jit(solution)/shard_map/ppermute | solution.py:457
  148.7 21.7 %copy-start.5 = (bf16[11,32,2048]{2,1,0:T(8,128)(2,1)}, bf16[11,32,2048]{2,1,0:T(8,128)(2,1)S(1)}, u32[]{:S(2)}) copy-start(bf16[11,32,2048]{2,1,0:T(8,128)(2,1)S(1)} %collective-permute-done.3.peer_ref) | copy-start | bytes 4325380
  148.7 48.9 %collective-permute-start.5 = (bf16[11,32,2048]{2,1,0:T(8,128)(2,1)S(1)}, bf16[11,32,2048]{2,1,0:T(8,128)(2,1)}, u32[]{:S(2)}, u32[]{:S(2)}) collective-permute-start(bf16[11,32,2048]{2,1,0:T(8,128)(2,1)S(1)} %collective-permute-done.3.peer_ref), channel_id=1, source_target_pairs={{0,128},{16,48},{32,160},{48,16},{64,192},{80,112},{96,224},{112,8... | collective-permute-start | bytes 4325384 | tf_op jit(solution)/shard_map/ppermute | solution.py:457
  161.0 34.7 %all-to-all-start.5 = ((bf16[32,128,128]{2,1,0:T(8,128)(2,1)}), bf16[32,128,128]{2,1,0:T(8,128)(2,1)S(1)}, u32[]{:S(2)}, u32[]{:S(2)}) async-start(bf16[32,128,128]{2,1,0:T(8,128)(2,1)} %get-tuple-element.41), calls=%async_computation.5 | async-start | bytes 2097152 | tf_op jit(solution)/shard_map/all_to_all | solution.py:406

commit v6 on v5

--- a/solution.py
+++ b/solution.py
@@ -52,10 +52,10 @@
     return jnp.where(condition, 1.0, 0.0).astype(dtype)
 
 
-def call(kernel, outs, *args, smem=(), near=()):
+def call(kernel, outs, *args, smem=(), near=(), far=()):
     args = [
         pltpu.with_memory_space_constraint(a, pltpu.VMEM)
-        if near is not None and (a.ndim > 2 or i in near)
+        if near is not None and i not in smem and i not in far and a.ndim > 2
         else a
         for i, a in enumerate(args)
     ]
@@ -142,18 +142,16 @@
         pay_ref[j, states:, :] = extra
 
 
-def local_kernel(x_ref, b_ref, c_ref, cum_ref, skip_ref, residual_ref, local_ref, back_ref):
+def local_kernel(x_ref, b_ref, c_ref, cum_ref, skip_ref, residual_ref, local_ref):
     tokens, features = x_ref.shape
-    heads = back_ref.shape[1]
+    heads = skip_ref.shape[1]
     width = features // heads
     square = (tokens, tokens)
     x = x_ref[...]
     cum = cum_ref[...]
     cum_t = cum.T
     inner = mm_nt(c_ref[...], b_ref[...])
-    inner_t = mm_nt(b_ref[...], c_ref[...])
     causal = iota(square, 1) <= iota(square, 0)
-    causal_t = iota(square, 0) <= iota(square, 1)
     lane = iota((tokens, features), 1)
     skip = per_head(skip_ref[...], (1, features), width)
     total = residual_ref[...].astype(f32) + skip * x.astype(f32)
@@ -165,18 +163,32 @@
         product = mm(high, x) + mm(low, x)
         inside = (lane >= head * width) & (lane < (head + 1) * width)
         total = total + jnp.where(inside, product, 0.0)
+    local_ref[...] = total
+
+
+def back_kernel(b_ref, c_ref, cum_ref, back_ref):
+    tokens, features = cum_ref.shape
+    heads = back_ref.shape[1]
+    width = features // heads
+    square = (tokens, tokens)
+    cum = cum_ref[...]
+    cum_t = cum.T
+    inner_t = mm_nt(b_ref[...], c_ref[...])
+    causal_t = iota(square, 0) <= iota(square, 1)
+    for head in range(heads):
+        column = cum[:, head * width : head * width + 1]
+        row = cum_t[head * width : head * width + 1, :]
         gap_t = jnp.where(causal_t, row - column, -jnp.inf)
         high, low = split2(inner_t * jnp.exp(gap_t))
         back_ref[0, head] = high
         back_ref[1, head] = low
-    local_ref[...] = total
 
 
 def block_sums(states_ref, rows_at):
     blocks = states_ref.shape[0]
     features = states_ref.shape[2]
-    extra = states_ref[:, rows_at : rows_at + 16, :].astype(f32)
-    place = iota((blocks, 16, features), 1)
+    extra = states_ref[:, rows_at : rows_at + 8, :].astype(f32)
+    place = iota((blocks, 8, features), 1)
     return [
         jnp.sum(jnp.where(place == k, extra, 0.0), axis=1).astype(bf16) for k in range(3)
     ]
@@ -255,7 +267,7 @@
         out_ref[lot, capacity:, here] = d_hidden[rows, :]
 
 
-def expert_kernel(rows_ref, own_ref, peer_ref, near_ref, far_ref, parts_ref, mine_ref, send_ref, held, sems):
+def expert_kernel(rows_ref, own_ref, peer_ref, near_ref, far_ref, parts_ref, mine_ref, near_units_ref, send_ref, held, sems):
     copies = [
         pltpu.make_async_copy(source, held.at[k], sems.at[k])
         for k, source in enumerate((own_ref, peer_ref, near_ref, far_ref))
@@ -286,8 +298,11 @@
         if k == 0:
             mine_ref[0] = activated
             mine_ref[1] = d_hidden
+        elif k == 2:
+            near_units_ref[0] = activated
+            near_units_ref[1] = d_hidden
         else:
-            pack_units(send_ref, chips + k - 1, activated, d_hidden)
+            pack_units(send_ref, chips + k // 2, activated, d_hidden)
         d_part = [mm_nt(d_hidden, piece) for piece in wide]
         out_part = mm(activated, narrow)
         d_total = d_part if k == 0 else [a + b for a, b in zip(d_total, d_part)]
@@ -307,10 +322,11 @@
         out_shape=[
             shape_of(rows.shape, bf16),
             shape_of((2, count, units), bf16),
-            shape_of((chips + 3, both, width), bf16),
+            shape_of((2, count, units), bf16),
+            shape_of((chips + 2, both, width), bf16),
         ],
         in_specs=[near] + [pl.BlockSpec(memory_space=pl.ANY)] * 4,
-        out_specs=[near] * 3,
+        out_specs=[near] * 4,
         scratch_shapes=[
             pltpu.VMEM((4,) + weights[0].shape, bf16),
             pltpu.SemaphoreType.DMA((4,)),
@@ -318,17 +334,17 @@
     )(pltpu.with_memory_space_constraint(rows, pltpu.VMEM), *weights)
 
 
-def weight_grad_kernel(own_ref, mine_ref, peer_ref, near_ref, far_ref, in_ref, down_ref):
+def weight_grad_kernel(own_ref, mine_ref, peer_ref, near_ref, near_units_ref, far_ref, in_ref, down_ref):
     chips, both, width = own_ref.shape
     capacity = both // 2
     count = chips * capacity
     units = mine_ref.shape[2]
-    lots = [own_ref, peer_ref, near_ref, far_ref]
+    lots = [own_ref, near_ref, peer_ref, far_ref]
     rows = jnp.concatenate([lot[:chips, :capacity, :].reshape(count, width) for lot in lots])
     cot = jnp.concatenate([lot[:chips, capacity:, :].reshape(count, width) for lot in lots])
-    activated = [mine_ref[0]]
-    d_hidden = [mine_ref[1]]
-    for k, lot in enumerate(lots[1:]):
+    activated = [mine_ref[0], near_units_ref[0]]
+    d_hidden = [mine_ref[1], near_units_ref[1]]
+    for k, lot in enumerate(lots[2:]):
         for j in range(count // capacity):
             here = slice(j * units, (j + 1) * units)
             activated.append(lot[chips + k, :capacity, here])
@@ -458,7 +474,7 @@
 
     state_pay, cum = call(
         state_kernel,
-        (shape_of((blocks, states + 16, features), bf16), shape_of((tokens, features), f32)),
+        (shape_of((blocks, states + 8, features), bf16), shape_of((tokens, features), f32)),
         ssd_input, state_in, log_decay.T,
     )
     state_all = swap(state_pay, "ctx")
@@ -478,9 +494,8 @@
         ),
         expert_ids, expert_ids.T, route_weight, out_grad, norm_gain.reshape(1, features),
     )
-    local, back = call(
-        local_kernel,
-        (shape_of((tokens, features), f32), shape_of((2, heads, tokens, tokens), bf16)),
+    local = call(
+        local_kernel, shape_of((tokens, features), f32),
         ssd_input, state_in, state_out, cum, skip, residual,
     )
     mixed, rows_pay, later = call(
@@ -492,6 +507,7 @@
         ),
         me, state_all, state_out, cum, local, to_rows, cot_pay,
         smem=(0,),
+        far=(6,),
     )
     arrived = swap(rows_pay, "exp")
     spread, raw, inv, gain = call(
@@ -506,15 +522,17 @@
     )
     expert_rows = swap(spread, "ctx", colours)
 
-    parts, mine, send = run_experts(expert_rows, (own_w, peer_w, near_w, far_w))
+    near_rows = near(expert_rows)
+    parts, mine, of_near, send = run_experts(expert_rows, (own_w, peer_w, near_w, far_w))
     parts_all = swap(parts, "ctx", colours)
     peer_lot = partner(send)
-    near_lot = near(send)
+    near_units = near(of_near)
     far_lot = near(peer_lot)
+    back = call(back_kernel, shape_of((2, heads, tokens, tokens), bf16), state_in, state_out, cum)
     grad_in, grad_down = call(
         weight_grad_kernel,
         (shape_of(matrix_in.shape, bf16), shape_of(matrix_down.shape, bf16)),
-        expert_rows, mine, peer_lot, near_lot, far_lot,
+        expert_rows, mine, peer_lot, near_rows, near_units, far_lot,
         near=None,
     )
 

time: 204 us -> 198 us (0.971)
  waiting for transfers between devices: 61.9 us -> 50.2 us
  starting transfers between devices: 55.9 us -> 59.4 us
    all_to_all x4, waiting for transfers between devices: 42.9 us -> 31.6 us  [swap(): lax.all_to_all(a, axis, split_axis=0, concat_axis=0, tiled=True, axis_ind...]
    ppermute x3 -> x4, starting transfers between devices: 9.43 us -> 12.8 us  [near(): return lax.ppermute(a, 'ctx', [(i, near_of[i]) for i in range(blocks)])]
    pallas_call x12 -> x13, Pallas kernels: 27.6 us -> 29.2 us  [call(): pl.pallas_call(kernel, out_shape=outs, in_specs=[pl.BlockSpec(memory_spac...]
    ppermute x3 -> x4, waiting for transfers between devices: 18.9 us -> 18.5 us  [near(): return lax.ppermute(a, 'ctx', [(i, near_of[i]) for i in range(blocks)])]
  transfers between devices with their start and end apart: 10 -> 11, of which waited for: 4 -> 4; matrix products, arithmetic and copies ran while one was open for 1% -> 1% of each run, Pallas kernels for 9% -> 11%
where the time goes in v6:
time: 198 us; the launch traced here: 196 us
  starting transfers between devices  59.4 us (30%)
  waiting for transfers between devices  50.2 us (25%)
  blocking collectives  44.2 us (22%)
  Pallas kernels  38.7 us (20%)
  local copies, waits for them, and re-layouts  3.08 us (2%)
    all_to_all x2, blocking collectives, swap(): lax.all_to_all(a, axis, split_axis=0, concat_axis=0, tiled=True, axis_ind...  44.2 us
    all_to_all x4, waiting for transfers between devices, swap(): lax.all_to_all(a, axis, split_axis=0, concat_axis=0, tiled=True, axis_ind...  31.6 us
    pallas_call x13, Pallas kernels, call(): pl.pallas_call(kernel, out_shape=outs, in_specs=[pl.BlockSpec(memory_spac...  29.2 us
    all_to_all x4, starting transfers between devices, swap(): lax.all_to_all(a, axis, split_axis=0, concat_axis=0, tiled=True, axis_ind...  28.6 us
    ppermute x4, waiting for transfers between devices, near(): return lax.ppermute(a, 'ctx', [(i, near_of[i]) for i in range(blocks)])  18.5 us
    ppermute x3, starting transfers between devices, partner(): return lax.ppermute(a, 'ctx', [(i, i ^ 1) for i in range(blocks)])  17.9 us
    ppermute x4, starting transfers between devices, near(): return lax.ppermute(a, 'ctx', [(i, near_of[i]) for i in range(blocks)])  12.8 us
    pallas_call x1, Pallas kernels, run_experts(): pl.pallas_call(expert_kernel, out_shape=[shape_of(rows.shape, bf16), shap...  9.55 us
  transfers between devices with their start and end apart: 11, of which 4 were waited for; matrix products, arithmetic and copies ran while one was open for 1% of the time, Pallas kernels for 11%

profile of v6, /device:TPU:1, one launch (start us, length us, event | category | flops | bytes accessed | tf_op | source)
XLA Modules:
  0.0 196.4 jit_solution(11286536305077035069)
XLA Ops:
  0.6 3.1 %shard_map.160.own_ref = bf16[2,256,2048]{2,1,0:T(8,128)(2,1)} custom-call(bf16[2048,256]{1,0:T(8,128)(2,1)} %bitcast.9, bf16[256,2048]{1,0:T(8,128)(2,1)} %bitcast.10), custom_call_target="tpu_custom_call" | custom-call | tf_op jit(solution)/shard_map/pallas_call | solution.py:62
  3.7 0.0 copy-start.3
  3.7 0.0 copy-start.6
  3.7 0.0 copy-start.5
  3.7 4.1 %collective-permute-start.1 = (bf16[2,256,2048]{2,1,0:T(8,128)(2,1)}, bf16[2,256,2048]{2,1,0:T(8,128)(2,1)}, u32[]{:S(2)}, u32[]{:S(2)}) collective-permute-start(bf16[2,256,2048]{2,1,0:T(8,128)(2,1)} %shard_map.160.own_ref), channel_id=1, source_target_pairs={{0,128},{16,48},{32,160},{48,16},{64,192},{80,112},{96,224},{112,8... | collective-permute-start | bytes 6291464 | tf_op jit(solution)/shard_map/ppermute | solution.py:473
  7.9 2.4 %shard_map.155 = (bf16[32,136,128]{2,1,0:T(8,128)(2,1)}, f32[128,128]{1,0:T(8,128)}) custom-call(bf16[128,128]{1,0:T(8,128)(2,1)} %x_ref.3, bf16[128,128]{1,0:T(8,128)(2,1)} %b_ref.7, f32[4,128]{1,0:T(4,128)} %bitcast.14), custom_call_target="tpu_custom_call" | custom-call | tf_op jit(solution)/shard_map/pallas_call | solution.py:62
  10.2 8.3 %all-to-all-start = ((bf16[32,136,128]{2,1,0:T(8,128)(2,1)}), bf16[32,136,128]{2,1,0:T(8,128)(2,1)S(1)}, u32[]{:S(2)}, u32[]{:S(2)}) async-start(bf16[32,136,128]{2,1,0:T(8,128)(2,1)} %get-tuple-element.26), calls=%async_computation | async-start | bytes 2228224 | tf_op jit(solution)/shard_map/all_to_all | solution.py:422
  18.6 0.0 copy-done.3
  18.6 2.3 %collective-permute-start = (bf16[2,256,2048]{2,1,0:T(8,128)(2,1)S(1)}, bf16[2,256,2048]{2,1,0:T(8,128)(2,1)}, u32[]{:S(2)}, u32[]{:S(2)}) collective-permute-start(bf16[2,256,2048]{2,1,0:T(8,128)(2,1)S(1)} %copy-done.3), channel_id=1, source_target_pairs={{0,16},{16,0},{32,48},{48,32},{64,80},{80,64},{96,112},{112,96},{1... | collective-permute-start | bytes 6291464 | tf_op jit(solution)/shard_map/ppermute | solution.py:470
  20.8 18.5 %collective-permute-done.1.near_ref = bf16[2,256,2048]{2,1,0:T(8,128)(2,1)} collective-permute-done((bf16[2,256,2048]{2,1,0:T(8,128)(2,1)}, bf16[2,256,2048]{2,1,0:T(8,128)(2,1)}, u32[]{:S(2)}, u32[]{:S(2)}) %collective-permute-start.1) | collective-permute-done | bytes 2097184 | tf_op jit(solution)/shard_map/ppermute | solution.py:473
  39.3 7.4 %collective-permute-start.2 = (bf16[2,256,2048]{2,1,0:T(8,128)(2,1)}, bf16[2,256,2048]{2,1,0:T(8,128)(2,1)}, u32[]{:S(2)}, u32[]{:S(2)}) collective-permute-start(bf16[2,256,2048]{2,1,0:T(8,128)(2,1)} %collective-permute-done.1.near_ref), channel_id=1, source_target_pairs={{0,16},{16,0},{32,48},{48,32},{64,80},{80,64},{96,112},{112,96},{1... | collective-permute-start | bytes 6291464 | tf_op jit(solution)/shard_map/ppermute | solution.py:470
  46.8 0.0 copy-done.6
  46.8 0.7 copy.18.weight_ref
  47.5 0.0 copy-done.5
  47.5 0.7 copy.17.ids_ref
  48.3 1.9 shard_map.156.local_ref
  50.1 2.0 %shard_map.157 = (bf16[256,128]{1,0:T(8,128)(2,1)}, bf16[2,128,256]{2,1,0:T(8,128)(2,1)}, bf16[16,24,128]{2,1,0:T(8,128)(2,1)}) custom-call(s32[128,2]{1,0:T(8,128)} %copy.17.ids_ref, s32[2,128]{1,0:T(2,128)} %bitcast.11, f32[128,2]{1,0:T(8,128)} %copy.18.weight_ref, bf16[128,128]{1,0:T(8,128)(2,1)} %grad_ref.3, f32[1,128]{1,0:T(1,128)} %bitcast.15), custom_call_target="tpu_custom_call" | custom-call | tf_op jit(solution)/shard_map/pallas_call | solution.py:62
  52.2 0.0 all-to-all-done.states_ref
  52.2 2.5 %shard_map.158 = (bf16[128,128]{1,0:T(8,128)(2,1)}, bf16[16,40,128]{2,1,0:T(8,128)(2,1)}, f32[32,128]{1,0:T(8,128)}) custom-call(s32[1]{0:T(128)} %bitcast.me_ref, bf16[32,136,128]{2,1,0:T(8,128)(2,1)S(1)} %all-to-all-done.states_ref, bf16[128,128]{1,0:T(8,128)(2,1)} %c_ref.7, f32[128,128]{1,0:T(8,128)} %get-tuple-element.27.cum_ref, ...), custom_call_target="tpu_custom_call" | custom-call | tf_op jit(solution)/shard_map/pallas_call | solution.py:62
  54.6 24.9 %all_to_all.30.in_ref = bf16[16,40,128]{2,1,0:T(8,128)(2,1)S(1)} all-to-all(bf16[16,40,128]{2,1,0:T(8,128)(2,1)} %get-tuple-element.30), channel_id=1, replica_groups=mesh['ctx'=32,'exp'=16] {'exp'}, dimensions={0} | all-to-all | bytes 327680 | tf_op jit(solution)/shard_map/all_to_all | solution.py:422
  79.6 1.2 shard_map.159
  80.8 3.7 %all-to-all-start.2 = ((bf16[8,32,2048]{2,1,0:T(8,128)(2,1)}), bf16[8,32,2048]{2,1,0:T(8,128)(2,1)S(1)}, u32[]{:S(2)}, u32[]{:S(2)}) async-start(bf16[8,32,2048]{2,1,0:T(8,128)(2,1)} %get-tuple-element.31), calls=%async_computation.2 | async-start | bytes 2097152 | tf_op jit(solution)/shard_map/all_to_all | solution.py:422
  84.5 0.0 collective-permute-done.peer_ref
  84.5 12.5 %all-to-all-done.2.rows_ref.own_ref = bf16[8,32,2048]{2,1,0:T(8,128)(2,1)S(1)} async-done(((bf16[8,32,2048]{2,1,0:T(8,128)(2,1)}), bf16[8,32,2048]{2,1,0:T(8,128)(2,1)S(1)}, u32[]{:S(2)}, u32[]{:S(2)}) %all-to-all-start.2) | async-done | bytes 1048608 | tf_op jit(solution)/shard_map/all_to_all | solution.py:422
  97.0 0.0 copy-start
  97.1 0.0 collective-permute-done.2.far_ref
  97.1 9.6 %shard_map.161 = (bf16[8,32,2048]{2,1,0:T(8,128)(2,1)}, bf16[2,128,256]{2,1,0:T(8,128)(2,1)}, bf16[2,128,256]{2,1,0:T(8,128)(2,1)}, bf16[10,32,2048]{2,1,0:T(8,128)(2,1)}) custom-call(bf16[8,32,2048]{2,1,0:T(8,128)(2,1)S(1)} %all-to-all-done.2.rows_ref.own_ref, bf16[2,256,2048]{2,1,0:T(8,128)(2,1)} %shard_map.160.own_ref, ...), custom_call_target="tpu_custom_call" | custom-call | tf_op jit(solution)/shard_map/pallas_call | solution.py:320
  106.6 8.2 %collective-permute-start.3 = (bf16[10,32,2048]{2,1,0:T(8,128)(2,1)}, bf16[10,32,2048]{2,1,0:T(8,128)(2,1)}, u32[]{:S(2)}, u32[]{:S(2)}) collective-permute-start(bf16[10,32,2048]{2,1,0:T(8,128)(2,1)} %get-tuple-element.43), channel_id=1, source_target_pairs={{0,16},{16,0},{32,48},{48,32},{64,80},{80,64},{96,112},{112,96},{1... | collective-permute-start | bytes 3932168 | tf_op jit(solution)/shard_map/ppermute | solution.py:470
  114.8 0.0 copy-start.2
  114.9 19.3 %all_to_all.31.parts_ref = bf16[8,32,2048]{2,1,0:T(8,128)(2,1)S(1)} all-to-all(bf16[8,32,2048]{2,1,0:T(8,128)(2,1)} %get-tuple-element.32), channel_id=1, replica_groups={{0,64,160,224,256,320,416,480},{32,96,128,192,288,352,384,448},{16,80,1..., dimensions={0} | all-to-all | bytes 2097152 | tf_op jit(solution)/shard_map/all_to_all | solution.py:422
  134.1 1.8 shard_map.162
  135.9 9.2 %all-to-all-start.4 = ((bf16[16,32,128]{2,1,0:T(8,128)(2,1)}), bf16[16,32,128]{2,1,0:T(8,128)(2,1)S(1)}, u32[]{:S(2)}, u32[]{:S(2)}) async-start(bf16[16,32,128]{2,1,0:T(8,128)(2,1)} %shard_map.162), calls=%async_computation.4 | async-start | bytes 262144 | tf_op jit(solution)/shard_map/all_to_all | solution.py:422
  145.1 0.0 copy-start.7
  145.2 0.0 collective-permute-done.3.peer_ref
  145.2 2.1 %collective-permute-start.6 = (bf16[10,32,2048]{2,1,0:T(8,128)(2,1)}, bf16[10,32,2048]{2,1,0:T(8,128)(2,1)}, u32[]{:S(2)}, u32[]{:S(2)}) collective-permute-start(bf16[10,32,2048]{2,1,0:T(8,128)(2,1)} %collective-permute-done.3.peer_ref), channel_id=1, source_target_pairs={{0,128},{16,48},{32,160},{48,16},{64,192},{80,112},{96,224},{112,8... | collective-permute-start | bytes 3932168 | tf_op jit(solution)/shard_map/ppermute | solution.py:473
  147.2 0.0 copy-done
  147.2 3.4 %collective-permute-start.4 = (bf16[8,32,2048]{2,1,0:T(8,128)(2,1)S(1)}, bf16[8,32,2048]{2,1,0:T(8,128)(2,1)}, u32[]{:S(2)}, u32[]{:S(2)}) collective-permute-start(bf16[8,32,2048]{2,1,0:T(8,128)(2,1)S(1)} %all-to-all-done.2.rows_ref.own_ref), channel_id=1, source_target_pairs={{0,128},{16,48},{32,160},{48,16},{64,192},{80,112},{96,224},{112,8... | collective-permute-start | bytes 3145736 | tf_op jit(solution)/shard_map/ppermute | solution.py:473
  150.6 6.5 %all-to-all-done.4.rows_ref = bf16[16,32,128]{2,1,0:T(8,128)(2,1)S(1)} async-done(((bf16[16,32,128]{2,1,0:T(8,128)(2,1)}), bf16[16,32,128]{2,1,0:T(8,128)(2,1)S(1)}, u32[]{:S(2)}, u32[]{:S(2)}) %all-to-all-start.4) | async-done | bytes 131104 | tf_op jit(solution)/shard_map/all_to_all | solution.py:422
  157.1 0.0 copy-done.2
  157.1 2.3 %shard_map.164 = (bf16[128,128]{1,0:T(8,128)(2,1)}, f32[128,128]{1,0:T(8,128)}, bf16[32,128,128]{2,1,0:T(8,128)(2,1)}) custom-call(bf16[16,32,128]{2,1,0:T(8,128)(2,1)S(1)} %all-to-all-done.4.rows_ref, bf16[2,128,256]{2,1,0:T(8,128)(2,1)S(1)} %copy-done.2, bf16[128,128]{1,0:T(8,128)(2,1)} %grad_ref.3, bf16[128,128]{1,0:T(8,128)(2,1)} %c_ref.7, ...), custom_call_target="tpu_custom_call" | custom-call | tf_op jit(solution)/shard_map/pallas_call | solution.py:62
  159.4 7.4 %all-to-all-start.5 = ((bf16[32,128,128]{2,1,0:T(8,128)(2,1)}), bf16[32,128,128]{2,1,0:T(8,128)(2,1)S(1)}, u32[]{:S(2)}, u32[]{:S(2)}) async-start(bf16[32,128,128]{2,1,0:T(8,128)(2,1)} %get-tuple-element.39), calls=%async_computation.5 | async-start | bytes 2097152 | tf_op jit(solution)/shard_map/all_to_all | solution.py:422
  166.8 0.0 copy-done.7
  166.8 3.3 %collective-permute-start.5 = (bf16[2,128,256]{2,1,0:T(8,128)(2,1)S(1)}, bf16[2,128,256]{2,1,0:T(8,128)(2,1)S(1)}, u32[]{:S(2)}, u32[]{:S(2)}) collective-permute-start(bf16[2,128,256]{2,1,0:T(8,128)(2,1)S(1)} %copy-done.7), channel_id=1, source_target_pairs={{0,128},{16,48},{32,160},{48,16},{64,192},{80,112},{96,224},{112,8... | collective-permute-start | bytes 393224 | tf_op jit(solution)/shard_map/ppermute | solution.py:473
  170.1 1.8 shard_map.165.back_ref
  171.9 0.0 copy-start.1
  171.9 0.9 copy-done.1
  172.8 1.7 shard_map.166.local_ref
  174.5 1.6 shard_map.163
  176.2 12.6 %all-to-all-done.5.states_ref = bf16[32,128,128]{2,1,0:T(8,128)(2,1)S(1)} async-done(((bf16[32,128,128]{2,1,0:T(8,128)(2,1)}), bf16[32,128,128]{2,1,0:T(8,128)(2,1)S(1)}, u32[]{:S(2)}, u32[]{:S(2)}) %all-to-all-start.5) | async-done | bytes 1048608 | tf_op jit(solution)/shard_map/all_to_all | solution.py:422
  188.8 1.9 shard_map.167
  190.7 0.0 collective-permute-done.4.near_ref
  190.7 0.0 collective-permute-done.5.near_units_ref
  190.7 0.0 copy-start.4
  190.7 0.0 collective-permute-done.6.far_ref
  190.7 0.6 copy-done.4
  191.3 5.1 %shard_map.168 = (bf16[2048,256]{1,0:T(8,128)(2,1)}, bf16[256,2048]{1,0:T(8,128)(2,1)}) custom-call(bf16[8,32,2048]{2,1,0:T(8,128)(2,1)} %copy-done, bf16[2,128,256]{2,1,0:T(8,128)(2,1)} %get-tuple-element.42.mine_ref, bf16[10,32,2048]{2,1,0:T(8,128)(2,1)} %collective-permute-done.3.peer_ref, bf16[8,32,2048]{2,1,0:T(8,128)(2,1)} %collective-permute-done.4.near_ref, ...), custom_call_target="tpu_custom_call" | custom-call | tf_op jit(solution)/shard_map/pallas_call | solution.py:62
Async XLA Ops:
  3.7 14.8 %copy-start.3 = (bf16[2,256,2048]{2,1,0:T(8,128)(2,1)S(1)}, bf16[2,256,2048]{2,1,0:T(8,128)(2,1)}, u32[]{:S(2)}) copy-start(bf16[2,256,2048]{2,1,0:T(8,128)(2,1)} %shard_map.160.own_ref) | copy-start | bytes 6291460
  3.7 43.1 %copy-start.6 = (f32[128,2]{0,1:T(2,128)S(1)}, f32[128,2]{0,1:T(2,128)}, u32[]{:S(2)}) copy-start(f32[128,2]{0,1:T(2,128)} %param.19) | copy-start | bytes 3076
  3.7 43.8 %copy-start.5 = (s32[128,2]{0,1:T(2,128)S(1)}, s32[128,2]{0,1:T(2,128)}, u32[]{:S(2)}) copy-start(s32[128,2]{0,1:T(2,128)} %param.20) | copy-start | bytes 3076
  3.7 35.6 %collective-permute-start.1 = (bf16[2,256,2048]{2,1,0:T(8,128)(2,1)}, bf16[2,256,2048]{2,1,0:T(8,128)(2,1)}, u32[]{:S(2)}, u32[]{:S(2)}) collective-permute-start(bf16[2,256,2048]{2,1,0:T(8,128)(2,1)} %shard_map.160.own_ref), channel_id=1, source_target_pairs={{0,128},{16,48},{32,160},{48,16},{64,192},{80,112},{96,224},{112,8... | collective-permute-start | bytes 6291464 | tf_op jit(solution)/shard_map/ppermute | solution.py:473
  10.2 41.9 %all-to-all-start = ((bf16[32,136,128]{2,1,0:T(8,128)(2,1)}), bf16[32,136,128]{2,1,0:T(8,128)(2,1)S(1)}, u32[]{:S(2)}, u32[]{:S(2)}) async-start(bf16[32,136,128]{2,1,0:T(8,128)(2,1)} %get-tuple-element.26), calls=%async_computation | async-start | bytes 2228224 | tf_op jit(solution)/shard_map/all_to_all | solution.py:422
  18.6 66.0 %collective-permute-start = (bf16[2,256,2048]{2,1,0:T(8,128)(2,1)S(1)}, bf16[2,256,2048]{2,1,0:T(8,128)(2,1)}, u32[]{:S(2)}, u32[]{:S(2)}) collective-permute-start(bf16[2,256,2048]{2,1,0:T(8,128)(2,1)S(1)} %copy-done.3), channel_id=1, source_target_pairs={{0,16},{16,0},{32,48},{48,32},{64,80},{80,64},{96,112},{112,96},{1... | collective-permute-start | bytes 6291464 | tf_op jit(solution)/shard_map/ppermute | solution.py:470
  39.3 57.7 %collective-permute-start.2 = (bf16[2,256,2048]{2,1,0:T(8,128)(2,1)}, bf16[2,256,2048]{2,1,0:T(8,128)(2,1)}, u32[]{:S(2)}, u32[]{:S(2)}) collective-permute-start(bf16[2,256,2048]{2,1,0:T(8,128)(2,1)} %collective-permute-done.1.near_ref), channel_id=1, source_target_pairs={{0,16},{16,0},{32,48},{48,32},{64,80},{80,64},{96,112},{112,96},{1... | collective-permute-start | bytes 6291464 | tf_op jit(solution)/shard_map/ppermute | solution.py:470
  80.8 16.3 %all-to-all-start.2 = ((bf16[8,32,2048]{2,1,0:T(8,128)(2,1)}), bf16[8,32,2048]{2,1,0:T(8,128)(2,1)S(1)}, u32[]{:S(2)}, u32[]{:S(2)}) async-start(bf16[8,32,2048]{2,1,0:T(8,128)(2,1)} %get-tuple-element.31), calls=%async_computation.2 | async-start | bytes 2097152 | tf_op jit(solution)/shard_map/all_to_all | solution.py:422
  97.0 50.2 %copy-start = (bf16[8,32,2048]{2,1,0:T(8,128)(2,1)}, bf16[8,32,2048]{2,1,0:T(8,128)(2,1)S(1)}, u32[]{:S(2)}) copy-start(bf16[8,32,2048]{2,1,0:T(8,128)(2,1)S(1)} %all-to-all-done.2.rows_ref.own_ref) | copy-start | bytes 3145732
  106.6 38.5 %collective-permute-start.3 = (bf16[10,32,2048]{2,1,0:T(8,128)(2,1)}, bf16[10,32,2048]{2,1,0:T(8,128)(2,1)}, u32[]{:S(2)}, u32[]{:S(2)}) collective-permute-start(bf16[10,32,2048]{2,1,0:T(8,128)(2,1)} %get-tuple-element.43), channel_id=1, source_target_pairs={{0,16},{16,0},{32,48},{48,32},{64,80},{80,64},{96,112},{112,96},{1... | collective-permute-start | bytes 3932168 | tf_op jit(solution)/shard_map/ppermute | solution.py:470
  114.8 42.3 %copy-start.2 = (bf16[2,128,256]{2,1,0:T(8,128)(2,1)S(1)}, bf16[2,128,256]{2,1,0:T(8,128)(2,1)}, u32[]{:S(2)}) copy-start(bf16[2,128,256]{2,1,0:T(8,128)(2,1)} %get-tuple-element.36.from_ref) | copy-start | bytes 393220
  135.9 21.2 %all-to-all-start.4 = ((bf16[16,32,128]{2,1,0:T(8,128)(2,1)}), bf16[16,32,128]{2,1,0:T(8,128)(2,1)S(1)}, u32[]{:S(2)}, u32[]{:S(2)}) async-start(bf16[16,32,128]{2,1,0:T(8,128)(2,1)} %shard_map.162), calls=%async_computation.4 | async-start | bytes 262144 | tf_op jit(solution)/shard_map/all_to_all | solution.py:422
  145.1 21.6 %copy-start.7 = (bf16[2,128,256]{2,1,0:T(8,128)(2,1)S(1)}, bf16[2,128,256]{2,1,0:T(8,128)(2,1)}, u32[]{:S(2)}) copy-start(bf16[2,128,256]{2,1,0:T(8,128)(2,1)} %get-tuple-element.44) | copy-start | bytes 393220
  145.2 45.5 %collective-permute-start.6 = (bf16[10,32,2048]{2,1,0:T(8,128)(2,1)}, bf16[10,32,2048]{2,1,0:T(8,128)(2,1)}, u32[]{:S(2)}, u32[]{:S(2)}) collective-permute-start(bf16[10,32,2048]{2,1,0:T(8,128)(2,1)} %collective-permute-done.3.peer_ref), channel_id=1, source_target_pairs={{0,128},{16,48},{32,160},{48,16},{64,192},{80,112},{96,224},{112,8... | collective-permute-start | bytes 3932168 | tf_op jit(solution)/shard_map/ppermute | solution.py:473
  147.2 43.4 %collective-permute-start.4 = (bf16[8,32,2048]{2,1,0:T(8,128)(2,1)S(1)}, bf16[8,32,2048]{2,1,0:T(8,128)(2,1)}, u32[]{:S(2)}, u32[]{:S(2)}) collective-permute-start(bf16[8,32,2048]{2,1,0:T(8,128)(2,1)S(1)} %all-to-all-done.2.rows_ref.own_ref), channel_id=1, source_target_pairs={{0,128},{16,48},{32,160},{48,16},{64,192},{80,112},{96,224},{112,8... | collective-permute-start | bytes 3145736 | tf_op jit(solution)/shard_map/ppermute | solution.py:473
  159.4 29.4 %all-to-all-start.5 = ((bf16[32,128,128]{2,1,0:T(8,128)(2,1)}), bf16[32,128,128]{2,1,0:T(8,128)(2,1)S(1)}, u32[]{:S(2)}, u32[]{:S(2)}) async-start(bf16[32,128,128]{2,1,0:T(8,128)(2,1)} %get-tuple-element.39), calls=%async_computation.5 | async-start | bytes 2097152 | tf_op jit(solution)/shard_map/all_to_all | solution.py:422
  166.8 23.9 %collective-permute-start.5 = (bf16[2,128,256]{2,1,0:T(8,128)(2,1)S(1)}, bf16[2,128,256]{2,1,0:T(8,128)(2,1)S(1)}, u32[]{:S(2)}, u32[]{:S(2)}) collective-permute-start(bf16[2,128,256]{2,1,0:T(8,128)(2,1)S(1)} %copy-done.7), channel_id=1, source_target_pairs={{0,128},{16,48},{32,160},{48,16},{64,192},{80,112},{96,224},{112,8... | collective-permute-start | bytes 393224 | tf_op jit(solution)/shard_map/ppermute | solution.py:473
  171.9 0.9 copy-start.1
  190.7 0.7 copy-start.4
